TPU v7x, 32 devices: a whole 2x2x4 slice. The times are simulated.
32 devices in a mesh: seq: 8 (over y, x, core), tp: 4 (over z).
Axes of the slice: x: 2, y: 2, z: 4, core: 2. Of those that a mesh axis runs over, the one named last changes fastest.
Arguments:
- byte_states: bfloat16 [2048, 1024], P('seq'), may hold values from -6 to 6
- enc_gain: bfloat16 [1024], replicated, may hold values from 0.25 to 1.75
- enc_qkv: bfloat16 [3, 1024, 1024], P(None, None, 'tp')
- enc_proj_out: bfloat16 [1024, 1024], P('tp'), may hold values from -0.1875 to 0.1875
- starts: int32 [8, 64], P('seq'), may hold values from 0 to 2048, as said below
- counts: int32 [8], P('seq'), may hold values from 32 to 64, as said below
- lift: bfloat16 [1024, 4096], P(None, 'tp')
- cross_kv: bfloat16 [2, 1024, 4096], P(None, None, 'tp')
- latent_gain: bfloat16 [4096], replicated, may hold values from 0.25 to 1.75
- lat_qkv: bfloat16 [3, 4096, 2048], P(None, 'seq', 'tp')
- lat_proj_out: bfloat16 [2048, 4096], P('tp', 'seq'), may hold values from -0.75 to 0.75
Outputs:
- byte_out: bfloat16 [2048, 1024], P('seq')
- latent_out: bfloat16 [512, 4096], P('seq', 'tp')
Inputs may be any that keep to these rules, and one draw needn't show every extreme that they name: `starts`: row s lists in increasing order the first byte (counted over all 2048 bytes) of each patch beginning in bytes s * 256 to (s + 1) * 256 - 1, then 2048 in unused places. Byte 0 begins a patch; every row's first patch begins fewer than 8 bytes into its block, and in some row exactly 7 bytes in. counts[s] is the number of patches listed in row s of starts; some row holds 64.
All inputs are finite; a program needn't handle non-finite values.
Results may differ from a plain program's by a relative error of at most 0.018.
Values may be sent and summed in bfloat16 or wider, within the bound.
A program may use at most 128 MiB of HBM per device.

v0:
```python
import math

import jax
import jax.numpy as jnp
from jax import lax
from jax.experimental import pallas as pl
from jax.experimental.pallas import tpu as pltpu
from jax.sharding import PartitionSpec as P

EH = 64
HD = 128
WIN = 512
SPILL = 8


epsilon = 1e-05
rope_base = 500000.0
far_position = 1 << 30


def from_behind(value, axis, steps):
    count = lax.axis_size(axis)
    leading, last = (max(0, -steps), min(count, count - steps))
    return lax.ppermute(value, axis, [(source, source + steps) for source in range(leading, last)])


def prefix(value, axis, join, neutral):
    count, mine = (lax.axis_size(axis), lax.axis_index(axis))
    pieces = lax.all_gather(value, axis)
    subtotal = jnp.full_like(value, 0) + jnp.asarray(neutral, value.dtype)

    def hop(position, subtotal):
        longer = join(subtotal, pieces[position])
        return jnp.where(position < mine, longer, subtotal)

    return lax.fori_loop(0, count - 1, hop, subtotal)


def shortened(value):

    def short(part):
        return part.astype(jnp.bfloat16) if part.dtype == jnp.float32 else part

    return jax.tree.map(short, value)


def rms_scale(values, gain_row):
    mean_square = jnp.mean(values * values, axis=-1, keepdims=True)
    return values * lax.rsqrt(mean_square + epsilon) * gain_row


def masked_softmax(scores, allowed):
    scores = jnp.where(allowed, scores, -1e30)
    largest = jnp.max(scores, axis=-1, keepdims=True)
    raised = jnp.where(allowed, jnp.exp(scores - largest), 0.0)
    return raised / jnp.sum(raised, axis=-1, keepdims=True)


def rotate(values, position):
    halfway = values.shape[-1] // 2
    frequency = jnp.power(
        rope_base, -2.0 * jnp.arange(halfway, dtype=jnp.float32) / values.shape[-1]
    )
    angles = position.astype(jnp.float32)[:, None] * frequency[None, :]
    cosine = jnp.cos(angles)[:, None, :]
    sine_rows = jnp.sin(angles)[:, None, :]
    lower_half = values[..., :halfway]
    upper_half = values[..., halfway:]
    return jnp.concatenate(
        [
            lower_half * cosine - upper_half * sine_rows,
            upper_half * cosine + lower_half * sine_rows,
        ],
        axis=-1,
    )


def patch_block(extended, first_byte, end_byte, in_use, anchor, lift, cross_kv):
    columns = anchor + jnp.arange(extended.shape[0], dtype=jnp.int32)
    inside = (
        (columns[None, :] >= first_byte[:, None])
        & (columns[None, :] < end_byte[:, None])
        & in_use[:, None]
    )
    member = inside.astype(jnp.bfloat16)
    totals = jnp.dot(member, extended, preferred_element_type=jnp.float32)
    lengths = jnp.maximum(jnp.sum(inside.astype(jnp.float32), axis=1), 1.0)
    pooled = (totals / lengths[:, None]).astype(jnp.bfloat16)
    lifted = jnp.dot(pooled, lift, preferred_element_type=jnp.float32)
    key_rows = jnp.dot(extended, cross_kv[0], preferred_element_type=jnp.float32).astype(
        jnp.bfloat16
    )
    value_rows = jnp.dot(extended, cross_kv[1], preferred_element_type=jnp.float32).astype(
        jnp.bfloat16
    )
    slot_total = first_byte.shape[0]
    head_count = lifted.shape[1] // HD
    queries = lifted.astype(jnp.bfloat16).reshape(slot_total, head_count, HD)
    scores = jnp.einsum(
        "phd,khd->hpk",
        queries,
        key_rows.reshape(-1, head_count, HD),
        preferred_element_type=jnp.float32,
    ) * (1.0 / math.sqrt(HD))
    allowed = inside | (~in_use)[:, None] & (columns[None, :] == anchor)
    weights = masked_softmax(scores, allowed[None]).astype(jnp.bfloat16)
    crossed = jnp.einsum(
        "hpk,khd->phd",
        weights,
        value_rows.reshape(-1, head_count, HD),
        preferred_element_type=jnp.float32,
    )
    crossed = crossed.reshape(slot_total, head_count * HD)
    return jnp.where(in_use[:, None], lifted + crossed, 0.0).astype(jnp.bfloat16)


def add_counts(earlier, later):
    return earlier + later


def gathered_shards(
    byte_states,
    enc_gain,
    enc_qkv,
    enc_proj_out,
    starts,
    counts,
    lift,
    cross_kv,
    latent_gain,
    lat_qkv,
    lat_proj_out,
):
    byte_rows = byte_states.shape[0]
    anchor = lax.axis_index("seq") * byte_rows
    states = byte_states.astype(jnp.float32)
    normed = rms_scale(states, enc_gain.astype(jnp.float32)).astype(jnp.bfloat16)
    projected = jnp.einsum(
        "bd,idc->ibc", normed, enc_qkv, preferred_element_type=jnp.float32
    ).astype(jnp.bfloat16)
    reach_blocks = max(WIN // byte_rows, 1)
    tail_rows = min(WIN, byte_rows)
    key_parts = []
    value_parts = []
    for distance in range(reach_blocks, 0, -1):
        moved_keys, moved_values = from_behind(
            (projected[1, byte_rows - tail_rows :], projected[2, byte_rows - tail_rows :]),
            "seq",
            distance,
        )
        key_parts.append(moved_keys)
        value_parts.append(moved_values)
    key_rows = jnp.concatenate(key_parts + [projected[1]], axis=0)
    value_rows = jnp.concatenate(value_parts + [projected[2]], axis=0)
    head_count = projected.shape[2] // EH
    scores = jnp.einsum(
        "qhd,khd->hqk",
        projected[0].reshape(byte_rows, head_count, EH),
        key_rows.reshape(-1, head_count, EH),
        preferred_element_type=jnp.float32,
    ) * (1.0 / math.sqrt(EH))
    query_pos = anchor + jnp.arange(byte_rows, dtype=jnp.int32)
    key_pos = anchor - WIN + jnp.arange(WIN + byte_rows, dtype=jnp.int32)
    allowed = (
        (key_pos[None, :] <= query_pos[:, None])
        & (key_pos[None, :] > query_pos[:, None] - WIN)
        & (key_pos[None, :] >= 0)
    )
    weights = masked_softmax(scores, allowed[None]).astype(jnp.bfloat16)
    attended = jnp.einsum(
        "hqk,khd->qhd",
        weights,
        value_rows.reshape(-1, head_count, EH),
        preferred_element_type=jnp.float32,
    )
    attended = attended.reshape(byte_rows, head_count * EH).astype(jnp.bfloat16)
    blended = lax.psum(jnp.dot(attended, enc_proj_out, preferred_element_type=jnp.float32), "tp")
    encoded = (states + blended).astype(jnp.bfloat16)
    patch_count = counts[0]
    local_starts = starts[0]
    first_local = (local_starts[0:1] - anchor).astype(jnp.bfloat16)
    next_rows, next_first = from_behind((encoded[:SPILL], first_local), "seq", -1)
    next_first = next_first.astype(jnp.int32)[0]
    extended = jnp.concatenate([encoded, next_rows], axis=0)
    slot_ids = jnp.arange(local_starts.shape[0], dtype=jnp.int32)
    in_use = slot_ids < patch_count
    following = jnp.concatenate([local_starts[1:], jnp.zeros((1,), jnp.int32)])
    patch_end = jnp.where(slot_ids + 1 < patch_count, following, anchor + byte_rows + next_first)
    patches = patch_block(extended, local_starts, patch_end, in_use, anchor, lift, cross_kv)
    offset = prefix(counts, "seq", add_counts, jnp.zeros((1,), jnp.int32))[0]
    position = offset + slot_ids
    slot_total = patches.shape[0]
    full_rows = lax.all_gather(patches, "tp", axis=1, tiled=True)
    normed_rows = rms_scale(full_rows.astype(jnp.float32), latent_gain.astype(jnp.float32)).astype(
        jnp.bfloat16
    )
    inner_width = lat_qkv.shape[2]
    projected = jnp.einsum(
        "pd,idc->ipc",
        normed_rows,
        lax.all_gather(lat_qkv, "seq", axis=1, tiled=True),
        preferred_element_type=jnp.float32,
    )
    heads_here = inner_width // HD
    queries = rotate(projected[0].reshape(slot_total, heads_here, HD), position).astype(
        jnp.bfloat16
    )
    latent_keys = (
        rotate(projected[1].reshape(slot_total, heads_here, HD), position)
        .astype(jnp.bfloat16)
        .reshape(slot_total, inner_width)
    )
    latent_values = projected[2].astype(jnp.bfloat16)
    latent_pos = jnp.where(in_use, position, far_position)
    largest = jnp.full((heads_here, slot_total), -1e30, jnp.float32)
    piece_keys = lax.all_gather(latent_keys, "seq", axis=0, tiled=True)
    piece_values = lax.all_gather(latent_values, "seq", axis=0, tiled=True)
    piece_pos = lax.all_gather(shortened(latent_pos), "seq", axis=0, tiled=True)
    rows_here = piece_keys.shape[0]
    piece_scores = jnp.einsum(
        "qhd,khd->hqk",
        queries,
        piece_keys.reshape(rows_here, heads_here, HD),
        preferred_element_type=jnp.float32,
    ) * (1.0 / math.sqrt(HD))
    permitted = (piece_pos[None, :] <= position[:, None])[None]
    piece_scores = jnp.where(permitted, piece_scores, -1e30)
    renewed = jnp.maximum(largest, jnp.max(piece_scores, axis=-1))
    raised = jnp.where(permitted, jnp.exp(piece_scores - renewed[..., None]), 0.0)
    weight_sum = jnp.sum(raised, axis=-1)
    weighted = jnp.einsum(
        "hqk,khd->hqd",
        raised.astype(jnp.bfloat16),
        piece_values.reshape(rows_here, heads_here, HD),
        preferred_element_type=jnp.float32,
    )
    largest, weight_sum, weighted = (renewed, weight_sum, weighted)
    latent_heads = (
        (weighted / weight_sum[..., None])
        .transpose(1, 0, 2)
        .reshape(slot_total, inner_width)
        .astype(jnp.bfloat16)
    )
    partials = jnp.dot(
        latent_heads,
        lax.all_gather(lat_proj_out, "seq", axis=1, tiled=True),
        preferred_element_type=jnp.float32,
    )
    reduced = lax.psum_scatter(partials, "tp", scatter_dimension=1, tiled=True)
    latent = jnp.where(in_use[:, None], patches.astype(jnp.float32) + reduced, 0.0).astype(
        jnp.bfloat16
    )
    return (encoded, latent)


MESH = pl.DeviceIdType.MESH
EDGE = 16


def greet(peers):
    barrier = pltpu.get_barrier_semaphore()
    for peer in peers:
        pl.semaphore_signal(barrier, inc=1, device_id=peer, device_id_type=MESH)
    pl.semaphore_wait(barrier, len(peers))


def exchange(values, out_shapes, plan, call_id):
    n_in, n_out = len(values), len(out_shapes)
    n_copies = 16

    def kernel(*refs):
        ins, outs = refs[:n_in], refs[n_in : n_in + n_out]
        send_sems, recv_sems = refs[n_in + n_out :]
        rounds = plan()
        greet([source for source, _, _ in rounds])
        copies = []
        for _, target, items in rounds:
            for in_id, in_view, out_id, out_view in items:
                copy = pltpu.make_async_remote_copy(
                    src_ref=in_view(ins[in_id]),
                    dst_ref=out_view(outs[out_id]),
                    send_sem=send_sems.at[len(copies)],
                    recv_sem=recv_sems.at[len(copies)],
                    device_id=target,
                    device_id_type=MESH,
                )
                copy.start()
                copies.append(copy)
        for copy in copies:
            copy.wait()

    return pl.pallas_call(
        kernel,
        out_shape=out_shapes,
        in_specs=[pl.BlockSpec(memory_space=pl.ANY)] * n_in,
        out_specs=[pl.BlockSpec(memory_space=pl.ANY)] * n_out,
        scratch_shapes=[
            pltpu.SemaphoreType.DMA((n_copies,)),
            pltpu.SemaphoreType.DMA((n_copies,)),
        ],
        compiler_params=pltpu.CompilerParams(collective_id=call_id, has_side_effects=True),
    )(*values)


def whole(ref):
    return ref


def slot(index):
    return lambda ref: ref.at[index]


def seq_peer(index):
    return {"seq": index}


def tp_peer(index):
    return {"tp": index}


def like(shape, dtype=jnp.bfloat16):
    return jax.ShapeDtypeStruct(shape, dtype)


def halo(projected, byte_states, info):
    size = lax.axis_size("seq")
    rows, width = projected.shape[1:]
    reach = WIN // rows

    def plan():
        s = lax.axis_index("seq")
        rounds = []
        for k in range(1, size):
            items = []
            if k <= reach:
                items.append((0, lambda ref: ref.at[pl.ds(1, 2)], 0, slot(k - 1)))
            if k == size - 1:
                items.append((0, lambda ref: ref.at[:, pl.ds(0, EDGE)], 1, whole))
                items.append((1, lambda ref: ref.at[pl.ds(0, EDGE)], 2, whole))
            items.append((2, whole, 3, slot(k - 1)))
            rounds.append(
                (seq_peer(lax.rem(s + size - k, size)), seq_peer(lax.rem(s + k, size)), items)
            )
        return rounds

    return exchange(
        [projected, byte_states, info],
        [
            like((reach, 2, rows, width)),
            like((3, EDGE, width)),
            like((EDGE, byte_states.shape[1])),
            like((size - 1, 8, 128), jnp.int32),
        ],
        plan,
        1,
    )


def encode_and_patch(
    projected, behind, edge, proj, byte_states, edge_states, bounds, used, lift, cross_kv, call_id
):
    count = lax.axis_size("tp")
    byte_rows, width = byte_states.shape
    share = byte_rows // count
    chunks = 2
    piece = share // chunks
    slots = bounds[0].shape[0]
    columns = lift.shape[1]
    total_rows = byte_rows + EDGE
    reach = behind.shape[0]
    group = 2 * HD
    panel_count = columns // group

    def kernel(
        own_ref, behind_ref, next_ref, proj_ref, states_ref, edge_ref, lo_ref, hi_ref, used_ref,
        lift_hbm, cross_hbm,
        enc_ref, patch_ref, rows_ref,
        sends, lands, tail_send, tail_land, blocks, lift_ref, cross_ref, pooled_ref, full_ref, panels, z_land,
        load_sems, rs_send, rs_recv, tail_s, tail_r, up_send, down_send, ag_recv,
        z_send, z_recv, plane_send, plane_recv, stay_sems,
    ):
        s, t = lax.axis_index("seq"), lax.axis_index("tp")
        p, c = s // 2, lax.rem(s, 2)

        def plane(index):
            return {"seq": 2 * index + c}

        loads = [
            pltpu.make_async_copy(lift_hbm, lift_ref, load_sems.at[0]),
            pltpu.make_async_copy(cross_hbm, cross_ref, load_sems.at[1]),
        ]
        for load in loads:
            load.start()
        key_rows, value_rows = (
            jnp.concatenate(
                [behind_ref[k, i] for k in range(reach - 1, -1, -1)]
                + [own_ref[i + 1], next_ref[i + 1]],
                axis=0,
            )
            for i in range(2)
        )
        query_rows = jnp.concatenate([own_ref[0], next_ref[0]], axis=0)
        reach_shape = (total_rows, WIN + total_rows)
        query_at = lax.broadcasted_iota(jnp.int32, reach_shape, 0)
        key_at = lax.broadcasted_iota(jnp.int32, reach_shape, 1) - WIN
        near = (
            (key_at <= query_at)
            & (key_at > query_at - WIN)
            & (key_at >= -lax.axis_index("seq") * byte_rows)
        )
        head_of = lax.broadcasted_iota(jnp.int32, query_rows.shape, 1) // EH
        attended = jnp.zeros(query_rows.shape, jnp.float32)
        for head in range(query_rows.shape[1] // EH):
            scores = lax.dot_general(
                jnp.where(head_of == head, query_rows, jnp.zeros_like(query_rows)),
                key_rows,
                (((1,), (1,)), ((), ())),
                preferred_element_type=jnp.float32,
            ) * (1.0 / math.sqrt(EH))
            weights = masked_softmax(scores, near).astype(jnp.bfloat16)
            seen = jnp.dot(weights, value_rows, preferred_element_type=jnp.float32)
            attended = jnp.where(head_of == head, seen, attended)
        blend = jnp.dot(
            attended.astype(jnp.bfloat16), proj_ref[...], preferred_element_type=jnp.float32
        ).astype(jnp.bfloat16)
        for q in range(count):
            for h in range(chunks):
                begin = q * share + h * piece
                sends[q, h] = blend[begin : begin + piece]
        tail_send[...] = blend[byte_rows:]
        greet(
            [tp_peer(lax.rem(t + k, count)) for k in range(1, count)]
            + [plane(lax.rem(p + k, count)) for k in range(1, count)]
        )
        scatter = [[], []]
        for h in range(chunks):
            for k in range(1, count):
                target = lax.rem(t + k, count)
                copy = pltpu.make_async_remote_copy(
                    src_ref=sends.at[target, h],
                    dst_ref=lands.at[h, k - 1],
                    send_sem=rs_send.at[h, k - 1],
                    recv_sem=rs_recv.at[h, k - 1],
                    device_id=tp_peer(target),
                    device_id_type=MESH,
                )
                copy.start()
                scatter[h].append(copy)
        tails = []
        for k in range(1, count):
            copy = pltpu.make_async_remote_copy(
                src_ref=tail_send,
                dst_ref=tail_land.at[k - 1],
                send_sem=tail_s.at[k - 1],
                recv_sem=tail_r.at[k - 1],
                device_id=tp_peer(lax.rem(t + k, count)),
                device_id_type=MESH,
            )
            copy.start()
            tails.append(copy)

        def pass_on(origin, h, up):
            step = 1 if up else -1
            return pltpu.make_async_remote_copy(
                src_ref=blocks.at[origin, h],
                dst_ref=blocks.at[origin, h],
                send_sem=(up_send if up else down_send).at[origin, h],
                recv_sem=ag_recv.at[origin, h],
                device_id=tp_peer(lax.rem(t + step + count, count)),
                device_id_type=MESH,
            )

        for h in range(chunks):
            for copy in scatter[h]:
                copy.wait_recv()
            total = sends[t, h].astype(jnp.float32)
            for k in range(count - 1):
                total = total + lands[h, k].astype(jnp.float32)
            rows = pl.ds(pl.multiple_of(t * share + h * piece, piece), piece)
            blocks[t, h] = (states_ref[rows].astype(jnp.float32) + total).astype(jnp.bfloat16)

            @pl.when(t < count - 1)
            def _():
                pass_on(t, h, True).start()

            @pl.when(t > 0)
            def _():
                pass_on(t, h, False).start()

        for copy in tails:
            copy.wait_recv()
        total = tail_send[...].astype(jnp.float32)
        for k in range(count - 1):
            total = total + tail_land[k].astype(jnp.float32)
        full_ref[byte_rows:] = (edge_ref[...].astype(jnp.float32) + total).astype(jnp.bfloat16)

        for d in range(1, count):
            for h in range(chunks):

                @pl.when(t - d >= 0)
                def _():
                    pass_on(t - d, h, True).wait_recv()

                    @pl.when(t < count - 1)
                    def _():
                        pass_on(t - d, h, True).start()

                @pl.when(t + d < count)
                def _():
                    pass_on(t + d, h, False).wait_recv()

                    @pl.when(t > 0)
                    def _():
                        pass_on(t + d, h, False).start()

        for q in range(count):
            for h in range(chunks):
                begin = q * share + h * piece
                full_ref[begin : begin + piece] = blocks[q, h]
                enc_ref[begin : begin + piece] = blocks[q, h]
        for load in loads:
            load.wait()

        where_at = lax.broadcasted_iota(jnp.int32, (slots, total_rows), 1)
        allowed = (where_at >= lo_ref[...]) & (where_at < hi_ref[...])
        in_use = used_ref[...] > 0.0
        member = jnp.where(allowed & in_use, 1.0, 0.0)
        lengths = jnp.maximum(jnp.sum(member, axis=1, keepdims=True), 1.0)
        totals = jnp.dot(
            member.astype(jnp.bfloat16), full_ref[...], preferred_element_type=jnp.float32
        )
        pooled_ref[...] = (totals / lengths).astype(jnp.bfloat16)

        def across(k, i):
            return pltpu.make_async_remote_copy(
                src_ref=panels.at[i],
                dst_ref=z_land.at[k - 1, i],
                send_sem=z_send.at[k - 1, i],
                recv_sem=z_recv.at[k - 1, i],
                device_id=tp_peer(lax.rem(t + k, count)),
                device_id_type=MESH,
            )

        def heads(i, carry):
            cols = pl.ds(pl.multiple_of(i * group, group), group)
            rows = full_ref[...]
            lifted = jnp.dot(pooled_ref[...], lift_ref[:, cols], preferred_element_type=jnp.float32)
            keys = jnp.dot(rows, cross_ref[0, :, cols], preferred_element_type=jnp.float32).astype(
                jnp.bfloat16
            )
            values = jnp.dot(
                rows, cross_ref[1, :, cols], preferred_element_type=jnp.float32
            ).astype(jnp.bfloat16)
            queries = lifted.astype(jnp.bfloat16)
            crossed = []
            for j in range(2):
                lanes = slice(j * HD, (j + 1) * HD)
                scores = lax.dot_general(
                    queries[:, lanes],
                    keys[:, lanes],
                    (((1,), (1,)), ((), ())),
                    preferred_element_type=jnp.float32,
                ) * (1.0 / math.sqrt(HD))
                weights = masked_softmax(scores, allowed).astype(jnp.bfloat16)
                crossed.append(
                    jnp.dot(weights, values[:, lanes], preferred_element_type=jnp.float32)
                )
            patch = lifted + jnp.concatenate(crossed, axis=1)
            panel = jnp.where(in_use, patch, 0.0).astype(jnp.bfloat16)
            patch_ref[:, cols] = panel
            panels[i] = panel
            for k in range(1, count):
                across(k, i).start()
            return carry

        lax.fori_loop(0, panel_count, heads, 0)
        onward = []
        for i in range(panel_count):
            for k in range(count):
                origin = lax.rem(t + count - k, count)
                if k == 0:
                    here = panels.at[i]
                else:
                    across(k, i).wait_recv()
                    here = z_land.at[k - 1, i]
                away = pltpu.make_async_remote_copy(
                    src_ref=here,
                    dst_ref=rows_ref.at[p, i],
                    send_sem=plane_send.at[k, i],
                    recv_sem=plane_recv.at[p, i],
                    device_id=plane(origin),
                    device_id_type=MESH,
                )
                stay = pltpu.make_async_copy(here, rows_ref.at[p, i], stay_sems.at[i])
                onward.append((origin, away, stay))

                @pl.when(origin != p)
                def _():
                    away.start()

                @pl.when(origin == p)
                def _():
                    stay.start()

        for q in range(count):

            @pl.when(p != q)
            def _():
                for i in range(panel_count):
                    pltpu.make_async_remote_copy(
                        src_ref=panels.at[i],
                        dst_ref=rows_ref.at[q, i],
                        send_sem=plane_send.at[q, i],
                        recv_sem=plane_recv.at[q, i],
                        device_id=plane(p),
                        device_id_type=MESH,
                    ).wait_recv()

        for i in range(panel_count):
            for k in range(1, count):
                across(k, i).wait_send()
        for origin, away, stay in onward:

            @pl.when(origin != p)
            def _():
                away.wait_send()

            @pl.when(origin == p)
            def _():
                stay.wait()

        for h in range(chunks):
            for copy in scatter[h]:
                copy.wait_send()
        for copy in tails:
            copy.wait_send()
        for q in range(count):
            for h in range(chunks):

                @pl.when((q <= t) & (t < count - 1))
                def _():
                    pass_on(q, h, True).wait_send()

                @pl.when((q >= t) & (t > 0))
                def _():
                    pass_on(q, h, False).wait_send()

    vmem = pl.BlockSpec(memory_space=pltpu.VMEM)
    hbm = pl.BlockSpec(memory_space=pl.ANY)
    dma = pltpu.SemaphoreType.DMA
    return pl.pallas_call(
        kernel,
        out_shape=[
            like((byte_rows, width)),
            like((slots, columns)),
            like((count, panel_count, slots, group)),
        ],
        in_specs=[vmem] * 9 + [hbm] * 2,
        out_specs=[vmem, vmem, hbm],
        scratch_shapes=[
            pltpu.VMEM((count, chunks, piece, width), jnp.bfloat16),
            pltpu.VMEM((chunks, count - 1, piece, width), jnp.bfloat16),
            pltpu.VMEM((EDGE, width), jnp.bfloat16),
            pltpu.VMEM((count - 1, EDGE, width), jnp.bfloat16),
            pltpu.VMEM((count, chunks, piece, width), jnp.bfloat16),
            pltpu.VMEM(lift.shape, lift.dtype),
            pltpu.VMEM(cross_kv.shape, cross_kv.dtype),
            pltpu.VMEM((slots, width), jnp.bfloat16),
            pltpu.VMEM((total_rows, width), jnp.bfloat16),
            pltpu.VMEM((panel_count, slots, group), jnp.bfloat16),
            pltpu.VMEM((count - 1, panel_count, slots, group), jnp.bfloat16),
            dma((2,)),
            dma((chunks, count - 1)),
            dma((chunks, count - 1)),
            dma((count - 1,)),
            dma((count - 1,)),
            dma((count, chunks)),
            dma((count, chunks)),
            dma((count, chunks)),
            dma((count - 1, panel_count)),
            dma((count - 1, panel_count)),
            dma((count, panel_count)),
            dma((count, panel_count)),
            dma((panel_count,)),
        ],
        compiler_params=pltpu.CompilerParams(collective_id=call_id, has_side_effects=True),
    )(projected, behind, edge, proj, byte_states, edge_states, *bounds, used, lift, cross_kv)


def latent_stage(rows, patches, used, gain, weights, projs, cosine, sine, query_pos, key_pos, call_id):
    count = lax.axis_size("tp")
    pair_count, panel_count, slot_count, group = rows.shape
    row_total, chip_width = pair_count * slot_count, panel_count * group
    half = chip_width // 2
    slots, columns = patches.shape
    full_width = columns * count

    def kernel(
        rows_ref, patch_ref, used_ref, gain_ref, cos_ref, sin_ref, qpos_ref, kpos_ref,
        w_own_hbm, w_other_hbm, o_own_hbm, o_other_hbm,
        out_ref,
        w_own, w_other, o_own, o_other, geared, qkv_send, qkv_land, sq_send, sq_land,
        kv_own, kv_other, att_all, parts, land, final,
        load_sems, qkv_s, qkv_r, sq_s, sq_r, kv_sems, att_s, att_r, a_s, a_r, b_s, b_r,
    ):
        s, t = lax.axis_index("seq"), lax.axis_index("tp")
        p, c = s // 2, lax.rem(s, 2)
        pair_refs = ((w_own_hbm, w_own), (w_other_hbm, w_other), (o_own_hbm, o_own), (o_other_hbm, o_other))
        loads = [
            pltpu.make_async_copy(source, target, load_sems.at[i])
            for i, (source, target) in enumerate(pair_refs)
        ]
        for load in loads:
            load.start()

        def plane(index):
            return {"seq": 2 * index + c}

        partner = seq_peer(s + 1 - 2 * c)
        greet(
            [plane(lax.rem(p + k, count)) for k in range(1, count)]
            + [tp_peer(lax.rem(t + k, count)) for k in range(1, count)]
            + [partner]
        )

        def send(source, target, send_sem, recv_sem, device):
            return pltpu.make_async_remote_copy(
                src_ref=source,
                dst_ref=target,
                send_sem=send_sem,
                recv_sem=recv_sem,
                device_id=device,
                device_id_type=MESH,
            )

        values = jnp.concatenate(
            [rows_ref[:, i].reshape(row_total, group) for i in range(panel_count)], axis=1
        ).astype(jnp.float32)
        squares = jnp.sum(values * values, axis=1, keepdims=True)
        eye = lax.broadcasted_iota(jnp.int32, (row_total, row_total), 0) == lax.broadcasted_iota(
            jnp.int32, (row_total, row_total), 1
        )
        flat = jnp.sum(jnp.where(eye, squares, 0.0), axis=0, keepdims=True)
        sq_send[...] = jnp.broadcast_to(flat, sq_send.shape)
        geared[...] = (values * gain_ref[...]).astype(jnp.bfloat16)
        sent = []
        for k in range(1, count):
            copy = send(
                sq_send, sq_land.at[k - 1], sq_s.at[k - 1], sq_r.at[k - 1], plane(lax.rem(p + k, count))
            )
            copy.start()
            sent.append(copy)
        loads[0].wait()
        loads[1].wait()
        mine = geared[:, pl.ds(pl.multiple_of(c * half, half), half)]
        theirs = geared[:, pl.ds(pl.multiple_of((1 - c) * half, half), half)]
        total = []
        for k in list(range(1, count)) + [0]:
            target = lax.rem(p + k, count)
            lanes = pl.ds(pl.multiple_of(target * HD, HD), HD)
            for i in range(3):
                part = jnp.dot(
                    mine, w_own[i, :, lanes], preferred_element_type=jnp.float32
                ) + jnp.dot(theirs, w_other[i, :, lanes], preferred_element_type=jnp.float32)
                if k:
                    qkv_send[k - 1, i] = part.astype(jnp.bfloat16)
                else:
                    total.append(part)
            if k:
                copy = send(
                    qkv_send.at[k - 1], qkv_land.at[k - 1], qkv_s.at[k - 1], qkv_r.at[k - 1], plane(target)
                )
                copy.start()
                sent.append(copy)
        for copy in sent:
            copy.wait_recv()
        flat = flat + jnp.sum(sq_land[:, 0:1, :], axis=0)
        square_sum = jnp.sum(jnp.where(eye, flat, 0.0), axis=1, keepdims=True)
        scale = lax.rsqrt(square_sum / full_width + epsilon)
        for i in range(3):
            for k in range(count - 1):
                total[i] = total[i] + qkv_land[k, i].astype(jnp.float32)
            total[i] = total[i] * scale

        def turned(vectors):
            return (
                vectors * cos_ref[...] + pltpu.roll(vectors, HD // 2, 1) * sin_ref[...]
            ).astype(jnp.bfloat16)

        queries = turned(total[0])
        kv_own[0] = turned(total[1])
        kv_own[1] = total[2].astype(jnp.bfloat16)
        swap = send(kv_own, kv_other, kv_sems.at[0], kv_sems.at[1], partner)
        swap.start()

        def scored(keys, first):
            scores = lax.dot_general(
                queries, keys, (((1,), (1,)), ((), ())), preferred_element_type=jnp.float32
            ) * (1.0 / math.sqrt(HD))
            permitted = kpos_ref[:, first : first + row_total] <= qpos_ref[...]
            return jnp.where(permitted, scores, -1e30), permitted

        scores_a, permitted_a = scored(kv_own[0], 0)
        swap.wait_recv()
        scores_b, permitted_b = scored(kv_other[0], row_total)
        largest = jnp.maximum(
            jnp.max(scores_a, axis=1, keepdims=True), jnp.max(scores_b, axis=1, keepdims=True)
        )
        raised_a = jnp.where(permitted_a, jnp.exp(scores_a - largest), 0.0)
        raised_b = jnp.where(permitted_b, jnp.exp(scores_b - largest), 0.0)
        weight_sum = jnp.sum(raised_a, axis=1, keepdims=True) + jnp.sum(
            raised_b, axis=1, keepdims=True
        )
        weighted = jnp.dot(
            raised_a.astype(jnp.bfloat16), kv_own[1], preferred_element_type=jnp.float32
        ) + jnp.dot(raised_b.astype(jnp.bfloat16), kv_other[1], preferred_element_type=jnp.float32)
        att_all[p] = (weighted / weight_sum).astype(jnp.bfloat16)
        heads = []
        for k in range(1, count):
            copy = send(
                att_all.at[p], att_all.at[p], att_s.at[k - 1], att_r.at[p], plane(lax.rem(p + k, count))
            )
            copy.start()
            heads.append(copy)
        for k in range(1, count):
            source = lax.rem(p + k, count)
            send(
                att_all.at[source], att_all.at[source], att_s.at[k - 1], att_r.at[source], plane(source)
            ).wait_recv()
        loads[2].wait()
        loads[3].wait()
        hops = []
        for k in list(range(1, count)) + [0]:
            target = lax.rem(p + k, count)
            take = pl.ds(pl.multiple_of(target * slots, slots), slots)
            attended = jnp.concatenate([att_all[j, take, :] for j in range(count)], axis=1)
            for output, core in ((o_own, c), (o_other, 1 - c)):
                parts[target, :, pl.ds(pl.multiple_of(core * half, half), half)] = jnp.dot(
                    attended, output[...], preferred_element_type=jnp.float32
                ).astype(jnp.bfloat16)
            if k:
                hop = send(
                    parts.at[target], land.at[k - 1], a_s.at[k - 1], a_r.at[k - 1], plane(target)
                )
                hop.start()
                hops.append(hop)
        onward = []
        for k in range(count):
            origin = lax.rem(p + count - k, count)
            if k == 0:
                here = parts.at[p]
            else:
                hops[k - 1].wait_recv()
                here = land.at[k - 1]
            away = send(here, final.at[t], b_s.at[k], b_r.at[t], tp_peer(origin))
            onward.append((origin, away))

            @pl.when(origin != t)
            def _():
                away.start()

            @pl.when(origin == t)
            def _():
                final[t] = here[...]

        summed = patch_ref[...].astype(jnp.float32)
        for q in range(count):

            @pl.when(t != q)
            def _():
                send(land.at[0], final.at[q], b_s.at[q], b_r.at[q], tp_peer(t)).wait_recv()

            summed = summed + final[q].astype(jnp.float32)
        out_ref[...] = jnp.where(used_ref[...] > 0.0, summed, 0.0).astype(jnp.bfloat16)
        for copy in sent + heads + hops + [swap]:
            copy.wait_send()
        for origin, away in onward:

            @pl.when(origin != t)
            def _():
                away.wait_send()

    vmem = pl.BlockSpec(memory_space=pltpu.VMEM)
    hbm = pl.BlockSpec(memory_space=pl.ANY)
    dma = pltpu.SemaphoreType.DMA
    near = count - 1
    return pl.pallas_call(
        kernel,
        out_shape=like((slots, columns)),
        in_specs=[vmem] * 8 + [hbm] * 4,
        out_specs=vmem,
        scratch_shapes=[
            pltpu.VMEM(weights[0].shape, jnp.bfloat16),
            pltpu.VMEM(weights[1].shape, jnp.bfloat16),
            pltpu.VMEM(projs[0].shape, jnp.bfloat16),
            pltpu.VMEM(projs[1].shape, jnp.bfloat16),
            pltpu.VMEM((row_total, chip_width), jnp.bfloat16),
            pltpu.VMEM((near, 3, row_total, HD), jnp.bfloat16),
            pltpu.VMEM((near, 3, row_total, HD), jnp.bfloat16),
            pltpu.VMEM((8, row_total), jnp.float32),
            pltpu.VMEM((near, 8, row_total), jnp.float32),
            pltpu.VMEM((2, row_total, HD), jnp.bfloat16),
            pltpu.VMEM((2, row_total, HD), jnp.bfloat16),
            pltpu.VMEM((count, row_total, HD), jnp.bfloat16),
            pltpu.VMEM((count, slots, columns), jnp.bfloat16),
            pltpu.VMEM((near, slots, columns), jnp.bfloat16),
            pltpu.VMEM((count, slots, columns), jnp.bfloat16),
            dma((4,)),
            dma((near,)),
            dma((near,)),
            dma((near,)),
            dma((near,)),
            dma((2,)),
            dma((near,)),
            dma((count,)),
            dma((near,)),
            dma((near,)),
            dma((count,)),
            dma((count,)),
        ],
        compiler_params=pltpu.CompilerParams(collective_id=call_id, has_side_effects=True),
    )(rows, patches, used, gain, cosine, sine, query_pos, key_pos, *weights, *projs)


def shards(
    byte_states,
    enc_gain,
    enc_qkv,
    enc_proj_out,
    starts,
    counts,
    lift,
    cross_kv,
    latent_gain,
    lat_qkv,
    lat_proj_out,
):
    size, tp_size = lax.axis_size("seq"), lax.axis_size("tp")
    s, t = lax.axis_index("seq"), lax.axis_index("tp")
    pairs = size // 2
    p, c = s // 2, lax.rem(s, 2)
    byte_rows = byte_states.shape[0]
    anchor = s * byte_rows
    both = [(i, i ^ 1) for i in range(size)]
    lat_qkv_other = lax.ppermute(lat_qkv, "seq", both)
    lat_proj_other = lax.ppermute(lat_proj_out, "seq", both)
    states = byte_states.astype(jnp.float32)
    normed = rms_scale(states, enc_gain.astype(jnp.float32)).astype(jnp.bfloat16)
    projected = jnp.einsum(
        "bd,idc->ibc", normed, enc_qkv, preferred_element_type=jnp.float32
    ).astype(jnp.bfloat16)
    patch_count = counts[0]
    local_starts = starts[0]
    lanes = lax.broadcasted_iota(jnp.int32, (8, 128), 1)
    info = jnp.where(lanes == 0, patch_count, jnp.where(lanes == 1, local_starts[0], 0))
    behind, edge, edge_states, infos = halo(projected, byte_states, info)
    recent = jnp.concatenate([info[None], infos], axis=0)
    ring = jnp.arange(size, dtype=jnp.int32)
    from_ring = lax.rem(s - ring + size, size)
    placed = from_ring[None, :] == ring[:, None]
    count_list = jnp.sum(jnp.where(placed, recent[None, :, 0, 0], 0), axis=1)
    offsets = jnp.sum(jnp.where(ring[None, :] < ring[:, None], count_list[None, :], 0), axis=1)
    next_first = jnp.where(s + 1 < size, recent[size - 1, 0, 1], size * byte_rows)

    slot_total = local_starts.shape[0]
    slot_ids = jnp.arange(slot_total, dtype=jnp.int32)
    in_use = slot_ids < patch_count
    following = jnp.concatenate([local_starts[1:], jnp.zeros((1,), jnp.int32)])
    patch_end = jnp.where(slot_ids + 1 < patch_count, following, next_first)
    lower = jnp.where(in_use, local_starts - anchor, 0)[:, None]
    upper = jnp.where(in_use, patch_end - anchor, 1)[:, None]
    used_rows = in_use.astype(jnp.float32)[:, None]
    encoded, patches, rows = encode_and_patch(
        projected,
        behind,
        edge,
        enc_proj_out,
        byte_states,
        edge_states,
        (lower, upper),
        used_rows,
        lift,
        cross_kv,
        2,
    )

    def slots_of(core):
        members = 2 * jnp.arange(pairs, dtype=jnp.int32) + core
        hit = members[:, None] == ring[None, :]
        begin = jnp.sum(jnp.where(hit, offsets[None, :], 0), axis=1)
        used = jnp.sum(jnp.where(hit, count_list[None, :], 0), axis=1)
        position = (begin[:, None] + slot_ids[None, :]).reshape(-1)
        return position, (slot_ids[None, :] < used[:, None]).reshape(-1)

    position, rows_used = slots_of(c)
    other_position, other_used = slots_of(1 - c)

    half = lat_qkv.shape[1]
    gain = lax.dynamic_slice_in_dim(latent_gain, p * 2 * half, 2 * half, 0).astype(jnp.float32)
    frequency = jnp.power(
        rope_base, -2.0 * jnp.arange(HD // 2, dtype=jnp.float32) / HD
    )
    angles = position.astype(jnp.float32)[:, None] * frequency[None, :]
    sine = jnp.sin(angles)
    cosine = jnp.cos(angles)
    key_position = jnp.concatenate(
        [
            jnp.where(rows_used, position, far_position),
            jnp.where(other_used, other_position, far_position),
        ]
    )
    latent = latent_stage(
        rows,
        patches,
        used_rows,
        gain[None],
        (lat_qkv, lat_qkv_other),
        (lat_proj_out, lat_proj_other),
        jnp.concatenate([cosine, cosine], axis=1),
        jnp.concatenate([-sine, sine], axis=1),
        position[:, None],
        key_position[None, :],
        5,
    )
    return (encoded, latent)


def fits_pairs(mesh, byte_states, enc_qkv, starts, lat_qkv):
    size, tp_size = mesh.shape["seq"], mesh.shape["tp"]
    byte_rows = byte_states.shape[0] // size
    return (
        size == 2 * tp_size
        and WIN % byte_rows == 0
        and WIN // byte_rows < size
        and byte_rows % (32 * tp_size) == 0
        and lat_qkv.shape[2] // tp_size == HD * tp_size
        and lat_qkv.shape[1] % (128 * size) == 0
        and starts.shape[1] * tp_size % 128 == 0
        and starts.shape[1] * tp_size <= 1024
        and starts.shape[1] % 16 == 0
        and enc_qkv.shape[2] % (128 * tp_size) == 0
    )


def solution(mesh):
    specs = dict(
        mesh=mesh,
        in_specs=(
            P("seq", None),
            P(),
            P(None, None, "tp"),
            P("tp", None),
            P("seq", None),
            P("seq"),
            P(None, "tp"),
            P(None, None, "tp"),
            P(),
            P(None, "seq", "tp"),
            P("tp", "seq"),
        ),
        out_specs=(P("seq", None), P("seq", "tp")),
        check_vma=False,
    )

    def run(*arrays):
        paired = fits_pairs(mesh, arrays[0], arrays[2], arrays[4], arrays[9])
        return jax.shard_map(shards if paired else gathered_shards, **specs)(*arrays)

    return run
```

profile of v0, /device:TPU:6, one launch (start us, length us, event | category | flops | bytes accessed | tf_op | source)
XLA Modules:
  0.0 126.4 jit_solution(13087187639096244877)
XLA Ops:
  0.7 0.5 collective-permute-start
  1.9 0.7 slice_bitcast_fusion
  2.6 0.6 compare_select_fusion.2
  3.3 0.7 subtract_bitcast_fusion
  4.0 1.2 fusion.1
  5.2 0.6 broadcast_select_fusion.1.refs_2_
  5.8 0.7 convert_element_type.36
  6.8 2.4 %fusion.refs_0_.own_ref = bf16[3,256,256]{2,1,0:T(8,128)(2,1)} fusion(bf16[3,1024,256]{2,1,0:T(8,128)(2,1)S(1)} %copy-done, bf16[256,1024]{1,0:T(8,128)(2,1)} %states_ref.1, f32[1024]{0:T(1024)S(1)} %convert_element_type.36, f32[256]{0:T(256)S(1)} %add_rsqrt_fusion), kind=kOutput, calls=%fused_computation.3 | convolution fusion | flops 403898368 | bytes 2495488 | tf_op jit(solution)/shard_map/bd,idc->ibc/dot_general | solution.py:949
  9.2 13.9 %shard_map.122 = (bf16[2,2,256,256]{3,2,1,0:T(8,128)(2,1)}, bf16[3,16,256]{2,1,0:T(8,128)(2,1)}, bf16[16,1024]{1,0:T(8,128)(2,1)}, s32[7,8,128]{2,1,0:T(8,128)}) custom-call(bf16[3,256,256]{2,1,0:T(8,128)(2,1)} %fusion.refs_0_.own_ref, bf16[256,1024]{1,0:T(8,128)(2,1)} %states_ref.1, s32[8,128]{1,0:T(8,128)} %broadcast_select_fusion.1.refs_2_), custom_call_target="tpu_custom_call" | custom-call | tf_op jit(solution)/shard_map/pallas_call | solution.py:292
  23.0 1.3 slice.16
  24.3 1.0 fusion.11
  26.1 0.8 add.125.qpos_ref
  27.5 0.6 fusion.9.used_ref
  28.1 0.6 subtract_select_fusion
  28.7 48.1 %shard_map.123 = (bf16[256,1024]{1,0:T(8,128)(2,1)}, bf16[64,1024]{1,0:T(8,128)(2,1)}, bf16[4,4,64,256]{3,2,1,0:T(8,128)(2,1)}) custom-call(bf16[3,256,256]{2,1,0:T(8,128)(2,1)} %fusion.refs_0_.own_ref, bf16[2,2,256,256]{3,2,1,0:T(8,128)(2,1)} %get-tuple-element.9.behind_ref, bf16[3,16,256]{2,1,0:T(8,128)(2,1)} %get-tuple-element.10.next_ref, ...), custom_call_target="tpu_custom_call" | custom-call | tf_op jit(solution)/shard_map/pallas_call | solution.py:651
  76.9 0.6 pad_add_fusion.1
  77.5 1.3 %dynamic-slice_convert_fusion = f32[1024]{0:T(1024)} fusion(bf16[4096]{0:T(1024)(128)(2,1)} %param.19, s32[]{:T(128)S(6)} %select_n.95), kind=kLoop, calls=%fused_computation.40 | loop fusion | flops 1024 | bytes 6148 | tf_op jit(solution)/shard_map/broadcast_in_dim | solution.py:1016
  78.7 0.5 fusion.8
  79.3 0.8 pad_maximum_fusion.cos_ref
  80.0 0.8 pad_maximum_fusion.1.sin_ref
  80.8 1.2 copy-done.1
  82.0 41.0 %shard_map.124 = bf16[64,1024]{1,0:T(8,128)(2,1)} custom-call(bf16[4,4,64,256]{3,2,1,0:T(8,128)(2,1)} %get-tuple-element.14.rows_ref, bf16[64,1024]{1,0:T(8,128)(2,1)} %get-tuple-element.15.patch_ref, f32[64,1]{1,0:T(8,128)} %fusion.9.used_ref, f32[1,1024]{1,0:T(1,128)} %bitcast.20, f32[256,128]{1,0:T(8,128)} %pad_maximum_fusion.cos_ref, ...), custom_call_target="tpu_custom_call" | custom-call | tf_op jit(solution)/shard_map/pallas_call | solution.py:887
  123.0 1.9 %copy.27 = bf16[256,1024]{1,0:T(8,128)(2,1)} copy(bf16[256,1024]{1,0:T(8,128)(2,1)} %get-tuple-element.31) | data formatting | bytes 1048576
  124.8 1.6 %copy.28 = bf16[64,1024]{1,0:T(8,128)(2,1)} copy(bf16[64,1024]{1,0:T(8,128)(2,1)} %shard_map.124) | data formatting | bytes 262144
  (23 shorter events, 1.2 us)
Async XLA Ops:
  0.6 6.1 %copy-start = (bf16[3,1024,256]{2,1,0:T(8,128)(2,1)S(1)}, bf16[3,1024,256]{2,1,0:T(8,128)(2,1)}, u32[]{:S(2)}) copy-start(bf16[3,1024,256]{2,1,0:T(8,128)(2,1)} %param.13) | copy-start | bytes 4718596
  0.6 80.2 %collective-permute-start.1 = (bf16[512,512]{1,0:T(8,128)(2,1)}, bf16[512,512]{1,0:T(8,128)(2,1)}, u32[]{:S(2)}, u32[]{:S(2)}) collective-permute-start(bf16[512,512]{1,0:T(8,128)(2,1)} %o_own_hbm.1), channel_id=1, source_target_pairs={{0,4},{4,0},{8,12},{12,8},{16,20},{20,16},{24,28},{28,24},{1,5},{5... | collective-permute-start | bytes 1572872 | tf_op jit(solution)/shard_map/ppermute | solution.py:946
  0.7 80.1 %collective-permute-start = (bf16[3,512,512]{2,1,0:T(8,128)(2,1)}, bf16[3,512,512]{2,1,0:T(8,128)(2,1)S(1)}, u32[]{:S(2)}, u32[]{:S(2)}) collective-permute-start(bf16[3,512,512]{2,1,0:T(8,128)(2,1)} %w_own_hbm.1), channel_id=1, source_target_pairs={{0,4},{4,0},{8,12},{12,8},{16,20},{20,16},{24,28},{28,24},{1,5},{5... | collective-permute-start | bytes 4718600 | tf_op jit(solution)/shard_map/ppermute | solution.py:945
  80.8 1.2 copy-start.1
where the time goes:
time: 127 us; the launch traced here: 126 us
  Pallas kernels  103 us (81%)
  other arithmetic  10.6 us (8%)
  local copies, waits for them, and re-layouts  7.81 us (6%)
  matrix products  2.42 us (2%)
  between operations  2.05 us (2%)
    pallas_call x1, Pallas kernels, encode_and_patch(): pl.pallas_call(kernel, out_shape=[like((byte_rows, width)), like((slots,...  48.1 us
    pallas_call x1, Pallas kernels, latent_stage(): pl.pallas_call(kernel, out_shape=like((slots, columns)), in_specs=[vmem]...  41 us
    pallas_call x1, Pallas kernels, exchange(): pl.pallas_call(kernel, out_shape=out_shapes, in_specs=[pl.BlockSpec(memor...  13.9 us
    unnamed x6, local copies, waits for them, and re-layouts  4.6 us
  transfers between devices with their start and end apart: 2, of which 0 were waited for; matrix products, arithmetic and copies ran while one was open for 13% of the time, Pallas kernels for 49%

commit v1 on v0

v1 whole, which is shorter than its diff:
```python
import math

import jax
import numpy as np
import jax.numpy as jnp
from jax import lax
from jax.experimental import pallas as pl
from jax.experimental.pallas import tpu as pltpu
from jax.sharding import PartitionSpec as P

EH = 64
HD = 128
WIN = 512
SPILL = 8


epsilon = 1e-05
rope_base = 500000.0
far_position = 1 << 30


def from_behind(value, axis, steps):
    count = lax.axis_size(axis)
    leading, last = (max(0, -steps), min(count, count - steps))
    return lax.ppermute(value, axis, [(source, source + steps) for source in range(leading, last)])


def prefix(value, axis, join, neutral):
    count, mine = (lax.axis_size(axis), lax.axis_index(axis))
    pieces = lax.all_gather(value, axis)
    subtotal = jnp.full_like(value, 0) + jnp.asarray(neutral, value.dtype)

    def hop(position, subtotal):
        longer = join(subtotal, pieces[position])
        return jnp.where(position < mine, longer, subtotal)

    return lax.fori_loop(0, count - 1, hop, subtotal)


def shortened(value):

    def short(part):
        return part.astype(jnp.bfloat16) if part.dtype == jnp.float32 else part

    return jax.tree.map(short, value)


def rms_scale(values, gain_row):
    mean_square = jnp.mean(values * values, axis=-1, keepdims=True)
    return values * lax.rsqrt(mean_square + epsilon) * gain_row


def masked_softmax(scores, allowed):
    scores = jnp.where(allowed, scores, -1e30)
    largest = jnp.max(scores, axis=-1, keepdims=True)
    raised = jnp.where(allowed, jnp.exp(scores - largest), 0.0)
    return raised / jnp.sum(raised, axis=-1, keepdims=True)


def rotate(values, position):
    halfway = values.shape[-1] // 2
    frequency = jnp.power(
        rope_base, -2.0 * jnp.arange(halfway, dtype=jnp.float32) / values.shape[-1]
    )
    angles = position.astype(jnp.float32)[:, None] * frequency[None, :]
    cosine = jnp.cos(angles)[:, None, :]
    sine_rows = jnp.sin(angles)[:, None, :]
    lower_half = values[..., :halfway]
    upper_half = values[..., halfway:]
    return jnp.concatenate(
        [
            lower_half * cosine - upper_half * sine_rows,
            upper_half * cosine + lower_half * sine_rows,
        ],
        axis=-1,
    )


def patch_block(extended, first_byte, end_byte, in_use, anchor, lift, cross_kv):
    columns = anchor + jnp.arange(extended.shape[0], dtype=jnp.int32)
    inside = (
        (columns[None, :] >= first_byte[:, None])
        & (columns[None, :] < end_byte[:, None])
        & in_use[:, None]
    )
    member = inside.astype(jnp.bfloat16)
    totals = jnp.dot(member, extended, preferred_element_type=jnp.float32)
    lengths = jnp.maximum(jnp.sum(inside.astype(jnp.float32), axis=1), 1.0)
    pooled = (totals / lengths[:, None]).astype(jnp.bfloat16)
    lifted = jnp.dot(pooled, lift, preferred_element_type=jnp.float32)
    key_rows = jnp.dot(extended, cross_kv[0], preferred_element_type=jnp.float32).astype(
        jnp.bfloat16
    )
    value_rows = jnp.dot(extended, cross_kv[1], preferred_element_type=jnp.float32).astype(
        jnp.bfloat16
    )
    slot_total = first_byte.shape[0]
    head_count = lifted.shape[1] // HD
    queries = lifted.astype(jnp.bfloat16).reshape(slot_total, head_count, HD)
    scores = jnp.einsum(
        "phd,khd->hpk",
        queries,
        key_rows.reshape(-1, head_count, HD),
        preferred_element_type=jnp.float32,
    ) * (1.0 / math.sqrt(HD))
    allowed = inside | (~in_use)[:, None] & (columns[None, :] == anchor)
    weights = masked_softmax(scores, allowed[None]).astype(jnp.bfloat16)
    crossed = jnp.einsum(
        "hpk,khd->phd",
        weights,
        value_rows.reshape(-1, head_count, HD),
        preferred_element_type=jnp.float32,
    )
    crossed = crossed.reshape(slot_total, head_count * HD)
    return jnp.where(in_use[:, None], lifted + crossed, 0.0).astype(jnp.bfloat16)


def add_counts(earlier, later):
    return earlier + later


def gathered_shards(
    byte_states,
    enc_gain,
    enc_qkv,
    enc_proj_out,
    starts,
    counts,
    lift,
    cross_kv,
    latent_gain,
    lat_qkv,
    lat_proj_out,
):
    byte_rows = byte_states.shape[0]
    anchor = lax.axis_index("seq") * byte_rows
    states = byte_states.astype(jnp.float32)
    normed = rms_scale(states, enc_gain.astype(jnp.float32)).astype(jnp.bfloat16)
    projected = jnp.einsum(
        "bd,idc->ibc", normed, enc_qkv, preferred_element_type=jnp.float32
    ).astype(jnp.bfloat16)
    reach_blocks = max(WIN // byte_rows, 1)
    tail_rows = min(WIN, byte_rows)
    key_parts = []
    value_parts = []
    for distance in range(reach_blocks, 0, -1):
        moved_keys, moved_values = from_behind(
            (projected[1, byte_rows - tail_rows :], projected[2, byte_rows - tail_rows :]),
            "seq",
            distance,
        )
        key_parts.append(moved_keys)
        value_parts.append(moved_values)
    key_rows = jnp.concatenate(key_parts + [projected[1]], axis=0)
    value_rows = jnp.concatenate(value_parts + [projected[2]], axis=0)
    head_count = projected.shape[2] // EH
    scores = jnp.einsum(
        "qhd,khd->hqk",
        projected[0].reshape(byte_rows, head_count, EH),
        key_rows.reshape(-1, head_count, EH),
        preferred_element_type=jnp.float32,
    ) * (1.0 / math.sqrt(EH))
    query_pos = anchor + jnp.arange(byte_rows, dtype=jnp.int32)
    key_pos = anchor - WIN + jnp.arange(WIN + byte_rows, dtype=jnp.int32)
    allowed = (
        (key_pos[None, :] <= query_pos[:, None])
        & (key_pos[None, :] > query_pos[:, None] - WIN)
        & (key_pos[None, :] >= 0)
    )
    weights = masked_softmax(scores, allowed[None]).astype(jnp.bfloat16)
    attended = jnp.einsum(
        "hqk,khd->qhd",
        weights,
        value_rows.reshape(-1, head_count, EH),
        preferred_element_type=jnp.float32,
    )
    attended = attended.reshape(byte_rows, head_count * EH).astype(jnp.bfloat16)
    blended = lax.psum(jnp.dot(attended, enc_proj_out, preferred_element_type=jnp.float32), "tp")
    encoded = (states + blended).astype(jnp.bfloat16)
    patch_count = counts[0]
    local_starts = starts[0]
    first_local = (local_starts[0:1] - anchor).astype(jnp.bfloat16)
    next_rows, next_first = from_behind((encoded[:SPILL], first_local), "seq", -1)
    next_first = next_first.astype(jnp.int32)[0]
    extended = jnp.concatenate([encoded, next_rows], axis=0)
    slot_ids = jnp.arange(local_starts.shape[0], dtype=jnp.int32)
    in_use = slot_ids < patch_count
    following = jnp.concatenate([local_starts[1:], jnp.zeros((1,), jnp.int32)])
    patch_end = jnp.where(slot_ids + 1 < patch_count, following, anchor + byte_rows + next_first)
    patches = patch_block(extended, local_starts, patch_end, in_use, anchor, lift, cross_kv)
    offset = prefix(counts, "seq", add_counts, jnp.zeros((1,), jnp.int32))[0]
    position = offset + slot_ids
    slot_total = patches.shape[0]
    full_rows = lax.all_gather(patches, "tp", axis=1, tiled=True)
    normed_rows = rms_scale(full_rows.astype(jnp.float32), latent_gain.astype(jnp.float32)).astype(
        jnp.bfloat16
    )
    inner_width = lat_qkv.shape[2]
    projected = jnp.einsum(
        "pd,idc->ipc",
        normed_rows,
        lax.all_gather(lat_qkv, "seq", axis=1, tiled=True),
        preferred_element_type=jnp.float32,
    )
    heads_here = inner_width // HD
    queries = rotate(projected[0].reshape(slot_total, heads_here, HD), position).astype(
        jnp.bfloat16
    )
    latent_keys = (
        rotate(projected[1].reshape(slot_total, heads_here, HD), position)
        .astype(jnp.bfloat16)
        .reshape(slot_total, inner_width)
    )
    latent_values = projected[2].astype(jnp.bfloat16)
    latent_pos = jnp.where(in_use, position, far_position)
    largest = jnp.full((heads_here, slot_total), -1e30, jnp.float32)
    piece_keys = lax.all_gather(latent_keys, "seq", axis=0, tiled=True)
    piece_values = lax.all_gather(latent_values, "seq", axis=0, tiled=True)
    piece_pos = lax.all_gather(shortened(latent_pos), "seq", axis=0, tiled=True)
    rows_here = piece_keys.shape[0]
    piece_scores = jnp.einsum(
        "qhd,khd->hqk",
        queries,
        piece_keys.reshape(rows_here, heads_here, HD),
        preferred_element_type=jnp.float32,
    ) * (1.0 / math.sqrt(HD))
    permitted = (piece_pos[None, :] <= position[:, None])[None]
    piece_scores = jnp.where(permitted, piece_scores, -1e30)
    renewed = jnp.maximum(largest, jnp.max(piece_scores, axis=-1))
    raised = jnp.where(permitted, jnp.exp(piece_scores - renewed[..., None]), 0.0)
    weight_sum = jnp.sum(raised, axis=-1)
    weighted = jnp.einsum(
        "hqk,khd->hqd",
        raised.astype(jnp.bfloat16),
        piece_values.reshape(rows_here, heads_here, HD),
        preferred_element_type=jnp.float32,
    )
    largest, weight_sum, weighted = (renewed, weight_sum, weighted)
    latent_heads = (
        (weighted / weight_sum[..., None])
        .transpose(1, 0, 2)
        .reshape(slot_total, inner_width)
        .astype(jnp.bfloat16)
    )
    partials = jnp.dot(
        latent_heads,
        lax.all_gather(lat_proj_out, "seq", axis=1, tiled=True),
        preferred_element_type=jnp.float32,
    )
    reduced = lax.psum_scatter(partials, "tp", scatter_dimension=1, tiled=True)
    latent = jnp.where(in_use[:, None], patches.astype(jnp.float32) + reduced, 0.0).astype(
        jnp.bfloat16
    )
    return (encoded, latent)


MESH = pl.DeviceIdType.MESH
EDGE = 16


def seq_peer(index):
    return {"seq": index}


def tp_peer(index):
    return {"tp": index}


def like(shape, dtype=jnp.bfloat16):
    return jax.ShapeDtypeStruct(shape, dtype)


def iota(shape, axis):
    return lax.broadcasted_iota(jnp.int32, shape, axis)


def across_lanes(left, right):
    return lax.dot_general(
        left, right, (((1,), (1,)), ((), ())), preferred_element_type=jnp.float32
    )


def product(left, right):
    return jnp.dot(left, right, preferred_element_type=jnp.float32)


def remote(source, target, send_sem, recv_sem, device):
    return pltpu.make_async_remote_copy(
        src_ref=source,
        dst_ref=target,
        send_sem=send_sem,
        recv_sem=recv_sem,
        device_id=device,
        device_id_type=MESH,
    )


def turn_table(rows):
    frequency = rope_base ** (-2.0 * np.arange(HD // 2, dtype=np.float64) / HD)
    frequency = frequency.astype(np.float32)
    angles = np.arange(rows, dtype=np.float32)[:, None] * frequency[None, :]
    angles = angles.astype(np.float64)
    return np.concatenate([np.cos(angles), np.sin(angles)], axis=1).astype(np.float32)


def whole_layer(
    states, gain, enc_qkv, proj, starts, counts, lift, cross_kv, latent_gain, lat_qkv, lat_proj,
    table, call_id,
):
    count, size = lax.axis_size("tp"), lax.axis_size("seq")
    near = count - 1
    byte_rows, width = states.shape
    total_rows = byte_rows + EDGE
    enc_cols = enc_qkv.shape[2]
    enc_heads = enc_cols // EH
    slots = starts.shape[1]
    columns = lift.shape[1]
    group = 2 * HD
    panel_count = columns // group
    row_total = count * slots
    half = lat_qkv.shape[1]
    full_width = columns * count
    rows_half = byte_rows // 2
    spans = ((0, rows_half), (rows_half, total_rows - rows_half))
    share = enc_cols // 2
    piece = share // count

    def kernel(
        states_hbm, gain_ref, qkv_hbm, proj_hbm, starts_ref, counts_ref, lift_hbm, cross_hbm,
        lgain_ref, w_own_hbm, o_own_hbm, table_ref,
        enc_ref, out_ref,
        states_ref, qkv_ref, query_ref, kv_ref, infos, proj_ref, att_ref,
        lift_ref, cross_ref, pooled_ref, full_ref, panels, z_land, rows_ref, patch_ref,
        w_own, w_other, o_own, o_other, geared, qkv_send, qkv_land, sq_send, sq_land,
        kv_own, kv_other, att_all, parts, land, final,
        load_sems, info_s, info_r, halo_s, halo_r, edge_s, edge_r, pz_s, pz_r, pp_s, pp_r, pc_s, pc_r,
        w_sems, up_send, down_send, ag_recv,
        z_send, z_recv, plane_send, plane_recv, stay_sems,
        qkv_s, qkv_r, sq_s, sq_r, kv_sems, att_s, att_r, a_s, a_r, b_s, b_r,
    ):
        s, t = lax.axis_index("seq"), lax.axis_index("tp")
        p, c = s // 2, lax.rem(s, 2)
        partner = seq_peer(s + 1 - 2 * c)

        def plane(index):
            return {"seq": 2 * index + c}

        def ring(k):
            return lax.rem(s + k + size, size)

        def tower(k):
            return lax.rem(t + k + count, count)

        barrier = pltpu.get_barrier_semaphore()
        for k in range(1, size):
            pl.semaphore_signal(barrier, inc=1, device_id=seq_peer(ring(k)), device_id_type=MESH)
        for k in range(1, count):
            pl.semaphore_signal(barrier, inc=1, device_id=tp_peer(tower(k)), device_id_type=MESH)
        load_plan = (
            (states_hbm, states_ref.at[pl.ds(0, byte_rows)]),
            (qkv_hbm, qkv_ref),
            (proj_hbm.at[pl.ds(0, share)], proj_ref.at[0, 0]),
            (proj_hbm.at[pl.ds(share, share)], proj_ref.at[0, 1]),
            (lift_hbm, lift_ref),
            (cross_hbm, cross_ref),
            (w_own_hbm, w_own),
            (o_own_hbm, o_own),
        )
        loads = [
            pltpu.make_async_copy(source, target, load_sems.at[i])
            for i, (source, target) in enumerate(load_plan)
        ]
        for load in loads:
            load.start()
        sent = []

        def launch(copy):
            copy.start()
            sent.append(copy)
            return copy

        info_lane = iota((8, 128), 1)
        infos[s] = jnp.where(
            info_lane == 0, counts_ref[0], jnp.where(info_lane == 1, starts_ref[0:1, 0:1], 0)
        )
        loads[0].wait()
        values = states_ref[0:byte_rows].astype(jnp.float32)
        normed = rms_scale(values, gain_ref[...].astype(jnp.float32)).astype(jnp.bfloat16)
        own = pl.ds(WIN, byte_rows)
        loads[1].wait()
        for i in range(2):
            kv_ref[i, own] = product(normed, qkv_ref[i + 1]).astype(jnp.bfloat16)
        query_ref[0:byte_rows] = (
            product(normed, qkv_ref[0]) * (1.0 / math.sqrt(EH))
        ).astype(jnp.bfloat16)
        pl.semaphore_wait(barrier, size - 1 + count - 1)

        reach = WIN // byte_rows
        halos = []
        for k in range(1, reach + 1):
            halos.append(
                launch(
                    remote(
                        kv_ref.at[:, own],
                        kv_ref.at[:, pl.ds(WIN - k * byte_rows, byte_rows)],
                        halo_s.at[k - 1],
                        halo_r.at[k - 1],
                        seq_peer(ring(k)),
                    )
                )
            )
        behind = seq_peer(ring(-1))
        edges = [
            launch(remote(source, target, edge_s.at[i], edge_r.at[i], behind))
            for i, (source, target) in enumerate(
                (
                    (kv_ref.at[:, pl.ds(WIN, EDGE)], kv_ref.at[:, pl.ds(WIN + byte_rows, EDGE)]),
                    (query_ref.at[pl.ds(0, EDGE)], query_ref.at[pl.ds(byte_rows, EDGE)]),
                    (states_ref.at[pl.ds(0, EDGE)], states_ref.at[pl.ds(byte_rows, EDGE)]),
                )
            )
        ]
        notes = [
            launch(
                remote(infos.at[s], infos.at[s], info_s.at[k - 1], info_r.at[k - 1], seq_peer(ring(k)))
            )
            for k in range(1, size)
        ]
        mine_at = pl.multiple_of(p * piece, piece)
        lifts = [
            launch(
                remote(
                    proj_hbm.at[pl.ds(pl.multiple_of(c * share + p * piece, piece), piece)],
                    proj_ref.at[k, c, pl.ds(mine_at, piece)],
                    pz_s.at[k - 1],
                    pz_r.at[k - 1],
                    tp_peer(tower(k)),
                )
            )
            for k in range(1, count)
        ]
        swaps = [
            launch(remote(w_own_hbm, w_other, w_sems.at[0], w_sems.at[1], partner)),
            launch(remote(o_own_hbm, o_other, w_sems.at[2], w_sems.at[3], partner)),
        ]
        for copy in lifts:
            copy.wait_recv()
        spread = [
            launch(
                remote(
                    proj_ref.at[pl.ds(1, near), c, pl.ds(mine_at, piece)],
                    proj_ref.at[pl.ds(1, near), c, pl.ds(mine_at, piece)],
                    pp_s.at[k - 1],
                    pp_r.at[k - 1],
                    plane(lax.rem(p + k, count)),
                )
            )
            for k in range(1, count)
        ]
        for copy in halos + edges:
            copy.wait_recv()

        def pass_on(origin, h, up):
            begin, rows = spans[h]
            step = 1 if up else -1
            return remote(
                att_ref.at[origin, pl.ds(begin, rows)],
                att_ref.at[origin, pl.ds(begin, rows)],
                (up_send if up else down_send).at[origin, h],
                ag_recv.at[origin, h],
                tp_peer(tower(step)),
            )

        def attend(begin, rows):
            reach_rows = rows + WIN
            keys = kv_ref[0, begin : begin + reach_rows]
            seen_values = kv_ref[1, begin : begin + reach_rows]
            queries = query_ref[begin : begin + rows]
            head_of = iota((rows, enc_cols), 1) // EH
            stacked = jnp.concatenate(
                [jnp.where(head_of == h, queries, jnp.zeros_like(queries)) for h in range(enc_heads)],
                axis=0,
            )
            query_at = iota((rows, reach_rows), 0) + begin
            key_at = iota((rows, reach_rows), 1) + (begin - WIN)
            near_by = (
                (key_at <= query_at) & (key_at > query_at - WIN) & (key_at >= -s * byte_rows)
            )
            bias = jnp.where(near_by, 0.0, -1e30)
            scores = across_lanes(stacked, keys)
            raised, sums = [], []
            for h in range(enc_heads):
                here = scores[h * rows : (h + 1) * rows] + bias
                here = jnp.exp(here - jnp.max(here, axis=1, keepdims=True))
                sums.append(jnp.sum(here, axis=1, keepdims=True))
                raised.append(here.astype(jnp.bfloat16))
            seen = product(jnp.concatenate(raised, axis=0), seen_values)
            attended = jnp.zeros((rows, enc_cols), jnp.float32)
            for h in range(enc_heads):
                attended = jnp.where(
                    head_of == h, seen[h * rows : (h + 1) * rows] / sums[h], attended
                )
            att_ref[t, begin : begin + rows] = attended.astype(jnp.bfloat16)

        for h in range(2):
            begin, rows = spans[h]
            attend(begin, rows_half)
            if rows > rows_half:
                attend(begin + rows_half, rows - rows_half)

            @pl.when(t < count - 1)
            def _():
                pass_on(t, h, True).start()

            @pl.when(t > 0)
            def _():
                pass_on(t, h, False).start()

        def relay(d, h):
            @pl.when(t - d >= 0)
            def _():
                pass_on(t - d, h, True).wait_recv()

                @pl.when(t < count - 1)
                def _():
                    pass_on(t - d, h, True).start()

            @pl.when(t + d < count)
            def _():
                pass_on(t + d, h, False).wait_recv()

                @pl.when(t > 0)
                def _():
                    pass_on(t + d, h, False).start()

        def finish(h):
            begin, rows = spans[h]
            total = states_ref[begin : begin + rows].astype(jnp.float32)
            for k in range(count):
                total = total + product(
                    att_ref[tower(-k), begin : begin + rows],
                    proj_ref[k].reshape(enc_cols, width),
                )
            full_ref[begin : begin + rows] = total.astype(jnp.bfloat16)

        for d in range(1, count - 1):
            for h in range(2):
                relay(d, h)
        for copy in spread:
            copy.wait_recv()
        shared = launch(
            remote(
                proj_ref.at[pl.ds(1, near), c],
                proj_ref.at[pl.ds(1, near), c],
                pc_s.at[0],
                pc_r.at[0],
                partner,
            )
        )
        loads[2].wait()
        loads[3].wait()
        relay(count - 1, 0)
        shared.wait_recv()
        finish(0)
        relay(count - 1, 1)
        finish(1)
        enc_ref[...] = full_ref[0:byte_rows]

        for copy in notes:
            copy.wait_recv()
        counted = [infos[m][0:1, 0:1] for m in range(size)]
        offsets = [jnp.zeros((1, 1), jnp.int32)]
        for m in range(size - 1):
            offsets.append(offsets[m] + counted[m])
        my_count = counts_ref[0]
        next_first = jnp.where(
            s + 1 < size, infos[jnp.minimum(s + 1, size - 1)][0:1, 1:2], size * byte_rows
        )
        square = (slots, slots)
        start_row = jnp.broadcast_to(starts_ref[...], square)
        apart = iota(square, 1) - iota(square, 0)
        first_byte = jnp.sum(jnp.where(apart == 0, start_row, 0), axis=1, keepdims=True)
        following = jnp.sum(jnp.where(apart == 1, start_row, 0), axis=1, keepdims=True)
        slot_at = iota((slots, 1), 0)
        in_use = slot_at < my_count
        patch_end = jnp.where(slot_at + 1 < my_count, following, next_first)
        anchor = s * byte_rows
        lower = jnp.where(in_use, first_byte - anchor, 0)
        upper = jnp.where(in_use, patch_end - anchor, 1)

        where_at = iota((slots, total_rows), 1)
        allowed = (where_at >= lower) & (where_at < upper)
        member = jnp.where(allowed & in_use, 1.0, 0.0)
        lengths = jnp.maximum(jnp.sum(member, axis=1, keepdims=True), 1.0)
        bias = jnp.where(allowed, 0.0, -1e30)
        totals = product(member.astype(jnp.bfloat16), full_ref[...])
        pooled_ref[...] = (totals / lengths).astype(jnp.bfloat16)
        loads[4].wait()
        loads[5].wait()

        def across(k, i):
            return remote(
                panels.at[i],
                z_land.at[k - 1, i],
                z_send.at[k - 1, i],
                z_recv.at[k - 1, i],
                tp_peer(tower(k)),
            )

        def heads(i, carry):
            cols = pl.ds(pl.multiple_of(i * group, group), group)
            rows = full_ref[...]
            lifted = product(pooled_ref[...], lift_ref[:, cols])
            keys = product(rows, cross_ref[0, :, cols]).astype(jnp.bfloat16)
            seen_values = product(rows, cross_ref[1, :, cols]).astype(jnp.bfloat16)
            queries = lifted.astype(jnp.bfloat16)
            crossed = []
            for j in range(2):
                lanes = slice(j * HD, (j + 1) * HD)
                scores = across_lanes(queries[:, lanes], keys[:, lanes])
                scores = scores * (1.0 / math.sqrt(HD)) + bias
                raised = jnp.exp(scores - jnp.max(scores, axis=1, keepdims=True))
                crossed.append(
                    product(raised.astype(jnp.bfloat16), seen_values[:, lanes])
                    / jnp.sum(raised, axis=1, keepdims=True)
                )
            patch = lifted + jnp.concatenate(crossed, axis=1)
            panel = jnp.where(in_use, patch, 0.0).astype(jnp.bfloat16)
            patch_ref[:, cols] = panel
            panels[i] = panel
            for k in range(1, count):
                across(k, i).start()
            return carry

        lax.fori_loop(0, panel_count, heads, 0)
        onward = []
        for i in range(panel_count):
            for k in range(count):
                origin = tower(-k)
                if k == 0:
                    here = panels.at[i]
                else:
                    across(k, i).wait_recv()
                    here = z_land.at[k - 1, i]
                away = remote(
                    here, rows_ref.at[p, i], plane_send.at[k, i], plane_recv.at[p, i], plane(origin)
                )
                stay = pltpu.make_async_copy(here, rows_ref.at[p, i], stay_sems.at[i])
                onward.append((origin, away, stay))

                @pl.when(origin != p)
                def _():
                    away.start()

                @pl.when(origin == p)
                def _():
                    stay.start()

        chosen = [
            (
                jnp.where(c == 0, offsets[2 * i], offsets[2 * i + 1]),
                jnp.where(c == 0, counted[2 * i], counted[2 * i + 1]),
                jnp.where(c == 0, offsets[2 * i + 1], offsets[2 * i]),
                jnp.where(c == 0, counted[2 * i + 1], counted[2 * i]),
            )
            for i in range(count)
        ]

        def laid(shape, axis, which):
            at = iota(shape, axis)
            block = at // slots
            result = jnp.broadcast_to(chosen[0][which], shape)
            for i in range(1, count):
                result = jnp.where(block == i, chosen[i][which], result)
            return at - block * slots, result

        row_slot, row_offset = laid((row_total, 1), 0, 0)
        position = row_offset + row_slot
        key_positions = []
        for which in (0, 2):
            key_slot, key_offset = laid((1, row_total), 1, which)
            _, key_count = laid((1, row_total), 1, which + 1)
            key_positions.append(
                jnp.where(key_slot < key_count, key_offset + key_slot, far_position)
            )
        table_rows = table_ref.shape[0]
        picked = jnp.where(iota((row_total, table_rows), 1) == position, 1.0, 0.0)
        turns = lax.dot_general(
            picked,
            table_ref[...],
            (((1,), (0,)), ((), ())),
            precision=lax.Precision.HIGHEST,
            preferred_element_type=jnp.float32,
        )
        swapped = pltpu.roll(turns, HD // 2, 1)
        low_lanes = iota((row_total, HD), 1) < HD // 2
        cosine = jnp.where(low_lanes, turns, swapped)
        sine = jnp.where(low_lanes, -swapped, turns)

        for q in range(count):

            @pl.when(p != q)
            def _():
                for i in range(panel_count):
                    remote(
                        panels.at[i],
                        rows_ref.at[q, i],
                        plane_send.at[q, i],
                        plane_recv.at[q, i],
                        plane(p),
                    ).wait_recv()

        for origin, away, stay in onward:

            @pl.when(origin == p)
            def _():
                stay.wait()

        values = jnp.concatenate(
            [rows_ref[:, i].reshape(row_total, group) for i in range(panel_count)], axis=1
        ).astype(jnp.float32)
        squares = jnp.sum(values * values, axis=1, keepdims=True)
        eye = iota((row_total, row_total), 0) == iota((row_total, row_total), 1)
        flat = jnp.sum(jnp.where(eye, squares, 0.0), axis=0, keepdims=True)
        sq_send[...] = jnp.broadcast_to(flat, sq_send.shape)
        chip_gain = lgain_ref[:, pl.ds(pl.multiple_of(p * columns, columns), columns)]
        geared[...] = (values * chip_gain.astype(jnp.float32)).astype(jnp.bfloat16)
        arriving = []
        for k in range(1, count):
            arriving.append(
                launch(
                    remote(
                        sq_send,
                        sq_land.at[k - 1],
                        sq_s.at[k - 1],
                        sq_r.at[k - 1],
                        plane(lax.rem(p + k, count)),
                    )
                )
            )
        loads[6].wait()
        swaps[0].wait_recv()
        mine = geared[:, pl.ds(pl.multiple_of(c * half, half), half)]
        theirs = geared[:, pl.ds(pl.multiple_of((1 - c) * half, half), half)]
        total = []
        for k in list(range(1, count)) + [0]:
            target = lax.rem(p + k, count)
            lanes = pl.ds(pl.multiple_of(target * HD, HD), HD)
            for i in range(3):
                part = product(mine, w_own[i, :, lanes]) + product(theirs, w_other[i, :, lanes])
                if k:
                    qkv_send[k - 1, i] = part.astype(jnp.bfloat16)
                else:
                    total.append(part)
            if k:
                arriving.append(
                    launch(
                        remote(
                            qkv_send.at[k - 1],
                            qkv_land.at[k - 1],
                            qkv_s.at[k - 1],
                            qkv_r.at[k - 1],
                            plane(target),
                        )
                    )
                )
        for copy in arriving:
            copy.wait_recv()
        flat = flat + jnp.sum(sq_land[:, 0:1, :], axis=0)
        square_sum = jnp.sum(jnp.where(eye, flat, 0.0), axis=1, keepdims=True)
        scale = lax.rsqrt(square_sum / full_width + epsilon)
        for i in range(3):
            for k in range(count - 1):
                total[i] = total[i] + qkv_land[k, i].astype(jnp.float32)
            total[i] = total[i] * scale

        def turned(vectors):
            return (vectors * cosine + pltpu.roll(vectors, HD // 2, 1) * sine).astype(jnp.bfloat16)

        queries = turned(total[0])
        kv_own[0] = turned(total[1])
        kv_own[1] = total[2].astype(jnp.bfloat16)
        swap = launch(remote(kv_own, kv_other, kv_sems.at[0], kv_sems.at[1], partner))

        def scored(keys, key_position):
            scores = across_lanes(queries, keys) * (1.0 / math.sqrt(HD))
            permitted = key_position <= position
            return jnp.where(permitted, scores, -1e30), permitted

        scores_a, permitted_a = scored(kv_own[0], key_positions[0])
        swap.wait_recv()
        scores_b, permitted_b = scored(kv_other[0], key_positions[1])
        largest = jnp.maximum(
            jnp.max(scores_a, axis=1, keepdims=True), jnp.max(scores_b, axis=1, keepdims=True)
        )
        raised_a = jnp.where(permitted_a, jnp.exp(scores_a - largest), 0.0)
        raised_b = jnp.where(permitted_b, jnp.exp(scores_b - largest), 0.0)
        weight_sum = jnp.sum(raised_a, axis=1, keepdims=True) + jnp.sum(
            raised_b, axis=1, keepdims=True
        )
        weighted = product(raised_a.astype(jnp.bfloat16), kv_own[1]) + product(
            raised_b.astype(jnp.bfloat16), kv_other[1]
        )
        att_all[p] = (weighted / weight_sum).astype(jnp.bfloat16)
        for k in range(1, count):
            launch(
                remote(
                    att_all.at[p],
                    att_all.at[p],
                    att_s.at[k - 1],
                    att_r.at[p],
                    plane(lax.rem(p + k, count)),
                )
            )
        for k in range(1, count):
            source = lax.rem(p + k, count)
            remote(
                att_all.at[source], att_all.at[source], att_s.at[k - 1], att_r.at[source], plane(source)
            ).wait_recv()
        loads[7].wait()
        swaps[1].wait_recv()
        hops = []
        for k in list(range(1, count)) + [0]:
            target = lax.rem(p + k, count)
            take = pl.ds(pl.multiple_of(target * slots, slots), slots)
            attended = jnp.concatenate([att_all[j, take, :] for j in range(count)], axis=1)
            for output, core in ((o_own, c), (o_other, 1 - c)):
                parts[target, :, pl.ds(pl.multiple_of(core * half, half), half)] = product(
                    attended, output[...]
                ).astype(jnp.bfloat16)
            if k:
                hops.append(
                    launch(
                        remote(
                            parts.at[target],
                            land.at[k - 1],
                            a_s.at[k - 1],
                            a_r.at[k - 1],
                            plane(target),
                        )
                    )
                )
        last = []
        for k in range(count):
            origin = lax.rem(p + count - k, count)
            if k == 0:
                here = parts.at[p]
            else:
                hops[k - 1].wait_recv()
                here = land.at[k - 1]
            away = remote(here, final.at[t], b_s.at[k], b_r.at[t], tp_peer(origin))
            last.append((origin, away))

            @pl.when(origin != t)
            def _():
                away.start()

            @pl.when(origin == t)
            def _():
                final[t] = here[...]

        summed = patch_ref[...].astype(jnp.float32)
        for q in range(count):

            @pl.when(t != q)
            def _():
                remote(land.at[0], final.at[q], b_s.at[q], b_r.at[q], tp_peer(t)).wait_recv()

            summed = summed + final[q].astype(jnp.float32)
        out_ref[...] = jnp.where(in_use, summed, 0.0).astype(jnp.bfloat16)

        for copy in sent:
            copy.wait_send()
        for h in range(2):
            for q in range(count):

                @pl.when((q <= t) & (t < count - 1))
                def _():
                    pass_on(q, h, True).wait_send()

                @pl.when((q >= t) & (t > 0))
                def _():
                    pass_on(q, h, False).wait_send()

        for i in range(panel_count):
            for k in range(1, count):
                across(k, i).wait_send()
        for origin, away, stay in onward:

            @pl.when(origin != p)
            def _():
                away.wait_send()

        for origin, away in last:

            @pl.when(origin != t)
            def _():
                away.wait_send()

    vmem = pl.BlockSpec(memory_space=pltpu.VMEM)
    hbm = pl.BlockSpec(memory_space=pl.ANY)
    smem = pl.BlockSpec(memory_space=pltpu.SMEM)
    dma = pltpu.SemaphoreType.DMA

    def buffer(*shape, dtype=jnp.bfloat16):
        return pltpu.VMEM(shape, dtype)

    return pl.pallas_call(
        kernel,
        out_shape=[like((byte_rows, width)), like((slots, columns))],
        in_specs=[hbm, vmem, hbm, hbm, vmem, smem, hbm, hbm, vmem, hbm, hbm, vmem],
        out_specs=[vmem, vmem],
        scratch_shapes=[
            buffer(total_rows, width),
            buffer(*enc_qkv.shape),
            buffer(total_rows, enc_cols),
            buffer(2, WIN + total_rows, enc_cols),
            buffer(size, 8, 128, dtype=jnp.int32),
            buffer(count, 2, share, width),
            buffer(count, total_rows, enc_cols),
            buffer(*lift.shape),
            buffer(*cross_kv.shape),
            buffer(slots, width),
            buffer(total_rows, width),
            buffer(panel_count, slots, group),
            buffer(near, panel_count, slots, group),
            buffer(count, panel_count, slots, group),
            buffer(slots, columns),
            buffer(*lat_qkv.shape),
            buffer(*lat_qkv.shape),
            buffer(*lat_proj.shape),
            buffer(*lat_proj.shape),
            buffer(row_total, columns),
            buffer(near, 3, row_total, HD),
            buffer(near, 3, row_total, HD),
            buffer(8, row_total, dtype=jnp.float32),
            buffer(near, 8, row_total, dtype=jnp.float32),
            buffer(2, row_total, HD),
            buffer(2, row_total, HD),
            buffer(count, row_total, HD),
            buffer(count, slots, columns),
            buffer(near, slots, columns),
            buffer(count, slots, columns),
            dma((8,)),
            dma((size - 1,)),
            dma((size - 1,)),
            dma((2,)),
            dma((2,)),
            dma((3,)),
            dma((3,)),
            dma((near,)),
            dma((near,)),
            dma((near,)),
            dma((near,)),
            dma((1,)),
            dma((1,)),
            dma((4,)),
            dma((count, 2)),
            dma((count, 2)),
            dma((count, 2)),
            dma((near, panel_count)),
            dma((near, panel_count)),
            dma((count, panel_count)),
            dma((count, panel_count)),
            dma((panel_count,)),
            dma((near,)),
            dma((near,)),
            dma((near,)),
            dma((near,)),
            dma((2,)),
            dma((near,)),
            dma((count,)),
            dma((near,)),
            dma((near,)),
            dma((count,)),
            dma((count,)),
        ],
        compiler_params=pltpu.CompilerParams(collective_id=call_id, has_side_effects=True),
    )(
        states, gain, enc_qkv, proj, starts, counts, lift, cross_kv, latent_gain, lat_qkv, lat_proj,
        table,
    )


def fused_shards(
    byte_states,
    enc_gain,
    enc_qkv,
    enc_proj_out,
    starts,
    counts,
    lift,
    cross_kv,
    latent_gain,
    lat_qkv,
    lat_proj_out,
):
    table = jnp.asarray(turn_table(lax.axis_size("seq") * starts.shape[1]))
    encoded, latent = whole_layer(
        byte_states,
        enc_gain[None],
        enc_qkv,
        enc_proj_out,
        starts,
        counts,
        lift,
        cross_kv,
        latent_gain[None],
        lat_qkv,
        lat_proj_out,
        table,
        1,
    )
    return (encoded, latent)


def fits_pairs(mesh, byte_states, enc_qkv, starts, lat_qkv):
    size, tp_size = mesh.shape["seq"], mesh.shape["tp"]
    byte_rows = byte_states.shape[0] // size
    return (
        size == 2 * tp_size
        and WIN % byte_rows == 0
        and WIN // byte_rows < size
        and byte_rows % (32 * tp_size) == 0
        and lat_qkv.shape[2] // tp_size == HD * tp_size
        and lat_qkv.shape[1] % (128 * size) == 0
        and starts.shape[1] * tp_size % 128 == 0
        and starts.shape[1] * tp_size <= 1024
        and starts.shape[1] % 16 == 0
        and enc_qkv.shape[2] % (128 * tp_size) == 0
    )


def solution(mesh):
    specs = dict(
        mesh=mesh,
        in_specs=(
            P("seq", None),
            P(),
            P(None, None, "tp"),
            P("tp", None),
            P("seq", None),
            P("seq"),
            P(None, "tp"),
            P(None, None, "tp"),
            P(),
            P(None, "seq", "tp"),
            P("tp", "seq"),
        ),
        out_specs=(P("seq", None), P("seq", "tp")),
        check_vma=False,
    )

    def run(*arrays):
        paired = fits_pairs(mesh, arrays[0], arrays[2], arrays[4], arrays[9])
        return jax.shard_map(fused_shards if paired else gathered_shards, **specs)(*arrays)

    return run
```

time: 127 us -> 91.6 us (0.72)
  the two profiles are of different devices: /device:TPU:6 before, /device:TPU:17 now
where the time goes in v1:
time: 91.6 us; the launch traced here: 91.3 us
  Pallas kernels  84 us (92%)
  local copies, waits for them, and re-layouts  6.03 us (7%)
  between operations  1.29 us (1%)
    pallas_call x1, Pallas kernels, whole_layer(): pl.pallas_call(kernel, out_shape=[like((byte_rows, width)), like((slots,...  84 us
    unnamed x2, local copies, waits for them, and re-layouts  3.44 us

profile of v1, /device:TPU:17, one launch (start us, length us, event | category | flops | bytes accessed | tf_op | source)
XLA Modules:
  0.0 91.3 jit_solution(5412676522096487940)
XLA Ops:
  1.3 1.3 %broadcast_in_dim.6.gain_ref = bf16[1,1024]{1,0:T(2,128)(2,1)} reshape(bf16[1024]{0:T(1024)(128)(2,1)} %param.13) | data formatting | bytes 4096 | tf_op jit(solution)/shard_map/broadcast_in_dim | solution.py:1001
  2.6 1.3 %broadcast_in_dim.7.lgain_ref = bf16[1,4096]{1,0:T(2,128)(2,1)} reshape(bf16[4096]{0:T(1024)(128)(2,1)} %param.20) | data formatting | bytes 16384 | tf_op jit(solution)/shard_map/broadcast_in_dim | solution.py:1008
  3.9 84.0 %shard_map.131 = (bf16[256,1024]{1,0:T(8,128)(2,1)}, bf16[64,1024]{1,0:T(8,128)(2,1)}) custom-call(bf16[256,1024]{1,0:T(8,128)(2,1)} %states_hbm.1, bf16[1,1024]{1,0:T(2,128)(2,1)} %broadcast_in_dim.6.gain_ref, bf16[3,1024,256]{2,1,0:T(8,128)(2,1)} %qkv_hbm.1, bf16[256,1024]{1,0:T(8,128)(2,1)} %proj_hbm.1, s32[1,64]{1,0:T(1,128)} %starts_ref.1, ...), custom_call_target="tpu_custom_call" | custom-call | tf_op jit(solution)/shard_map/pallas_call | solution.py:908
  87.8 1.9 %copy.17 = bf16[256,1024]{1,0:T(8,128)(2,1)} copy(bf16[256,1024]{1,0:T(8,128)(2,1)} %get-tuple-element.4) | data formatting | bytes 1048576
  89.7 1.6 %copy.18 = bf16[64,1024]{1,0:T(8,128)(2,1)} copy(bf16[64,1024]{1,0:T(8,128)(2,1)} %get-tuple-element.5) | data formatting | bytes 262144

commit v2 on v1

--- a/solution.py
+++ b/solution.py
@@ -327,16 +327,17 @@
 
     def kernel(
         states_hbm, gain_ref, qkv_hbm, proj_hbm, starts_ref, counts_ref, lift_hbm, cross_hbm,
-        lgain_ref, w_own_hbm, o_own_hbm, table_ref,
-        enc_ref, out_ref,
-        states_ref, qkv_ref, query_ref, kv_ref, infos, proj_ref, att_ref,
-        lift_ref, cross_ref, pooled_ref, full_ref, panels, z_land, rows_ref, patch_ref,
-        w_own, w_other, o_own, o_other, geared, qkv_send, qkv_land, sq_send, sq_land,
-        kv_own, kv_other, att_all, parts, land, final,
+        lgain_ref, w_own_hbm, o_hbm, table_hbm,
+        enc_hbm, out_ref,
+        states_ref, qkv_ref, query_ref, kv_ref, infos, proj_ref, att_ref, table_ref, cos_ref, sin_ref,
+        lift_ref, cross_ref, pooled_ref, full_ref, panels, rows_ref, patch_ref,
+        w_own, w_other, geared, qkv_send, qkv_land, sq_send, sq_land,
+        kv_own, kv_other, out_quarter, out_rows, tall, parts, land,
         load_sems, info_s, info_r, halo_s, halo_r, edge_s, edge_r, pz_s, pz_r, pp_s, pp_r, pc_s, pc_r,
         w_sems, up_send, down_send, ag_recv,
-        z_send, z_recv, plane_send, plane_recv, stay_sems,
-        qkv_s, qkv_r, sq_s, sq_r, kv_sems, att_s, att_r, a_s, a_r, b_s, b_r,
+        zup_send, zdown_send, z_recv, plane_send, plane_recv, stay_sems,
+        qkv_s, qkv_r, sq_s, sq_r, kv_sems,
+        oq_s, oq_r, oz_s, oz_r, oc_sems, own_sems, tz_s, tz_r, a_s, a_r, enc_sem,
     ):
         s, t = lax.axis_index("seq"), lax.axis_index("tp")
         p, c = s // 2, lax.rem(s, 2)
@@ -350,21 +351,34 @@
 
         def tower(k):
             return lax.rem(t + k + count, count)
+
+        def flip(k):
+            if k == 0:
+                return p
+            if k == 1:
+                return p + 1 - 2 * lax.rem(p, 2)
+            if k == 2:
+                return lax.rem(p + 2, 4)
+            return 3 - p
+
+        far_first = (3, 2, 1)
 
         barrier = pltpu.get_barrier_semaphore()
         for k in range(1, size):
             pl.semaphore_signal(barrier, inc=1, device_id=seq_peer(ring(k)), device_id_type=MESH)
         for k in range(1, count):
             pl.semaphore_signal(barrier, inc=1, device_id=tp_peer(tower(k)), device_id_type=MESH)
+        own_rows = pl.ds(pl.multiple_of(p * HD, HD), HD)
         load_plan = (
             (states_hbm, states_ref.at[pl.ds(0, byte_rows)]),
             (qkv_hbm, qkv_ref),
+            (table_hbm, table_ref),
             (proj_hbm.at[pl.ds(0, share)], proj_ref.at[0, 0]),
             (proj_hbm.at[pl.ds(share, share)], proj_ref.at[0, 1]),
             (lift_hbm, lift_ref),
             (cross_hbm, cross_ref),
             (w_own_hbm, w_own),
-            (o_own_hbm, o_own),
+            (o_hbm.at[own_rows], out_quarter.at[p]),
         )
         loads = [
             pltpu.make_async_copy(source, target, load_sems.at[i])
@@ -378,54 +392,11 @@
             copy.start()
             sent.append(copy)
             return copy
-
         info_lane = iota((8, 128), 1)
         infos[s] = jnp.where(
             info_lane == 0, counts_ref[0], jnp.where(info_lane == 1, starts_ref[0:1, 0:1], 0)
         )
-        loads[0].wait()
-        values = states_ref[0:byte_rows].astype(jnp.float32)
-        normed = rms_scale(values, gain_ref[...].astype(jnp.float32)).astype(jnp.bfloat16)
-        own = pl.ds(WIN, byte_rows)
-        loads[1].wait()
-        for i in range(2):
-            kv_ref[i, own] = product(normed, qkv_ref[i + 1]).astype(jnp.bfloat16)
-        query_ref[0:byte_rows] = (
-            product(normed, qkv_ref[0]) * (1.0 / math.sqrt(EH))
-        ).astype(jnp.bfloat16)
         pl.semaphore_wait(barrier, size - 1 + count - 1)
-
-        reach = WIN // byte_rows
-        halos = []
-        for k in range(1, reach + 1):
-            halos.append(
-                launch(
-                    remote(
-                        kv_ref.at[:, own],
-                        kv_ref.at[:, pl.ds(WIN - k * byte_rows, byte_rows)],
-                        halo_s.at[k - 1],
-                        halo_r.at[k - 1],
-                        seq_peer(ring(k)),
-                    )
-                )
-            )
-        behind = seq_peer(ring(-1))
-        edges = [
-            launch(remote(source, target, edge_s.at[i], edge_r.at[i], behind))
-            for i, (source, target) in enumerate(
-                (
-                    (kv_ref.at[:, pl.ds(WIN, EDGE)], kv_ref.at[:, pl.ds(WIN + byte_rows, EDGE)]),
-                    (query_ref.at[pl.ds(0, EDGE)], query_ref.at[pl.ds(byte_rows, EDGE)]),
-                    (states_ref.at[pl.ds(0, EDGE)], states_ref.at[pl.ds(byte_rows, EDGE)]),
-                )
-            )
-        ]
-        notes = [
-            launch(
-                remote(infos.at[s], infos.at[s], info_s.at[k - 1], info_r.at[k - 1], seq_peer(ring(k)))
-            )
-            for k in range(1, size)
-        ]
         mine_at = pl.multiple_of(p * piece, piece)
         lifts = [
             launch(
@@ -439,133 +410,61 @@
             )
             for k in range(1, count)
         ]
-        swaps = [
-            launch(remote(w_own_hbm, w_other, w_sems.at[0], w_sems.at[1], partner)),
-            launch(remote(o_own_hbm, o_other, w_sems.at[2], w_sems.at[3], partner)),
+        notes = [
+            launch(
+                remote(infos.at[s], infos.at[s], info_s.at[k - 1], info_r.at[k - 1], seq_peer(ring(k)))
+            )
+            for k in range(1, size)
         ]
-        for copy in lifts:
-            copy.wait_recv()
-        spread = [
-            launch(
-                remote(
-                    proj_ref.at[pl.ds(1, near), c, pl.ds(mine_at, piece)],
-                    proj_ref.at[pl.ds(1, near), c, pl.ds(mine_at, piece)],
-                    pp_s.at[k - 1],
-                    pp_r.at[k - 1],
-                    plane(lax.rem(p + k, count)),
-                )
-            )
-            for k in range(1, count)
+        loads[0].wait()
+        values = states_ref[0:byte_rows].astype(jnp.float32)
+        chip_row = gain_ref[...].astype(jnp.float32).reshape(1, width)
+        normed = rms_scale(values, chip_row).astype(jnp.bfloat16)
+        own = pl.ds(WIN, byte_rows)
+        loads[1].wait()
+        halos = []
+        for i in range(2):
+            kv_ref[i, own] = product(normed, qkv_ref[i + 1]).astype(jnp.bfloat16)
+            halos.append(
+                launch(
+                    remote(
+                        kv_ref.at[i, own],
+                        kv_ref.at[i, pl.ds(0, byte_rows)],
+                        halo_s.at[0, i],
+                        halo_r.at[0, i],
+                        seq_peer(ring(2)),
+                    )
+                )
+            )
+        behind = seq_peer(ring(-1))
+        query_ref[0:byte_rows] = (
+            product(normed, qkv_ref[0]) * (1.0 / math.sqrt(EH))
+        ).astype(jnp.bfloat16)
+        edges = [
+            launch(remote(source, target, edge_s.at[i], edge_r.at[i], behind))
+            for i, (source, target) in enumerate(
+                (
+                    (kv_ref.at[:, pl.ds(WIN, EDGE)], kv_ref.at[:, pl.ds(WIN + byte_rows, EDGE)]),
+                    (query_ref.at[pl.ds(0, EDGE)], query_ref.at[pl.ds(byte_rows, EDGE)]),
+                    (states_ref.at[pl.ds(0, EDGE)], states_ref.at[pl.ds(byte_rows, EDGE)]),
+                )
+            )
         ]
-        for copy in halos + edges:
-            copy.wait_recv()
-
-        def pass_on(origin, h, up):
-            begin, rows = spans[h]
-            step = 1 if up else -1
+
+        def beside(i):
+            first = pl.multiple_of(jnp.where(c == 0, WIN, 0), byte_rows)
             return remote(
-                att_ref.at[origin, pl.ds(begin, rows)],
-                att_ref.at[origin, pl.ds(begin, rows)],
-                (up_send if up else down_send).at[origin, h],
-                ag_recv.at[origin, h],
-                tp_peer(tower(step)),
-            )
-
-        def attend(begin, rows):
-            reach_rows = rows + WIN
-            keys = kv_ref[0, begin : begin + reach_rows]
-            seen_values = kv_ref[1, begin : begin + reach_rows]
-            queries = query_ref[begin : begin + rows]
-            head_of = iota((rows, enc_cols), 1) // EH
-            stacked = jnp.concatenate(
-                [jnp.where(head_of == h, queries, jnp.zeros_like(queries)) for h in range(enc_heads)],
-                axis=0,
-            )
-            query_at = iota((rows, reach_rows), 0) + begin
-            key_at = iota((rows, reach_rows), 1) + (begin - WIN)
-            near_by = (
-                (key_at <= query_at) & (key_at > query_at - WIN) & (key_at >= -s * byte_rows)
-            )
-            bias = jnp.where(near_by, 0.0, -1e30)
-            scores = across_lanes(stacked, keys)
-            raised, sums = [], []
-            for h in range(enc_heads):
-                here = scores[h * rows : (h + 1) * rows] + bias
-                here = jnp.exp(here - jnp.max(here, axis=1, keepdims=True))
-                sums.append(jnp.sum(here, axis=1, keepdims=True))
-                raised.append(here.astype(jnp.bfloat16))
-            seen = product(jnp.concatenate(raised, axis=0), seen_values)
-            attended = jnp.zeros((rows, enc_cols), jnp.float32)
-            for h in range(enc_heads):
-                attended = jnp.where(
-                    head_of == h, seen[h * rows : (h + 1) * rows] / sums[h], attended
-                )
-            att_ref[t, begin : begin + rows] = attended.astype(jnp.bfloat16)
-
-        for h in range(2):
-            begin, rows = spans[h]
-            attend(begin, rows_half)
-            if rows > rows_half:
-                attend(begin + rows_half, rows - rows_half)
-
-            @pl.when(t < count - 1)
-            def _():
-                pass_on(t, h, True).start()
-
-            @pl.when(t > 0)
-            def _():
-                pass_on(t, h, False).start()
-
-        def relay(d, h):
-            @pl.when(t - d >= 0)
-            def _():
-                pass_on(t - d, h, True).wait_recv()
-
-                @pl.when(t < count - 1)
-                def _():
-                    pass_on(t - d, h, True).start()
-
-            @pl.when(t + d < count)
-            def _():
-                pass_on(t + d, h, False).wait_recv()
-
-                @pl.when(t > 0)
-                def _():
-                    pass_on(t + d, h, False).start()
-
-        def finish(h):
-            begin, rows = spans[h]
-            total = states_ref[begin : begin + rows].astype(jnp.float32)
-            for k in range(count):
-                total = total + product(
-                    att_ref[tower(-k), begin : begin + rows],
-                    proj_ref[k].reshape(enc_cols, width),
-                )
-            full_ref[begin : begin + rows] = total.astype(jnp.bfloat16)
-
-        for d in range(1, count - 1):
-            for h in range(2):
-                relay(d, h)
-        for copy in spread:
-            copy.wait_recv()
-        shared = launch(
-            remote(
-                proj_ref.at[pl.ds(1, near), c],
-                proj_ref.at[pl.ds(1, near), c],
-                pc_s.at[0],
-                pc_r.at[0],
+                kv_ref.at[i, pl.ds(first, byte_rows)],
+                kv_ref.at[i, pl.ds(byte_rows, byte_rows)],
+                halo_s.at[1, i],
+                halo_r.at[1, i],
                 partner,
             )
-        )
-        loads[2].wait()
-        loads[3].wait()
-        relay(count - 1, 0)
-        shared.wait_recv()
-        finish(0)
-        relay(count - 1, 1)
-        finish(1)
-        enc_ref[...] = full_ref[0:byte_rows]
-
+
+        @pl.when(c == 0)
+        def _():
+            for i in range(2):
+                beside(i).start()
         for copy in notes:
             copy.wait_recv()
         counted = [infos[m][0:1, 0:1] for m in range(size)]
@@ -587,25 +486,232 @@
         anchor = s * byte_rows
         lower = jnp.where(in_use, first_byte - anchor, 0)
         upper = jnp.where(in_use, patch_end - anchor, 1)
-
         where_at = iota((slots, total_rows), 1)
         allowed = (where_at >= lower) & (where_at < upper)
         member = jnp.where(allowed & in_use, 1.0, 0.0)
         lengths = jnp.maximum(jnp.sum(member, axis=1, keepdims=True), 1.0)
+        member = member.astype(jnp.bfloat16)
         bias = jnp.where(allowed, 0.0, -1e30)
-        totals = product(member.astype(jnp.bfloat16), full_ref[...])
+        chosen = [
+            (
+                jnp.where(c == 0, offsets[2 * i], offsets[2 * i + 1]),
+                jnp.where(c == 0, counted[2 * i], counted[2 * i + 1]),
+                jnp.where(c == 0, offsets[2 * i + 1], offsets[2 * i]),
+                jnp.where(c == 0, counted[2 * i + 1], counted[2 * i]),
+            )
+            for i in range(count)
+        ]
+
+        def laid(shape, axis, which):
+            at = iota(shape, axis)
+            block = at // slots
+            result = jnp.broadcast_to(chosen[0][which], shape)
+            for i in range(1, count):
+                result = jnp.where(block == i, chosen[i][which], result)
+            return at - block * slots, result
+
+        row_slot, row_offset = laid((row_total, 1), 0, 0)
+        position = row_offset + row_slot
+        key_positions = []
+        for which in (0, 2):
+            key_slot, key_offset = laid((1, row_total), 1, which)
+            _, key_count = laid((1, row_total), 1, which + 1)
+            key_positions.append(
+                jnp.where(key_slot < key_count, key_offset + key_slot, far_position)
+            )
+        loads[2].wait()
+        table_rows = table_ref.shape[0]
+        picked = jnp.where(iota((row_total, table_rows), 1) == position, 1.0, 0.0)
+        turns = lax.dot_general(
+            picked,
+            table_ref[...],
+            (((1,), (0,)), ((), ())),
+            precision=lax.Precision.HIGHEST,
+            preferred_element_type=jnp.float32,
+        )
+        swapped = pltpu.roll(turns, HD // 2, 1)
+        low_lanes = iota((row_total, HD), 1) < HD // 2
+        cos_ref[...] = jnp.where(low_lanes, turns, swapped)
+        sin_ref[...] = jnp.where(low_lanes, -swapped, turns)
+        for copy in lifts:
+            copy.wait_recv()
+        spread = [
+            launch(
+                remote(
+                    proj_ref.at[pl.ds(1, near), c, pl.ds(mine_at, piece)],
+                    proj_ref.at[pl.ds(1, near), c, pl.ds(mine_at, piece)],
+                    pp_s.at[k - 1],
+                    pp_r.at[k - 1],
+                    plane(flip(k)),
+                )
+            )
+            for k in far_first
+        ]
+        quarters = [
+            launch(
+                remote(
+                    o_hbm.at[pl.ds(pl.multiple_of(flip(k) * HD, HD), HD)],
+                    out_quarter.at[p],
+                    oq_s.at[k - 1],
+                    oq_r.at[k - 1],
+                    plane(flip(k)),
+                )
+            )
+            for k in far_first
+        ]
+        for i in range(2):
+            halos[i].wait_recv()
+
+            @pl.when(c == 1)
+            def _():
+                beside(i).start()
+
+        for copy in edges:
+            copy.wait_recv()
+        for i in range(2):
+            beside(i).wait_recv()
+        swaps = [launch(remote(w_own_hbm, w_other, w_sems.at[0], w_sems.at[1], partner))]
+
+        def pass_on(origin, h, up):
+            begin, rows = spans[h]
+            step = 1 if up else -1
+            return remote(
+                att_ref.at[origin, pl.ds(begin, rows)],
+                att_ref.at[origin, pl.ds(begin, rows)],
+                (up_send if up else down_send).at[origin, h],
+                ag_recv.at[origin, h],
+                tp_peer(tower(step)),
+            )
+
+        def attend(begin, rows):
+            reach_rows = rows + WIN
+            keys = kv_ref[0, begin : begin + reach_rows]
+            seen_values = kv_ref[1, begin : begin + reach_rows]
+            queries = query_ref[begin : begin + rows]
+            head_of = iota((rows, enc_cols), 1) // EH
+            stacked = jnp.concatenate(
+                [jnp.where(head_of == h, queries, jnp.zeros_like(queries)) for h in range(enc_heads)],
+                axis=0,
+            )
+            query_at = iota((rows, reach_rows), 0) + begin
+            key_at = iota((rows, reach_rows), 1) + (begin - WIN)
+            near_by = (
+                (key_at <= query_at) & (key_at > query_at - WIN) & (key_at >= -s * byte_rows)
+            )
+            near_bias = jnp.where(near_by, 0.0, -1e30)
+            scores = across_lanes(stacked, keys)
+            raised, sums = [], []
+            for h in range(enc_heads):
+                here = scores[h * rows : (h + 1) * rows] + near_bias
+                here = jnp.exp(here - jnp.max(here, axis=1, keepdims=True))
+                sums.append(jnp.sum(here, axis=1, keepdims=True))
+                raised.append(here.astype(jnp.bfloat16))
+            seen = product(jnp.concatenate(raised, axis=0), seen_values)
+            attended = jnp.zeros((rows, enc_cols), jnp.float32)
+            for h in range(enc_heads):
+                attended = jnp.where(
+                    head_of == h, seen[h * rows : (h + 1) * rows] / sums[h], attended
+                )
+            att_ref[t, begin : begin + rows] = attended.astype(jnp.bfloat16)
+        for h in range(2):
+            begin, rows = spans[h]
+            attend(begin, rows_half)
+            if rows > rows_half:
+                attend(begin + rows_half, rows - rows_half)
+
+            @pl.when(t < count - 1)
+            def _():
+                pass_on(t, h, True).start()
+
+            @pl.when(t > 0)
+            def _():
+                pass_on(t, h, False).start()
+
+        def relay(d, h):
+            @pl.when(t - d >= 0)
+            def _():
+                pass_on(t - d, h, True).wait_recv()
+
+                @pl.when(t < count - 1)
+                def _():
+                    pass_on(t - d, h, True).start()
+
+            @pl.when(t + d < count)
+            def _():
+                pass_on(t + d, h, False).wait_recv()
+
+                @pl.when(t > 0)
+                def _():
+                    pass_on(t + d, h, False).start()
+
+        def finish(h):
+            begin, rows = spans[h]
+            total = states_ref[begin : begin + rows].astype(jnp.float32)
+            for k in range(count):
+                total = total + product(
+                    att_ref[tower(-k), begin : begin + rows],
+                    proj_ref[k].reshape(enc_cols, width),
+                )
+            full_ref[begin : begin + rows] = total.astype(jnp.bfloat16)
+        for copy in spread:
+            copy.wait_recv()
+        shared = launch(
+            remote(
+                proj_ref.at[pl.ds(1, near), c],
+                proj_ref.at[pl.ds(1, near), c],
+                pc_s.at[0],
+                pc_r.at[0],
+                partner,
+            )
+        )
+        for d in range(1, count - 1):
+            for h in range(2):
+                relay(d, h)
+        loads[3].wait()
+        loads[4].wait()
+        relay(count - 1, 0)
+        shared.wait_recv()
+        finish(0)
+        relay(count - 1, 1)
+        finish(1)
+        enc_out = pltpu.make_async_copy(full_ref.at[pl.ds(0, byte_rows)], enc_hbm, enc_sem.at[0])
+        enc_out.start()
+
+        totals = product(member, full_ref[...])
         pooled_ref[...] = (totals / lengths).astype(jnp.bfloat16)
-        loads[4].wait()
         loads[5].wait()
-
-        def across(k, i):
+        loads[6].wait()
+
+        def climb(origin, i, up):
+            step = 1 if up else -1
             return remote(
-                panels.at[i],
-                z_land.at[k - 1, i],
-                z_send.at[k - 1, i],
-                z_recv.at[k - 1, i],
-                tp_peer(tower(k)),
-            )
+                panels.at[origin, i],
+                panels.at[origin, i],
+                (zup_send if up else zdown_send).at[origin, i],
+                z_recv.at[origin, i],
+                tp_peer(tower(step)),
+            )
+
+        def away(origin, i):
+            return remote(
+                panels.at[origin, i],
+                rows_ref.at[p, i],
+                plane_send.at[origin, i],
+                plane_recv.at[p, i],
+                plane(origin),
+            )
+
+        def stay(i):
+            return pltpu.make_async_copy(panels.at[p, i], rows_ref.at[p, i], stay_sems.at[i])
+
+        def spill(origin, i):
+            @pl.when(origin != p)
+            def _():
+                away(origin, i).start()
+
+            @pl.when(origin == p)
+            def _():
+                stay(i).start()
 
         def heads(i, carry):
             cols = pl.ds(pl.multiple_of(i * group, group), group)
@@ -627,95 +733,73 @@
             patch = lifted + jnp.concatenate(crossed, axis=1)
             panel = jnp.where(in_use, patch, 0.0).astype(jnp.bfloat16)
             patch_ref[:, cols] = panel
-            panels[i] = panel
-            for k in range(1, count):
-                across(k, i).start()
+            panels[t, i] = panel
+
+            @pl.when(t < count - 1)
+            def _():
+                climb(t, i, True).start()
+
+            @pl.when(t > 0)
+            def _():
+                climb(t, i, False).start()
+
+            spill(t, i)
             return carry
-
         lax.fori_loop(0, panel_count, heads, 0)
-        onward = []
-        for i in range(panel_count):
-            for k in range(count):
-                origin = tower(-k)
-                if k == 0:
-                    here = panels.at[i]
-                else:
-                    across(k, i).wait_recv()
-                    here = z_land.at[k - 1, i]
-                away = remote(
-                    here, rows_ref.at[p, i], plane_send.at[k, i], plane_recv.at[p, i], plane(origin)
-                )
-                stay = pltpu.make_async_copy(here, rows_ref.at[p, i], stay_sems.at[i])
-                onward.append((origin, away, stay))
-
-                @pl.when(origin != p)
+        for d in range(1, count):
+            for i in range(panel_count):
+
+                @pl.when(t - d >= 0)
                 def _():
-                    away.start()
-
-                @pl.when(origin == p)
+                    climb(t - d, i, True).wait_recv()
+
+                    @pl.when(t < count - 1)
+                    def _():
+                        climb(t - d, i, True).start()
+
+                    spill(t - d, i)
+
+                @pl.when(t + d < count)
                 def _():
-                    stay.start()
-
-        chosen = [
-            (
-                jnp.where(c == 0, offsets[2 * i], offsets[2 * i + 1]),
-                jnp.where(c == 0, counted[2 * i], counted[2 * i + 1]),
-                jnp.where(c == 0, offsets[2 * i + 1], offsets[2 * i]),
-                jnp.where(c == 0, counted[2 * i + 1], counted[2 * i]),
-            )
-            for i in range(count)
+                    climb(t + d, i, False).wait_recv()
+
+                    @pl.when(t > 0)
+                    def _():
+                        climb(t + d, i, False).start()
+
+                    spill(t + d, i)
+        for copy in quarters:
+            copy.wait_recv()
+        loads[8].wait()
+        mine_out = pltpu.make_async_copy(out_quarter.at[t], out_rows.at[c, t], own_sems.at[0])
+        mine_out.start()
+        ups = [
+            launch(
+                remote(
+                    out_quarter.at[tower(k)],
+                    out_rows.at[c, t],
+                    oz_s.at[k - 1],
+                    oz_r.at[k - 1],
+                    tp_peer(tower(k)),
+                )
+            )
+            for k in range(1, count)
         ]
-
-        def laid(shape, axis, which):
-            at = iota(shape, axis)
-            block = at // slots
-            result = jnp.broadcast_to(chosen[0][which], shape)
-            for i in range(1, count):
-                result = jnp.where(block == i, chosen[i][which], result)
-            return at - block * slots, result
-
-        row_slot, row_offset = laid((row_total, 1), 0, 0)
-        position = row_offset + row_slot
-        key_positions = []
-        for which in (0, 2):
-            key_slot, key_offset = laid((1, row_total), 1, which)
-            _, key_count = laid((1, row_total), 1, which + 1)
-            key_positions.append(
-                jnp.where(key_slot < key_count, key_offset + key_slot, far_position)
-            )
-        table_rows = table_ref.shape[0]
-        picked = jnp.where(iota((row_total, table_rows), 1) == position, 1.0, 0.0)
-        turns = lax.dot_general(
-            picked,
-            table_ref[...],
-            (((1,), (0,)), ((), ())),
-            precision=lax.Precision.HIGHEST,
-            preferred_element_type=jnp.float32,
-        )
-        swapped = pltpu.roll(turns, HD // 2, 1)
-        low_lanes = iota((row_total, HD), 1) < HD // 2
-        cosine = jnp.where(low_lanes, turns, swapped)
-        sine = jnp.where(low_lanes, -swapped, turns)
-
         for q in range(count):
 
             @pl.when(p != q)
             def _():
                 for i in range(panel_count):
                     remote(
-                        panels.at[i],
+                        panels.at[0, i],
                         rows_ref.at[q, i],
                         plane_send.at[q, i],
                         plane_recv.at[q, i],
                         plane(p),
                     ).wait_recv()
 
-        for origin, away, stay in onward:
-
-            @pl.when(origin == p)
-            def _():
-                stay.wait()
-
+        for i in range(panel_count):
+            stay(i).wait()
         values = jnp.concatenate(
             [rows_ref[:, i].reshape(row_total, group) for i in range(panel_count)], axis=1
         ).astype(jnp.float32)
@@ -723,10 +807,11 @@
         eye = iota((row_total, row_total), 0) == iota((row_total, row_total), 1)
         flat = jnp.sum(jnp.where(eye, squares, 0.0), axis=0, keepdims=True)
         sq_send[...] = jnp.broadcast_to(flat, sq_send.shape)
-        chip_gain = lgain_ref[:, pl.ds(pl.multiple_of(p * columns, columns), columns)]
-        geared[...] = (values * chip_gain.astype(jnp.float32)).astype(jnp.bfloat16)
+        chip_gain = lgain_ref[pl.ds(pl.multiple_of(p * columns, columns), columns)]
+        chip_gain = chip_gain.astype(jnp.float32).reshape(1, columns)
+        geared[...] = (values * chip_gain).astype(jnp.bfloat16)
         arriving = []
-        for k in range(1, count):
+        for k in far_first:
             arriving.append(
                 launch(
                     remote(
@@ -734,17 +819,17 @@
                         sq_land.at[k - 1],
                         sq_s.at[k - 1],
                         sq_r.at[k - 1],
-                        plane(lax.rem(p + k, count)),
+                        plane(flip(k)),
                     )
                 )
             )
-        loads[6].wait()
+        loads[7].wait()
         swaps[0].wait_recv()
         mine = geared[:, pl.ds(pl.multiple_of(c * half, half), half)]
         theirs = geared[:, pl.ds(pl.multiple_of((1 - c) * half, half), half)]
         total = []
-        for k in list(range(1, count)) + [0]:
-            target = lax.rem(p + k, count)
+        for k in far_first + (0,):
+            target = flip(k)
             lanes = pl.ds(pl.multiple_of(target * HD, HD), HD)
             for i in range(3):
                 part = product(mine, w_own[i, :, lanes]) + product(theirs, w_other[i, :, lanes])
@@ -775,102 +860,99 @@
             total[i] = total[i] * scale
 
         def turned(vectors):
-            return (vectors * cosine + pltpu.roll(vectors, HD // 2, 1) * sine).astype(jnp.bfloat16)
+            return (
+                vectors * cos_ref[...] + pltpu.roll(vectors, HD // 2, 1) * sin_ref[...]
+            ).astype(jnp.bfloat16)
 
         queries = turned(total[0])
         kv_own[0] = turned(total[1])
         kv_own[1] = total[2].astype(jnp.bfloat16)
         swap = launch(remote(kv_own, kv_other, kv_sems.at[0], kv_sems.at[1], partner))
-
         def scored(keys, key_position):
             scores = across_lanes(queries, keys) * (1.0 / math.sqrt(HD))
-            permitted = key_position <= position
-            return jnp.where(permitted, scores, -1e30), permitted
-
-        scores_a, permitted_a = scored(kv_own[0], key_positions[0])
+            return jnp.where(key_position <= position, scores, -1e30)
+
+        scores_a = scored(kv_own[0], key_positions[0])
+        for copy in ups:
+            copy.wait_recv()
+        mine_out.wait()
+        halves = launch(
+            remote(out_rows.at[c], out_rows.at[c], oc_sems.at[0], oc_sems.at[1], partner)
+        )
         swap.wait_recv()
-        scores_b, permitted_b = scored(kv_other[0], key_positions[1])
+        scores_b = scored(kv_other[0], key_positions[1])
         largest = jnp.maximum(
             jnp.max(scores_a, axis=1, keepdims=True), jnp.max(scores_b, axis=1, keepdims=True)
         )
-        raised_a = jnp.where(permitted_a, jnp.exp(scores_a - largest), 0.0)
-        raised_b = jnp.where(permitted_b, jnp.exp(scores_b - largest), 0.0)
+        raised_a = jnp.exp(scores_a - largest)
+        raised_b = jnp.exp(scores_b - largest)
         weight_sum = jnp.sum(raised_a, axis=1, keepdims=True) + jnp.sum(
             raised_b, axis=1, keepdims=True
         )
         weighted = product(raised_a.astype(jnp.bfloat16), kv_own[1]) + product(
             raised_b.astype(jnp.bfloat16), kv_other[1]
         )
-        att_all[p] = (weighted / weight_sum).astype(jnp.bfloat16)
-        for k in range(1, count):
-            launch(
+        tall[t] = (weighted / weight_sum).astype(jnp.bfloat16)
+        risen = {}
+        for k in far_first + (0,):
+            take = pl.ds(pl.multiple_of(flip(k) * slots, slots), slots)
+            for d in range(count - 1, 0, -1):
+                risen[k, d] = launch(
+                    remote(
+                        tall.at[t, take],
+                        tall.at[t, take],
+                        tz_s.at[k, d - 1],
+                        tz_r.at[k, d - 1],
+                        tp_peer(tower(d)),
+                    )
+                )
+        halves.wait_recv()
+        hops, parts_own = [], []
+        summed = patch_ref[...].astype(jnp.float32)
+        for k in far_first + (0,):
+            for d in range(1, count):
+                take = pl.ds(pl.multiple_of(flip(k) * slots, slots), slots)
                 remote(
-                    att_all.at[p],
-                    att_all.at[p],
-                    att_s.at[k - 1],
-                    att_r.at[p],
-                    plane(lax.rem(p + k, count)),
-                )
-            )
-        for k in range(1, count):
-            source = lax.rem(p + k, count)
-            remote(
-                att_all.at[source], att_all.at[source], att_s.at[k - 1], att_r.at[source], plane(source)
-            ).wait_recv()
-        loads[7].wait()
-        swaps[1].wait_recv()
-        hops = []
-        for k in list(range(1, count)) + [0]:
-            target = lax.rem(p + k, count)
-            take = pl.ds(pl.multiple_of(target * slots, slots), slots)
-            attended = jnp.concatenate([att_all[j, take, :] for j in range(count)], axis=1)
-            for output, core in ((o_own, c), (o_other, 1 - c)):
-                parts[target, :, pl.ds(pl.multiple_of(core * half, half), half)] = product(
-                    attended, output[...]
-                ).astype(jnp.bfloat16)
+                    tall.at[tower(-d), take],
+                    tall.at[tower(-d), take],
+                    tz_s.at[k, d - 1],
+                    tz_r.at[k, d - 1],
+                    tp_peer(tower(-d)),
+                ).wait_recv()
+            attended = jnp.concatenate(
+                [tall[q, pl.ds(pl.multiple_of(flip(k) * slots, slots), slots)] for q in range(count)],
+                axis=1,
+            )
+            for core in range(2):
+                lanes = slice(core * half, (core + 1) * half)
+                part = product(attended, out_rows[core].reshape(count * HD, half))
+                if k:
+                    parts[k - 1, :, lanes] = part.astype(jnp.bfloat16)
+                else:
+                    parts_own.append(part)
             if k:
                 hops.append(
                     launch(
                         remote(
-                            parts.at[target],
+                            parts.at[k - 1],
                             land.at[k - 1],
                             a_s.at[k - 1],
                             a_r.at[k - 1],
-                            plane(target),
+                            plane(flip(k)),
                         )
                     )
                 )
-        last = []
-        for k in range(count):
-            origin = lax.rem(p + count - k, count)
-            if k == 0:
-                here = parts.at[p]
-            else:
-                hops[k - 1].wait_recv()
-                here = land.at[k - 1]
-            away = remote(here, final.at[t], b_s.at[k], b_r.at[t], tp_peer(origin))
-            last.append((origin, away))
-
-            @pl.when(origin != t)
-            def _():
-                away.start()
-
-            @pl.when(origin == t)
-            def _():
-                final[t] = here[...]
-
-        summed = patch_ref[...].astype(jnp.float32)
-        for q in range(count):
-
-            @pl.when(t != q)
-            def _():
-                remote(land.at[0], final.at[q], b_s.at[q], b_r.at[q], tp_peer(t)).wait_recv()
-
-            summed = summed + final[q].astype(jnp.float32)
+        summed = summed + jnp.concatenate(parts_own, axis=1)
+        for copy in hops:
+            copy.wait_recv()
+        for k in range(count - 1):
+            summed = summed + land[k].astype(jnp.float32)
         out_ref[...] = jnp.where(in_use, summed, 0.0).astype(jnp.bfloat16)
-
+        enc_out.wait()
         for copy in sent:
             copy.wait_send()
+        for i in range(2):
+            beside(i).wait_send()
         for h in range(2):
             for q in range(count):
 
@@ -883,20 +965,19 @@
                     pass_on(q, h, False).wait_send()
 
         for i in range(panel_count):
-            for k in range(1, count):
-                across(k, i).wait_send()
-        for origin, away, stay in onward:
-
-            @pl.when(origin != p)
-            def _():
-                away.wait_send()
-
-        for origin, away in last:
-
-            @pl.when(origin != t)
-            def _():
-                away.wait_send()
-
+            for q in range(count):
+
+                @pl.when((q <= t) & (t < count - 1))
+                def _():
+                    climb(q, i, True).wait_send()
+
+                @pl.when((q >= t) & (t > 0))
+                def _():
+                    climb(q, i, False).wait_send()
+
+                @pl.when(p != q)
+                def _():
+                    away(q, i).wait_send()
     vmem = pl.BlockSpec(memory_space=pltpu.VMEM)
     hbm = pl.BlockSpec(memory_space=pl.ANY)
     smem = pl.BlockSpec(memory_space=pltpu.SMEM)
@@ -908,8 +989,8 @@
     return pl.pallas_call(
         kernel,
         out_shape=[like((byte_rows, width)), like((slots, columns))],
-        in_specs=[hbm, vmem, hbm, hbm, vmem, smem, hbm, hbm, vmem, hbm, hbm, vmem],
-        out_specs=[vmem, vmem],
+        in_specs=[hbm, vmem, hbm, hbm, vmem, smem, hbm, hbm, vmem, hbm, hbm, hbm],
+        out_specs=[hbm, vmem],
         scratch_shapes=[
             buffer(total_rows, width),
             buffer(*enc_qkv.shape),
@@ -918,18 +999,18 @@
             buffer(size, 8, 128, dtype=jnp.int32),
             buffer(count, 2, share, width),
             buffer(count, total_rows, enc_cols),
+            buffer(*table.shape, dtype=jnp.float32),
+            buffer(row_total, HD, dtype=jnp.float32),
+            buffer(row_total, HD, dtype=jnp.float32),
             buffer(*lift.shape),
             buffer(*cross_kv.shape),
             buffer(slots, width),
             buffer(total_rows, width),
-            buffer(panel_count, slots, group),
-            buffer(near, panel_count, slots, group),
+            buffer(count, panel_count, slots, group),
             buffer(count, panel_count, slots, group),
             buffer(slots, columns),
             buffer(*lat_qkv.shape),
             buffer(*lat_qkv.shape),
-            buffer(*lat_proj.shape),
-            buffer(*lat_proj.shape),
             buffer(row_total, columns),
             buffer(near, 3, row_total, HD),
             buffer(near, 3, row_total, HD),
@@ -937,15 +1018,16 @@
             buffer(near, 8, row_total, dtype=jnp.float32),
             buffer(2, row_total, HD),
             buffer(2, row_total, HD),
+            buffer(count, HD, half),
+            buffer(2, count, HD, half),
             buffer(count, row_total, HD),
-            buffer(count, slots, columns),
             buffer(near, slots, columns),
-            buffer(count, slots, columns),
-            dma((8,)),
+            buffer(near, slots, columns),
+            dma((9,)),
             dma((size - 1,)),
             dma((size - 1,)),
-            dma((2,)),
-            dma((2,)),
+            dma((2, 2)),
+            dma((2, 2)),
             dma((3,)),
             dma((3,)),
             dma((near,)),
@@ -954,12 +1036,13 @@
             dma((near,)),
             dma((1,)),
             dma((1,)),
-            dma((4,)),
+            dma((2,)),
             dma((count, 2)),
             dma((count, 2)),
             dma((count, 2)),
-            dma((near, panel_count)),
-            dma((near, panel_count)),
+            dma((count, panel_count)),
+            dma((count, panel_count)),
+            dma((count, panel_count)),
             dma((count, panel_count)),
             dma((count, panel_count)),
             dma((panel_count,)),
@@ -969,11 +1052,16 @@
             dma((near,)),
             dma((2,)),
             dma((near,)),
-            dma((count,)),
-            dma((near,)),
-            dma((near,)),
-            dma((count,)),
-            dma((count,)),
+            dma((near,)),
+            dma((near,)),
+            dma((near,)),
+            dma((2,)),
+            dma((1,)),
+            dma((count, near)),
+            dma((count, near)),
+            dma((near,)),
+            dma((near,)),
+            dma((1,)),
         ],
         compiler_params=pltpu.CompilerParams(collective_id=call_id, has_side_effects=True),
     )(
@@ -998,14 +1086,14 @@
     table = jnp.asarray(turn_table(lax.axis_size("seq") * starts.shape[1]))
     encoded, latent = whole_layer(
         byte_states,
-        enc_gain[None],
+        enc_gain,
         enc_qkv,
         enc_proj_out,
         starts,
         counts,
         lift,
         cross_kv,
-        latent_gain[None],
+        latent_gain,
         lat_qkv,
         lat_proj_out,
         table,
@@ -1019,8 +1107,9 @@
     byte_rows = byte_states.shape[0] // size
     return (
         size == 2 * tp_size
+        and tp_size == 4
         and WIN % byte_rows == 0
-        and WIN // byte_rows < size
+        and WIN == 2 * byte_rows
         and byte_rows % (32 * tp_size) == 0
         and lat_qkv.shape[2] // tp_size == HD * tp_size
         and lat_qkv.shape[1] % (128 * size) == 0

time: 91.6 us -> 82.7 us (0.903)
  the two profiles are of different devices: /device:TPU:17 before, /device:TPU:0 now
where the time goes in v2:
time: 82.7 us; the launch traced here: 82.5 us
  Pallas kernels  77.7 us (94%)
  local copies, waits for them, and re-layouts  3.44 us (4%)
  between operations  1.29 us (2%)
    pallas_call x1, Pallas kernels, whole_layer(): pl.pallas_call(kernel, out_shape=[like((byte_rows, width)), like((slots,...  77.7 us
    unnamed x2, local copies, waits for them, and re-layouts  3.44 us

profile of v2, /device:TPU:0, one launch (start us, length us, event | category | flops | bytes accessed | tf_op | source)
XLA Modules:
  0.0 82.5 jit_solution(11529915200111036533)
XLA Ops:
  1.3 77.7 %shard_map.131 = (bf16[256,1024]{1,0:T(8,128)(2,1)}, bf16[64,1024]{1,0:T(8,128)(2,1)}) custom-call(bf16[256,1024]{1,0:T(8,128)(2,1)} %states_hbm.1, bf16[1024]{0:T(1024)(128)(2,1)} %gain_ref.1, bf16[3,1024,256]{2,1,0:T(8,128)(2,1)} %qkv_hbm.1, bf16[256,1024]{1,0:T(8,128)(2,1)} %proj_hbm.1, s32[1,64]{1,0:T(1,128)} %starts_ref.1, s32[1]{0:T(128)S(6)} %copy.16.counts_ref, ...), custom_call_target="tpu_custom_call" | custom-call | tf_op jit(solution)/shard_map/pallas_call | solution.py:989
  79.0 1.9 %copy.17 = bf16[256,1024]{1,0:T(8,128)(2,1)} copy(bf16[256,1024]{1,0:T(8,128)(2,1)} %get-tuple-element.4) | data formatting | bytes 1048576
  80.9 1.6 %copy.18 = bf16[64,1024]{1,0:T(8,128)(2,1)} copy(bf16[64,1024]{1,0:T(8,128)(2,1)} %get-tuple-element.5) | data formatting | bytes 262144

commit v3 on v2

--- a/solution.py
+++ b/solution.py
@@ -321,7 +321,8 @@
     half = lat_qkv.shape[1]
     full_width = columns * count
     rows_half = byte_rows // 2
-    spans = ((0, rows_half), (rows_half, total_rows - rows_half))
+    part_rows = slots // 2
+    half_total = row_total // 2
     share = enc_cols // 2
     piece = share // count
 
@@ -329,13 +330,13 @@
         states_hbm, gain_ref, qkv_hbm, proj_hbm, starts_ref, counts_ref, lift_hbm, cross_hbm,
         lgain_ref, w_own_hbm, o_hbm, table_hbm,
         enc_hbm, out_ref,
-        states_ref, qkv_ref, query_ref, kv_ref, infos, proj_ref, att_ref, table_ref, cos_ref, sin_ref,
+        states_ref, qkv_ref, query_ref, kv_ref, infos, proj_ref, att_ref, blend_ref, table_ref, cos_ref, sin_ref,
         lift_ref, cross_ref, pooled_ref, full_ref, panels, rows_ref, patch_ref,
-        w_own, w_other, geared, qkv_send, qkv_land, sq_send, sq_land,
+        w_own, w_other, geared, own_part, qkv_send, qkv_land, sq_send, sq_land,
         kv_own, kv_other, out_quarter, out_rows, tall, parts, land,
         load_sems, info_s, info_r, halo_s, halo_r, edge_s, edge_r, pz_s, pz_r, pp_s, pp_r, pc_s, pc_r,
-        w_sems, up_send, down_send, ag_recv,
-        zup_send, zdown_send, z_recv, plane_send, plane_recv, stay_sems,
+        w_sems, heads_send, heads_recv,
+        z_send, z_recv, plane_send, plane_recv, stay_sems,
         qkv_s, qkv_r, sq_s, sq_r, kv_sems,
         oq_s, oq_r, oz_s, oz_r, oc_sems, own_sems, tz_s, tz_r, a_s, a_r, enc_sem,
     ):
@@ -362,6 +363,28 @@
             return 3 - p
 
         far_first = (3, 2, 1)
+        low = t < 2
+        inner = (t == 1) | (t == 2)
+        first_from = jnp.where(low, t + 1, t - 1)
+        second_from = jnp.where(low, t + 2, t - 2)
+        third_from = jnp.where(lax.rem(t, 2) == 0, count - 1, 0)
+        outer = jnp.where(low, 0, count - 1)
+
+        def to_near(copy_to):
+            copy_to(first_from, 0).start()
+
+            @pl.when(inner)
+            def _():
+                copy_to(outer, 1).start()
+
+        def sent_near(copy_to, over):
+            copy_to(first_from, 0).wait_send()
+
+            @pl.when(inner)
+            def _():
+                copy_to(outer, 1).wait_send()
+                for i in range(3):
+                    over(i).wait_send()
 
         barrier = pltpu.get_barrier_semaphore()
         for k in range(1, size):
@@ -374,7 +397,7 @@
             (qkv_hbm, qkv_ref),
             (table_hbm, table_ref),
             (proj_hbm.at[pl.ds(0, share)], proj_ref.at[0, 0]),
-            (proj_hbm.at[pl.ds(share, share)], proj_ref.at[0, 1]),
+            (proj_hbm.at[pl.ds(share, share)], proj_ref.at[1, 0]),
             (lift_hbm, lift_ref),
             (cross_hbm, cross_ref),
             (w_own_hbm, w_own),
@@ -402,7 +425,7 @@
             launch(
                 remote(
                     proj_hbm.at[pl.ds(pl.multiple_of(c * share + p * piece, piece), piece)],
-                    proj_ref.at[k, c, pl.ds(mine_at, piece)],
+                    proj_ref.at[c, k, pl.ds(mine_at, piece)],
                     pz_s.at[k - 1],
                     pz_r.at[k - 1],
                     tp_peer(tower(k)),
@@ -422,20 +445,22 @@
         normed = rms_scale(values, chip_row).astype(jnp.bfloat16)
         own = pl.ds(WIN, byte_rows)
         loads[1].wait()
-        halos = []
         for i in range(2):
-            kv_ref[i, own] = product(normed, qkv_ref[i + 1]).astype(jnp.bfloat16)
-            halos.append(
-                launch(
-                    remote(
-                        kv_ref.at[i, own],
-                        kv_ref.at[i, pl.ds(0, byte_rows)],
-                        halo_s.at[0, i],
-                        halo_r.at[0, i],
-                        seq_peer(ring(2)),
-                    )
+            fresh = product(normed, qkv_ref[i + 1]).astype(jnp.bfloat16)
+            for h in range(2):
+                kv_ref[h, i, own] = fresh[:, h * share : (h + 1) * share]
+        halos = [
+            launch(
+                remote(
+                    kv_ref.at[h, :, own],
+                    kv_ref.at[h, :, pl.ds(0, byte_rows)],
+                    halo_s.at[0, h],
+                    halo_r.at[0, h],
+                    seq_peer(ring(2)),
                 )
             )
+            for h in range(2)
+        ]
         behind = seq_peer(ring(-1))
         query_ref[0:byte_rows] = (
             product(normed, qkv_ref[0]) * (1.0 / math.sqrt(EH))
@@ -444,7 +469,10 @@
             launch(remote(source, target, edge_s.at[i], edge_r.at[i], behind))
             for i, (source, target) in enumerate(
                 (
-                    (kv_ref.at[:, pl.ds(WIN, EDGE)], kv_ref.at[:, pl.ds(WIN + byte_rows, EDGE)]),
+                    (
+                        kv_ref.at[:, :, pl.ds(WIN, EDGE)],
+                        kv_ref.at[:, :, pl.ds(WIN + byte_rows, EDGE)],
+                    ),
                     (query_ref.at[pl.ds(0, EDGE)], query_ref.at[pl.ds(byte_rows, EDGE)]),
                     (states_ref.at[pl.ds(0, EDGE)], states_ref.at[pl.ds(byte_rows, EDGE)]),
                 )
@@ -454,8 +482,8 @@
         def beside(i):
             first = pl.multiple_of(jnp.where(c == 0, WIN, 0), byte_rows)
             return remote(
-                kv_ref.at[i, pl.ds(first, byte_rows)],
-                kv_ref.at[i, pl.ds(byte_rows, byte_rows)],
+                kv_ref.at[i, :, pl.ds(first, byte_rows)],
+                kv_ref.at[i, :, pl.ds(byte_rows, byte_rows)],
                 halo_s.at[1, i],
                 halo_r.at[1, i],
                 partner,
@@ -504,11 +532,13 @@
 
         def laid(shape, axis, which):
             at = iota(shape, axis)
-            block = at // slots
+            band = at // half_total
+            within = at - band * half_total
+            block = within // part_rows
             result = jnp.broadcast_to(chosen[0][which], shape)
             for i in range(1, count):
                 result = jnp.where(block == i, chosen[i][which], result)
-            return at - block * slots, result
+            return band * part_rows + within - block * part_rows, result
 
         row_slot, row_offset = laid((row_total, 1), 0, 0)
         position = row_offset + row_slot
@@ -538,8 +568,8 @@
         spread = [
             launch(
                 remote(
-                    proj_ref.at[pl.ds(1, near), c, pl.ds(mine_at, piece)],
-                    proj_ref.at[pl.ds(1, near), c, pl.ds(mine_at, piece)],
+                    proj_ref.at[c, pl.ds(1, near), pl.ds(mine_at, piece)],
+                    proj_ref.at[c, pl.ds(1, near), pl.ds(mine_at, piece)],
                     pp_s.at[k - 1],
                     pp_r.at[k - 1],
                     plane(flip(k)),
@@ -547,6 +577,105 @@
             )
             for k in far_first
         ]
+        def halo_arrives(h):
+            halos[h].wait_recv()
+
+            @pl.when(c == 1)
+            def _():
+                beside(h).start()
+
+        halo_arrives(0)
+        for copy in edges:
+            copy.wait_recv()
+
+        beside(0).wait_recv()
+        def share_heads(origin, h, target, sem):
+            return remote(
+                att_ref.at[origin, h],
+                att_ref.at[origin, h],
+                heads_send.at[h, sem],
+                heads_recv.at[h, origin],
+                tp_peer(target),
+            )
+
+        def attend(pair, begin, rows):
+            reach_rows = rows + WIN
+            keys = kv_ref[pair, 0, begin : begin + reach_rows]
+            seen_values = kv_ref[pair, 1, begin : begin + reach_rows]
+            queries = query_ref[begin : begin + rows, pair * share : (pair + 1) * share]
+            head_of = iota((rows, share), 1) // EH
+            stacked = jnp.concatenate(
+                [jnp.where(head_of == h, queries, jnp.zeros_like(queries)) for h in range(share // EH)],
+                axis=0,
+            )
+            query_at = iota((rows, reach_rows), 0) + begin
+            key_at = iota((rows, reach_rows), 1) + (begin - WIN)
+            near_by = (
+                (key_at <= query_at) & (key_at > query_at - WIN) & (key_at >= -s * byte_rows)
+            )
+            near_bias = jnp.where(near_by, 0.0, -1e30)
+            scores = across_lanes(stacked, keys)
+            raised, sums = [], []
+            for h in range(share // EH):
+                here = scores[h * rows : (h + 1) * rows] + near_bias
+                here = jnp.exp(here - jnp.max(here, axis=1, keepdims=True))
+                sums.append(jnp.sum(here, axis=1, keepdims=True))
+                raised.append(here.astype(jnp.bfloat16))
+            seen = product(jnp.concatenate(raised, axis=0), seen_values)
+            attended = jnp.zeros((rows, share), jnp.float32)
+            for h in range(share // EH):
+                attended = jnp.where(
+                    head_of == h, seen[h * rows : (h + 1) * rows] / sums[h], attended
+                )
+            att_ref[t, pair, begin : begin + rows] = attended.astype(jnp.bfloat16)
+
+        for h in range(2):
+            if h:
+                halo_arrives(1)
+                beside(1).wait_recv()
+            for begin, rows in ((0, rows_half), (rows_half, rows_half), (byte_rows, EDGE)):
+                attend(h, begin, rows)
+            to_near(lambda target, sem: share_heads(t, h, target, sem))
+
+        swaps = [launch(remote(w_own_hbm, w_other, w_sems.at[0], w_sems.at[1], partner))]
+        sources = (first_from, second_from, third_from)
+        beyond = (outer, outer, first_from)
+
+        def hand_over(which, h):
+            return share_heads(sources[which], h, beyond[which], 2 + which)
+
+        def gain_heads(which, h):
+            hand_over(which, h).wait_recv()
+
+            @pl.when(inner)
+            def _():
+                hand_over(which, h).start()
+
+        def blended(h):
+            attended = jnp.concatenate([att_ref[tower(-k), h] for k in range(count)], axis=1)
+            return product(attended, proj_ref[h].reshape(count * share, width))
+        gain_heads(0, 0)
+
+        @pl.when(inner)
+        def _():
+            gain_heads(2, 0)
+
+        gain_heads(0, 1)
+
+        @pl.when(inner)
+        def _():
+            gain_heads(2, 1)
+        for copy in spread:
+            copy.wait_recv()
+        shared = launch(
+            remote(
+                proj_ref.at[c, pl.ds(1, near)],
+                proj_ref.at[c, pl.ds(1, near)],
+                pc_s.at[0],
+                pc_r.at[0],
+                partner,
+            )
+        )
         quarters = [
             launch(
                 remote(
@@ -559,121 +688,21 @@
             )
             for k in far_first
         ]
-        for i in range(2):
-            halos[i].wait_recv()
-
-            @pl.when(c == 1)
-            def _():
-                beside(i).start()
-
-        for copy in edges:
-            copy.wait_recv()
-        for i in range(2):
-            beside(i).wait_recv()
-        swaps = [launch(remote(w_own_hbm, w_other, w_sems.at[0], w_sems.at[1], partner))]
-
-        def pass_on(origin, h, up):
-            begin, rows = spans[h]
-            step = 1 if up else -1
-            return remote(
-                att_ref.at[origin, pl.ds(begin, rows)],
-                att_ref.at[origin, pl.ds(begin, rows)],
-                (up_send if up else down_send).at[origin, h],
-                ag_recv.at[origin, h],
-                tp_peer(tower(step)),
-            )
-
-        def attend(begin, rows):
-            reach_rows = rows + WIN
-            keys = kv_ref[0, begin : begin + reach_rows]
-            seen_values = kv_ref[1, begin : begin + reach_rows]
-            queries = query_ref[begin : begin + rows]
-            head_of = iota((rows, enc_cols), 1) // EH
-            stacked = jnp.concatenate(
-                [jnp.where(head_of == h, queries, jnp.zeros_like(queries)) for h in range(enc_heads)],
-                axis=0,
-            )
-            query_at = iota((rows, reach_rows), 0) + begin
-            key_at = iota((rows, reach_rows), 1) + (begin - WIN)
-            near_by = (
-                (key_at <= query_at) & (key_at > query_at - WIN) & (key_at >= -s * byte_rows)
-            )
-            near_bias = jnp.where(near_by, 0.0, -1e30)
-            scores = across_lanes(stacked, keys)
-            raised, sums = [], []
-            for h in range(enc_heads):
-                here = scores[h * rows : (h + 1) * rows] + near_bias
-                here = jnp.exp(here - jnp.max(here, axis=1, keepdims=True))
-                sums.append(jnp.sum(here, axis=1, keepdims=True))
-                raised.append(here.astype(jnp.bfloat16))
-            seen = product(jnp.concatenate(raised, axis=0), seen_values)
-            attended = jnp.zeros((rows, enc_cols), jnp.float32)
-            for h in range(enc_heads):
-                attended = jnp.where(
-                    head_of == h, seen[h * rows : (h + 1) * rows] / sums[h], attended
-                )
-            att_ref[t, begin : begin + rows] = attended.astype(jnp.bfloat16)
-        for h in range(2):
-            begin, rows = spans[h]
-            attend(begin, rows_half)
-            if rows > rows_half:
-                attend(begin + rows_half, rows - rows_half)
-
-            @pl.when(t < count - 1)
-            def _():
-                pass_on(t, h, True).start()
-
-            @pl.when(t > 0)
-            def _():
-                pass_on(t, h, False).start()
-
-        def relay(d, h):
-            @pl.when(t - d >= 0)
-            def _():
-                pass_on(t - d, h, True).wait_recv()
-
-                @pl.when(t < count - 1)
-                def _():
-                    pass_on(t - d, h, True).start()
-
-            @pl.when(t + d < count)
-            def _():
-                pass_on(t + d, h, False).wait_recv()
-
-                @pl.when(t > 0)
-                def _():
-                    pass_on(t + d, h, False).start()
-
-        def finish(h):
-            begin, rows = spans[h]
-            total = states_ref[begin : begin + rows].astype(jnp.float32)
-            for k in range(count):
-                total = total + product(
-                    att_ref[tower(-k), begin : begin + rows],
-                    proj_ref[k].reshape(enc_cols, width),
-                )
-            full_ref[begin : begin + rows] = total.astype(jnp.bfloat16)
-        for copy in spread:
-            copy.wait_recv()
-        shared = launch(
-            remote(
-                proj_ref.at[pl.ds(1, near), c],
-                proj_ref.at[pl.ds(1, near), c],
-                pc_s.at[0],
-                pc_r.at[0],
-                partner,
-            )
-        )
-        for d in range(1, count - 1):
-            for h in range(2):
-                relay(d, h)
         loads[3].wait()
         loads[4].wait()
-        relay(count - 1, 0)
+        gain_heads(1, 0)
+
+        @pl.when(jnp.logical_not(inner))
+        def _():
+            gain_heads(2, 0)
         shared.wait_recv()
-        finish(0)
-        relay(count - 1, 1)
-        finish(1)
+        blend_ref[...] = states_ref[...].astype(jnp.float32) + blended(0)
+        gain_heads(1, 1)
+
+        @pl.when(jnp.logical_not(inner))
+        def _():
+            gain_heads(2, 1)
+        full_ref[...] = (blend_ref[...] + blended(1)).astype(jnp.bfloat16)
         enc_out = pltpu.make_async_copy(full_ref.at[pl.ds(0, byte_rows)], enc_hbm, enc_sem.at[0])
         enc_out.start()
 
@@ -682,36 +711,54 @@
         loads[5].wait()
         loads[6].wait()
 
-        def climb(origin, i, up):
-            step = 1 if up else -1
+        half_lanes = columns // 2
+
+        def window(r, i):
+            if r == 0:
+                return pl.ds(pl.multiple_of(i * group, group), group)
+            return pl.ds(i * half_lanes, half_lanes)
+
+        def slot_of(r, i):
+            return i if r == 0 else panel_count + i
+
+        def climb(origin, r, i, target, sem):
             return remote(
-                panels.at[origin, i],
-                panels.at[origin, i],
-                (zup_send if up else zdown_send).at[origin, i],
-                z_recv.at[origin, i],
-                tp_peer(tower(step)),
-            )
-
-        def away(origin, i):
+                panels.at[origin, r, :, window(r, i)],
+                panels.at[origin, r, :, window(r, i)],
+                z_send.at[slot_of(r, i), sem],
+                z_recv.at[slot_of(r, i), origin],
+                tp_peer(target),
+            )
+
+        def climb_over(which, r, i):
+            return climb(sources[which], r, i, beyond[which], 2 + which)
+
+        def away(origin, r, i):
             return remote(
-                panels.at[origin, i],
-                rows_ref.at[p, i],
-                plane_send.at[origin, i],
-                plane_recv.at[p, i],
+                panels.at[origin, r, :, window(r, i)],
+                rows_ref.at[r, p, :, window(r, i)],
+                plane_send.at[origin, slot_of(r, i)],
+                plane_recv.at[p, slot_of(r, i)],
                 plane(origin),
             )
 
-        def stay(i):
-            return pltpu.make_async_copy(panels.at[p, i], rows_ref.at[p, i], stay_sems.at[i])
-
-        def spill(origin, i):
+        def stay(r, i):
+            return pltpu.make_async_copy(
+                panels.at[p, r, :, window(r, i)],
+                rows_ref.at[r, p, :, window(r, i)],
+                stay_sems.at[slot_of(r, i)],
+            )
+
+        def spill(origin, r, i):
             @pl.when(origin != p)
             def _():
-                away(origin, i).start()
+                away(origin, r, i).start()
 
             @pl.when(origin == p)
             def _():
-                stay(i).start()
+                stay(r, i).start()
+
+        widths = (panel_count, 2)
 
         def heads(i, carry):
             cols = pl.ds(pl.multiple_of(i * group, group), group)
@@ -733,131 +780,139 @@
             patch = lifted + jnp.concatenate(crossed, axis=1)
             panel = jnp.where(in_use, patch, 0.0).astype(jnp.bfloat16)
             patch_ref[:, cols] = panel
-            panels[t, i] = panel
-
-            @pl.when(t < count - 1)
-            def _():
-                climb(t, i, True).start()
-
-            @pl.when(t > 0)
-            def _():
-                climb(t, i, False).start()
-
-            spill(t, i)
+            for r in range(2):
+                panels[t, r, :, cols] = panel[r * part_rows : (r + 1) * part_rows]
+            to_near(lambda target, sem: climb(t, 0, i, target, sem))
+            spill(t, 0, i)
             return carry
         lax.fori_loop(0, panel_count, heads, 0)
-        for d in range(1, count):
-            for i in range(panel_count):
-
-                @pl.when(t - d >= 0)
-                def _():
-                    climb(t - d, i, True).wait_recv()
-
-                    @pl.when(t < count - 1)
-                    def _():
-                        climb(t - d, i, True).start()
-
-                    spill(t - d, i)
-
-                @pl.when(t + d < count)
-                def _():
-                    climb(t + d, i, False).wait_recv()
-
-                    @pl.when(t > 0)
-                    def _():
-                        climb(t + d, i, False).start()
-
-                    spill(t + d, i)
-        for copy in quarters:
-            copy.wait_recv()
-        loads[8].wait()
-        mine_out = pltpu.make_async_copy(out_quarter.at[t], out_rows.at[c, t], own_sems.at[0])
-        mine_out.start()
-        ups = [
-            launch(
-                remote(
-                    out_quarter.at[tower(k)],
-                    out_rows.at[c, t],
-                    oz_s.at[k - 1],
-                    oz_r.at[k - 1],
-                    tp_peer(tower(k)),
-                )
-            )
-            for k in range(1, count)
-        ]
-        for q in range(count):
-
-            @pl.when(p != q)
+        for i in range(widths[1]):
+            to_near(lambda target, sem: climb(t, 1, i, target, sem))
+            spill(t, 1, i)
+
+        def gain_panel(which, r, i):
+            climb_over(which, r, i).wait_recv()
+
+            @pl.when(inner)
             def _():
-                for i in range(panel_count):
-                    remote(
-                        panels.at[0, i],
-                        rows_ref.at[q, i],
-                        plane_send.at[q, i],
-                        plane_recv.at[q, i],
-                        plane(p),
-                    ).wait_recv()
-
-        for i in range(panel_count):
-            stay(i).wait()
-        values = jnp.concatenate(
-            [rows_ref[:, i].reshape(row_total, group) for i in range(panel_count)], axis=1
-        ).astype(jnp.float32)
-        squares = jnp.sum(values * values, axis=1, keepdims=True)
-        eye = iota((row_total, row_total), 0) == iota((row_total, row_total), 1)
-        flat = jnp.sum(jnp.where(eye, squares, 0.0), axis=0, keepdims=True)
-        sq_send[...] = jnp.broadcast_to(flat, sq_send.shape)
+                climb_over(which, r, i).start()
+
+            spill(sources[which], r, i)
+
+        for r in range(2):
+            @pl.when(inner)
+            def _():
+                for i in range(widths[r]):
+                    gain_panel(0, r, i)
+                for i in range(widths[r]):
+                    gain_panel(2, r, i)
+                    if i:
+                        gain_panel(1, r, i - 1)
+                gain_panel(1, r, widths[r] - 1)
+
+            @pl.when(jnp.logical_not(inner))
+            def _():
+                for which in range(3):
+                    for i in range(widths[r]):
+                        gain_panel(which, r, i)
+
+        arriving, total, flats = [], [], []
+        eye = iota((half_total, half_total), 0) == iota((half_total, half_total), 1)
         chip_gain = lgain_ref[pl.ds(pl.multiple_of(p * columns, columns), columns)]
         chip_gain = chip_gain.astype(jnp.float32).reshape(1, columns)
-        geared[...] = (values * chip_gain).astype(jnp.bfloat16)
-        arriving = []
-        for k in far_first:
-            arriving.append(
-                launch(
-                    remote(
-                        sq_send,
-                        sq_land.at[k - 1],
-                        sq_s.at[k - 1],
-                        sq_r.at[k - 1],
-                        plane(flip(k)),
+        for r in range(2):
+            for q in range(count):
+
+                @pl.when(p != q)
+                def _():
+                    for i in range(widths[r]):
+                        remote(
+                            panels.at[0, r, :, window(r, i)],
+                            rows_ref.at[r, q, :, window(r, i)],
+                            plane_send.at[q, slot_of(r, i)],
+                            plane_recv.at[q, slot_of(r, i)],
+                            plane(p),
+                        ).wait_recv()
+
+            for i in range(widths[r]):
+                stay(r, i).wait()
+            if r:
+                for copy in quarters:
+                    copy.wait_recv()
+                loads[8].wait()
+                mine_out = pltpu.make_async_copy(out_quarter.at[t], out_rows.at[c, t], own_sems.at[0])
+                mine_out.start()
+                ups = [
+                    launch(
+                        remote(
+                            out_quarter.at[tower(k)],
+                            out_rows.at[c, t],
+                            oz_s.at[k - 1],
+                            oz_r.at[k - 1],
+                            tp_peer(tower(k)),
+                        )
                     )
-                )
-            )
-        loads[7].wait()
-        swaps[0].wait_recv()
-        mine = geared[:, pl.ds(pl.multiple_of(c * half, half), half)]
-        theirs = geared[:, pl.ds(pl.multiple_of((1 - c) * half, half), half)]
-        total = []
-        for k in far_first + (0,):
-            target = flip(k)
-            lanes = pl.ds(pl.multiple_of(target * HD, HD), HD)
-            for i in range(3):
-                part = product(mine, w_own[i, :, lanes]) + product(theirs, w_other[i, :, lanes])
-                if k:
-                    qkv_send[k - 1, i] = part.astype(jnp.bfloat16)
-                else:
-                    total.append(part)
-            if k:
+                    for k in range(1, count)
+                ]
+            values = rows_ref[r].reshape(half_total, columns).astype(jnp.float32)
+            squares = jnp.sum(values * values, axis=1, keepdims=True)
+            flat = jnp.sum(jnp.where(eye, squares, 0.0), axis=0, keepdims=True)
+            flats.append(flat)
+            sq_send[r] = jnp.broadcast_to(flat, (8, half_total))
+            geared[...] = (values * chip_gain).astype(jnp.bfloat16)
+            for k in far_first:
                 arriving.append(
                     launch(
                         remote(
-                            qkv_send.at[k - 1],
-                            qkv_land.at[k - 1],
-                            qkv_s.at[k - 1],
-                            qkv_r.at[k - 1],
-                            plane(target),
+                            sq_send.at[r],
+                            sq_land.at[r, k - 1],
+                            sq_s.at[r, k - 1],
+                            sq_r.at[r, k - 1],
+                            plane(flip(k)),
                         )
                     )
                 )
+            if r == 0:
+                loads[7].wait()
+                swaps[0].wait_recv()
+            mine = geared[:, pl.ds(pl.multiple_of(c * half, half), half)]
+            theirs = geared[:, pl.ds(pl.multiple_of((1 - c) * half, half), half)]
+            for k in far_first + (0,):
+                target = flip(k)
+                lanes = pl.ds(pl.multiple_of(target * HD, HD), HD)
+                for i in range(3):
+                    part = product(mine, w_own[i, :, lanes]) + product(theirs, w_other[i, :, lanes])
+                    if k:
+                        qkv_send[r, k - 1, i] = part.astype(jnp.bfloat16)
+                    else:
+                        own_part[r, i] = part
+                if k:
+                    arriving.append(
+                        launch(
+                            remote(
+                                qkv_send.at[r, k - 1],
+                                qkv_land.at[r, k - 1],
+                                qkv_s.at[r, k - 1],
+                                qkv_r.at[r, k - 1],
+                                plane(target),
+                            )
+                        )
+                    )
         for copy in arriving:
             copy.wait_recv()
-        flat = flat + jnp.sum(sq_land[:, 0:1, :], axis=0)
-        square_sum = jnp.sum(jnp.where(eye, flat, 0.0), axis=1, keepdims=True)
-        scale = lax.rsqrt(square_sum / full_width + epsilon)
+        scales = []
+        for r in range(2):
+            flat = flats[r] + jnp.sum(sq_land[r, :, 0:1, :], axis=0)
+            square_sum = jnp.sum(jnp.where(eye, flat, 0.0), axis=1, keepdims=True)
+            scales.append(lax.rsqrt(square_sum / full_width + epsilon))
         for i in range(3):
-            for k in range(count - 1):
-                total[i] = total[i] + qkv_land[k, i].astype(jnp.float32)
-            total[i] = total[i] * scale
+            bands = []
+            for r in range(2):
+                band = own_part[r, i]
+                for k in range(count - 1):
+                    band = band + qkv_land[r, k, i].astype(jnp.float32)
+                bands.append(band * scales[r])
+            total.append(jnp.concatenate(bands, axis=0))
 
         def turned(vectors):
             return (
@@ -892,15 +947,15 @@
         weighted = product(raised_a.astype(jnp.bfloat16), kv_own[1]) + product(
             raised_b.astype(jnp.bfloat16), kv_other[1]
         )
-        tall[t] = (weighted / weight_sum).astype(jnp.bfloat16)
+        tall[t] = (weighted / weight_sum).astype(jnp.bfloat16).reshape(2, half_total, HD)
         risen = {}
         for k in far_first + (0,):
-            take = pl.ds(pl.multiple_of(flip(k) * slots, slots), slots)
+            take = pl.ds(pl.multiple_of(flip(k) * part_rows, part_rows), part_rows)
             for d in range(count - 1, 0, -1):
                 risen[k, d] = launch(
                     remote(
-                        tall.at[t, take],
-                        tall.at[t, take],
+                        tall.at[t, :, take],
+                        tall.at[t, :, take],
                         tz_s.at[k, d - 1],
                         tz_r.at[k, d - 1],
                         tp_peer(tower(d)),
@@ -911,17 +966,17 @@
         summed = patch_ref[...].astype(jnp.float32)
         for k in far_first + (0,):
             for d in range(1, count):
-                take = pl.ds(pl.multiple_of(flip(k) * slots, slots), slots)
+                take = pl.ds(pl.multiple_of(flip(k) * part_rows, part_rows), part_rows)
                 remote(
-                    tall.at[tower(-d), take],
-                    tall.at[tower(-d), take],
+                    tall.at[tower(-d), :, take],
+                    tall.at[tower(-d), :, take],
                     tz_s.at[k, d - 1],
                     tz_r.at[k, d - 1],
                     tp_peer(tower(-d)),
                 ).wait_recv()
+            take = pl.ds(pl.multiple_of(flip(k) * part_rows, part_rows), part_rows)
             attended = jnp.concatenate(
-                [tall[q, pl.ds(pl.multiple_of(flip(k) * slots, slots), slots)] for q in range(count)],
-                axis=1,
+                [tall[q, :, take].reshape(slots, HD) for q in range(count)], axis=1
             )
             for core in range(2):
                 lanes = slice(core * half, (core + 1) * half)
@@ -954,30 +1009,21 @@
         for i in range(2):
             beside(i).wait_send()
         for h in range(2):
-            for q in range(count):
-
-                @pl.when((q <= t) & (t < count - 1))
-                def _():
-                    pass_on(q, h, True).wait_send()
-
-                @pl.when((q >= t) & (t > 0))
-                def _():
-                    pass_on(q, h, False).wait_send()
-
-        for i in range(panel_count):
-            for q in range(count):
-
-                @pl.when((q <= t) & (t < count - 1))
-                def _():
-                    climb(q, i, True).wait_send()
-
-                @pl.when((q >= t) & (t > 0))
-                def _():
-                    climb(q, i, False).wait_send()
-
-                @pl.when(p != q)
-                def _():
-                    away(q, i).wait_send()
+            sent_near(
+                lambda target, sem: share_heads(t, h, target, sem), lambda which: hand_over(which, h)
+            )
+
+        for r in range(2):
+            for i in range(widths[r]):
+                sent_near(
+                    lambda target, sem: climb(t, r, i, target, sem),
+                    lambda which: climb_over(which, r, i),
+                )
+                for q in range(count):
+
+                    @pl.when(p != q)
+                    def _():
+                        away(q, r, i).wait_send()
     vmem = pl.BlockSpec(memory_space=pltpu.VMEM)
     hbm = pl.BlockSpec(memory_space=pl.ANY)
     smem = pl.BlockSpec(memory_space=pltpu.SMEM)
@@ -995,10 +1041,11 @@
             buffer(total_rows, width),
             buffer(*enc_qkv.shape),
             buffer(total_rows, enc_cols),
-            buffer(2, WIN + total_rows, enc_cols),
+            buffer(2, 2, WIN + total_rows, share),
             buffer(size, 8, 128, dtype=jnp.int32),
-            buffer(count, 2, share, width),
-            buffer(count, total_rows, enc_cols),
+            buffer(2, count, share, width),
+            buffer(count, 2, total_rows, share),
+            buffer(total_rows, width, dtype=jnp.float32),
             buffer(*table.shape, dtype=jnp.float32),
             buffer(row_total, HD, dtype=jnp.float32),
             buffer(row_total, HD, dtype=jnp.float32),
@@ -1006,21 +1053,22 @@
             buffer(*cross_kv.shape),
             buffer(slots, width),
             buffer(total_rows, width),
-            buffer(count, panel_count, slots, group),
-            buffer(count, panel_count, slots, group),
+            buffer(count, 2, part_rows, columns),
+            buffer(2, count, part_rows, columns),
             buffer(slots, columns),
             buffer(*lat_qkv.shape),
             buffer(*lat_qkv.shape),
-            buffer(row_total, columns),
-            buffer(near, 3, row_total, HD),
-            buffer(near, 3, row_total, HD),
-            buffer(8, row_total, dtype=jnp.float32),
-            buffer(near, 8, row_total, dtype=jnp.float32),
+            buffer(half_total, columns),
+            buffer(2, 3, half_total, HD, dtype=jnp.float32),
+            buffer(2, near, 3, half_total, HD),
+            buffer(2, near, 3, half_total, HD),
+            buffer(2, 8, half_total, dtype=jnp.float32),
+            buffer(2, near, 8, half_total, dtype=jnp.float32),
             buffer(2, row_total, HD),
             buffer(2, row_total, HD),
             buffer(count, HD, half),
             buffer(2, count, HD, half),
-            buffer(count, row_total, HD),
+            buffer(count, 2, half_total, HD),
             buffer(near, slots, columns),
             buffer(near, slots, columns),
             dma((9,)),
@@ -1037,19 +1085,17 @@
             dma((1,)),
             dma((1,)),
             dma((2,)),
-            dma((count, 2)),
-            dma((count, 2)),
-            dma((count, 2)),
-            dma((count, panel_count)),
-            dma((count, panel_count)),
-            dma((count, panel_count)),
-            dma((count, panel_count)),
-            dma((count, panel_count)),
-            dma((panel_count,)),
-            dma((near,)),
-            dma((near,)),
-            dma((near,)),
-            dma((near,)),
+            dma((2, 5)),
+            dma((2, count)),
+            dma((panel_count + 2, 5)),
+            dma((panel_count + 2, count)),
+            dma((count, panel_count + 2)),
+            dma((count, panel_count + 2)),
+            dma((panel_count + 2,)),
+            dma((2, near)),
+            dma((2, near)),
+            dma((2, near)),
+            dma((2, near)),
             dma((2,)),
             dma((near,)),
             dma((near,)),
@@ -1068,6 +1114,33 @@
         states, gain, enc_qkv, proj, starts, counts, lift, cross_kv, latent_gain, lat_qkv, lat_proj,
         table,
     )
+
+
+def settle(*arrays):
+    total = len(arrays)
+
+    def kernel(*refs):
+        ins, outs, holds = refs[:total], refs[total : 2 * total], refs[2 * total : 3 * total]
+        in_sems, out_sems = refs[3 * total :]
+        takes = [pltpu.make_async_copy(ins[i], holds[i], in_sems.at[i]) for i in range(total)]
+        puts = [pltpu.make_async_copy(holds[i], outs[i], out_sems.at[i]) for i in range(total)]
+        for take in takes:
+            take.start()
+        for take, put in zip(takes, puts):
+            take.wait()
+            put.start()
+        for put in puts:
+            put.wait()
+
+    hbm = pl.BlockSpec(memory_space=pl.ANY)
+    return pl.pallas_call(
+        kernel,
+        out_shape=[like(value.shape, value.dtype) for value in arrays],
+        in_specs=[hbm] * total,
+        out_specs=[hbm] * total,
+        scratch_shapes=[pltpu.VMEM(value.shape, value.dtype) for value in arrays]
+        + [pltpu.SemaphoreType.DMA((total,))] * 2,
+    )(*arrays)
 
 
 def fused_shards(
@@ -1099,7 +1172,7 @@
         table,
         1,
     )
-    return (encoded, latent)
+    return settle(encoded, latent)
 
 
 def fits_pairs(mesh, byte_states, enc_qkv, starts, lat_qkv):

time: 82.7 us -> 78.7 us (0.952)
  local copies, waits for them, and re-layouts: 3.44 us -> 0 us
    unnamed x2 -> x0, local copies, waits for them, and re-layouts: 3.44 us -> none
    pallas_call x1, Pallas kernels: 77.7 us -> 75.3 us  [whole_layer(): pl.pallas_call(kernel, out_shape=[like((byte_rows, width)), like((slots,...]
    pallas_call x0 -> x1, Pallas kernels: none -> 1.9 us  [settle(): pl.pallas_call(kernel, out_shape=[like(value.shape, value.dtype) for valu...]
where the time goes in v3:
time: 78.7 us; the launch traced here: 78.4 us
  Pallas kernels  77.2 us (98%)
  between operations  1.29 us (2%)
    pallas_call x1, Pallas kernels, whole_layer(): pl.pallas_call(kernel, out_shape=[like((byte_rows, width)), like((slots,...  75.3 us
    pallas_call x1, Pallas kernels, settle(): pl.pallas_call(kernel, out_shape=[like(value.shape, value.dtype) for valu...  1.9 us

profile of v3, /device:TPU:0, one launch (start us, length us, event | category | flops | bytes accessed | tf_op | source)
XLA Modules:
  0.0 78.4 jit_solution(3917753528753533505)
XLA Ops:
  1.3 75.3 %shard_map.131 = (bf16[256,1024]{1,0:T(8,128)(2,1)}, bf16[64,1024]{1,0:T(8,128)(2,1)}) custom-call(bf16[256,1024]{1,0:T(8,128)(2,1)} %states_hbm.1, bf16[1024]{0:T(1024)(128)(2,1)} %gain_ref.1, bf16[3,1024,256]{2,1,0:T(8,128)(2,1)} %qkv_hbm.1, bf16[256,1024]{1,0:T(8,128)(2,1)} %proj_hbm.1, s32[1,64]{1,0:T(1,128)} %starts_ref.1, s32[1]{0:T(128)S(6)} %copy.14.counts_ref, ...), custom_call_target="tpu_custom_call" | custom-call | tf_op jit(solution)/shard_map/pallas_call | solution.py:1035
  76.5 1.9 %shard_map.132 = (bf16[256,1024]{1,0:T(8,128)(2,1)}, bf16[64,1024]{1,0:T(8,128)(2,1)}) custom-call(bf16[256,1024]{1,0:T(8,128)(2,1)} %get-tuple-element.4.refs_0_, bf16[64,1024]{1,0:T(8,128)(2,1)} %get-tuple-element.5.refs_1_), custom_call_target="tpu_custom_call" | custom-call | tf_op jit(solution)/shard_map/pallas_call | solution.py:1136

commit v4 on v3

--- a/solution.py
+++ b/solution.py
@@ -336,8 +336,8 @@
         kv_own, kv_other, out_quarter, out_rows, tall, parts, land,
         load_sems, info_s, info_r, halo_s, halo_r, edge_s, edge_r, pz_s, pz_r, pp_s, pp_r, pc_s, pc_r,
         w_sems, heads_send, heads_recv,
-        z_send, z_recv, plane_send, plane_recv, stay_sems,
-        qkv_s, qkv_r, sq_s, sq_r, kv_sems,
+        panel_send, panel_recv, stay_sems,
+        qkv_s, qkv_r, sq_s, sq_r, kv_s, kv_r,
         oq_s, oq_r, oz_s, oz_r, oc_sems, own_sems, tz_s, tz_r, a_s, a_r, enc_sem,
     ):
         s, t = lax.axis_index("seq"), lax.axis_index("tp")
@@ -391,6 +391,13 @@
             pl.semaphore_signal(barrier, inc=1, device_id=seq_peer(ring(k)), device_id_type=MESH)
         for k in range(1, count):
             pl.semaphore_signal(barrier, inc=1, device_id=tp_peer(tower(k)), device_id_type=MESH)
+
+        @pl.when(p != t)
+        def _():
+            for k in far_first:
+                away_peer = {"seq": 2 * flip(k) + c, "tp": p}
+                pl.semaphore_signal(barrier, inc=1, device_id=away_peer, device_id_type=MESH)
+
         own_rows = pl.ds(pl.multiple_of(p * HD, HD), HD)
         load_plan = (
             (states_hbm, states_ref.at[pl.ds(0, byte_rows)]),
@@ -419,7 +426,29 @@
         infos[s] = jnp.where(
             info_lane == 0, counts_ref[0], jnp.where(info_lane == 1, starts_ref[0:1, 0:1], 0)
         )
-        pl.semaphore_wait(barrier, size - 1 + count - 1)
+        loads[0].wait()
+        values = states_ref[0:byte_rows].astype(jnp.float32)
+        chip_row = gain_ref[...].astype(jnp.float32).reshape(1, width)
+        normed = rms_scale(values, chip_row).astype(jnp.bfloat16)
+        own = pl.ds(WIN, byte_rows)
+        loads[1].wait()
+        for i in range(2):
+            fresh = product(normed, qkv_ref[i + 1]).astype(jnp.bfloat16)
+            for h in range(2):
+                kv_ref[h, i, own] = fresh[:, h * share : (h + 1) * share]
+        query_ref[0:byte_rows] = (
+            product(normed, qkv_ref[0]) * (1.0 / math.sqrt(EH))
+        ).astype(jnp.bfloat16)
+        greetings = size - 1 + count - 1
+
+        @pl.when(p == t)
+        def _():
+            pl.semaphore_wait(barrier, greetings)
+
+        @pl.when(p != t)
+        def _():
+            pl.semaphore_wait(barrier, greetings + count - 1)
+
         mine_at = pl.multiple_of(p * piece, piece)
         lifts = [
             launch(
@@ -439,32 +468,7 @@
             )
             for k in range(1, size)
         ]
-        loads[0].wait()
-        values = states_ref[0:byte_rows].astype(jnp.float32)
-        chip_row = gain_ref[...].astype(jnp.float32).reshape(1, width)
-        normed = rms_scale(values, chip_row).astype(jnp.bfloat16)
-        own = pl.ds(WIN, byte_rows)
-        loads[1].wait()
-        for i in range(2):
-            fresh = product(normed, qkv_ref[i + 1]).astype(jnp.bfloat16)
-            for h in range(2):
-                kv_ref[h, i, own] = fresh[:, h * share : (h + 1) * share]
-        halos = [
-            launch(
-                remote(
-                    kv_ref.at[h, :, own],
-                    kv_ref.at[h, :, pl.ds(0, byte_rows)],
-                    halo_s.at[0, h],
-                    halo_r.at[0, h],
-                    seq_peer(ring(2)),
-                )
-            )
-            for h in range(2)
-        ]
         behind = seq_peer(ring(-1))
-        query_ref[0:byte_rows] = (
-            product(normed, qkv_ref[0]) * (1.0 / math.sqrt(EH))
-        ).astype(jnp.bfloat16)
         edges = [
             launch(remote(source, target, edge_s.at[i], edge_r.at[i], behind))
             for i, (source, target) in enumerate(
@@ -478,7 +482,18 @@
                 )
             )
         ]
-
+        halos = [
+            launch(
+                remote(
+                    kv_ref.at[h, :, own],
+                    kv_ref.at[h, :, pl.ds(0, byte_rows)],
+                    halo_s.at[0, h],
+                    halo_r.at[0, h],
+                    seq_peer(ring(2)),
+                )
+            )
+            for h in range(2)
+        ]
         def beside(i):
             first = pl.multiple_of(jnp.where(c == 0, WIN, 0), byte_rows)
             return remote(
@@ -563,6 +578,14 @@
         low_lanes = iota((row_total, HD), 1) < HD // 2
         cos_ref[...] = jnp.where(low_lanes, turns, swapped)
         sin_ref[...] = jnp.where(low_lanes, -swapped, turns)
+        def halo_arrives(h):
+            halos[h].wait_recv()
+
+            @pl.when(c == 1)
+            def _():
+                beside(h).start()
+
+        halo_arrives(0)
         for copy in lifts:
             copy.wait_recv()
         spread = [
@@ -577,14 +600,6 @@
             )
             for k in far_first
         ]
-        def halo_arrives(h):
-            halos[h].wait_recv()
-
-            @pl.when(c == 1)
-            def _():
-                beside(h).start()
-
-        halo_arrives(0)
         for copy in edges:
             copy.wait_recv()
 
@@ -665,6 +680,11 @@
         @pl.when(inner)
         def _():
             gain_heads(2, 1)
+        gain_heads(1, 0)
+
+        @pl.when(jnp.logical_not(inner))
+        def _():
+            gain_heads(2, 0)
         for copy in spread:
             copy.wait_recv()
         shared = launch(
@@ -690,18 +710,13 @@
         ]
         loads[3].wait()
         loads[4].wait()
-        gain_heads(1, 0)
-
-        @pl.when(jnp.logical_not(inner))
-        def _():
-            gain_heads(2, 0)
-        shared.wait_recv()
-        blend_ref[...] = states_ref[...].astype(jnp.float32) + blended(0)
         gain_heads(1, 1)
 
         @pl.when(jnp.logical_not(inner))
         def _():
             gain_heads(2, 1)
+        shared.wait_recv()
+        blend_ref[...] = states_ref[...].astype(jnp.float32) + blended(0)
         full_ref[...] = (blend_ref[...] + blended(1)).astype(jnp.bfloat16)
         enc_out = pltpu.make_async_copy(full_ref.at[pl.ds(0, byte_rows)], enc_hbm, enc_sem.at[0])
         enc_out.start()
@@ -721,40 +736,31 @@
         def slot_of(r, i):
             return i if r == 0 else panel_count + i
 
-        def climb(origin, r, i, target, sem):
+        def away(k, r, i):
             return remote(
-                panels.at[origin, r, :, window(r, i)],
-                panels.at[origin, r, :, window(r, i)],
-                z_send.at[slot_of(r, i), sem],
-                z_recv.at[slot_of(r, i), origin],
-                tp_peer(target),
-            )
-
-        def climb_over(which, r, i):
-            return climb(sources[which], r, i, beyond[which], 2 + which)
-
-        def away(origin, r, i):
-            return remote(
-                panels.at[origin, r, :, window(r, i)],
+                panels.at[r, :, window(r, i)],
                 rows_ref.at[r, p, :, window(r, i)],
-                plane_send.at[origin, slot_of(r, i)],
-                plane_recv.at[p, slot_of(r, i)],
-                plane(origin),
+                panel_send.at[k, slot_of(r, i)],
+                panel_recv.at[p, slot_of(r, i)],
+                {"seq": 2 * t + c, "tp": tower(k)},
             )
 
         def stay(r, i):
             return pltpu.make_async_copy(
-                panels.at[p, r, :, window(r, i)],
+                panels.at[r, :, window(r, i)],
                 rows_ref.at[r, p, :, window(r, i)],
                 stay_sems.at[slot_of(r, i)],
             )
 
-        def spill(origin, r, i):
-            @pl.when(origin != p)
+        def ship(r, i):
+            for k in (2, 1, 3):
+                away(k, r, i).start()
+
+            @pl.when(p != t)
             def _():
-                away(origin, r, i).start()
-
-            @pl.when(origin == p)
+                away(0, r, i).start()
+
+            @pl.when(p == t)
             def _():
                 stay(r, i).start()
 
@@ -781,79 +787,35 @@
             panel = jnp.where(in_use, patch, 0.0).astype(jnp.bfloat16)
             patch_ref[:, cols] = panel
             for r in range(2):
-                panels[t, r, :, cols] = panel[r * part_rows : (r + 1) * part_rows]
-            to_near(lambda target, sem: climb(t, 0, i, target, sem))
-            spill(t, 0, i)
+                panels[r, :, cols] = panel[r * part_rows : (r + 1) * part_rows]
+            ship(0, i)
             return carry
         lax.fori_loop(0, panel_count, heads, 0)
         for i in range(widths[1]):
-            to_near(lambda target, sem: climb(t, 1, i, target, sem))
-            spill(t, 1, i)
-
-        def gain_panel(which, r, i):
-            climb_over(which, r, i).wait_recv()
-
-            @pl.when(inner)
-            def _():
-                climb_over(which, r, i).start()
-
-            spill(sources[which], r, i)
-
-        for r in range(2):
-            @pl.when(inner)
-            def _():
-                for i in range(widths[r]):
-                    gain_panel(0, r, i)
-                for i in range(widths[r]):
-                    gain_panel(2, r, i)
-                    if i:
-                        gain_panel(1, r, i - 1)
-                gain_panel(1, r, widths[r] - 1)
-
-            @pl.when(jnp.logical_not(inner))
-            def _():
-                for which in range(3):
-                    for i in range(widths[r]):
-                        gain_panel(which, r, i)
-
-        arriving, total, flats = [], [], []
+            ship(1, i)
+
+        arriving, flats = ([], []), []
         eye = iota((half_total, half_total), 0) == iota((half_total, half_total), 1)
         chip_gain = lgain_ref[pl.ds(pl.multiple_of(p * columns, columns), columns)]
         chip_gain = chip_gain.astype(jnp.float32).reshape(1, columns)
         for r in range(2):
             for q in range(count):
 
-                @pl.when(p != q)
+                @pl.when((p != q) | (p != t))
                 def _():
                     for i in range(widths[r]):
                         remote(
-                            panels.at[0, r, :, window(r, i)],
+                            panels.at[r, :, window(r, i)],
                             rows_ref.at[r, q, :, window(r, i)],
-                            plane_send.at[q, slot_of(r, i)],
-                            plane_recv.at[q, slot_of(r, i)],
+                            panel_send.at[0, slot_of(r, i)],
+                            panel_recv.at[q, slot_of(r, i)],
                             plane(p),
                         ).wait_recv()
 
-            for i in range(widths[r]):
-                stay(r, i).wait()
-            if r:
-                for copy in quarters:
-                    copy.wait_recv()
-                loads[8].wait()
-                mine_out = pltpu.make_async_copy(out_quarter.at[t], out_rows.at[c, t], own_sems.at[0])
-                mine_out.start()
-                ups = [
-                    launch(
-                        remote(
-                            out_quarter.at[tower(k)],
-                            out_rows.at[c, t],
-                            oz_s.at[k - 1],
-                            oz_r.at[k - 1],
-                            tp_peer(tower(k)),
-                        )
-                    )
-                    for k in range(1, count)
-                ]
+            @pl.when(p == t)
+            def _():
+                for i in range(widths[r]):
+                    stay(r, i).wait()
             values = rows_ref[r].reshape(half_total, columns).astype(jnp.float32)
             squares = jnp.sum(values * values, axis=1, keepdims=True)
             flat = jnp.sum(jnp.where(eye, squares, 0.0), axis=0, keepdims=True)
@@ -861,7 +823,7 @@
             sq_send[r] = jnp.broadcast_to(flat, (8, half_total))
             geared[...] = (values * chip_gain).astype(jnp.bfloat16)
             for k in far_first:
-                arriving.append(
+                arriving[r].append(
                     launch(
                         remote(
                             sq_send.at[r],
@@ -887,7 +849,7 @@
                     else:
                         own_part[r, i] = part
                 if k:
-                    arriving.append(
+                    arriving[r].append(
                         launch(
                             remote(
                                 qkv_send.at[r, k - 1],
@@ -898,44 +860,69 @@
                             )
                         )
                     )
-        for copy in arriving:
-            copy.wait_recv()
-        scales = []
+            if r == 0:
+                for copy in quarters:
+                    copy.wait_recv()
+                loads[8].wait()
+                mine_out = pltpu.make_async_copy(
+                    out_quarter.at[t], out_rows.at[c, t], own_sems.at[0]
+                )
+                mine_out.start()
+                ups = [
+                    remote(
+                        out_quarter.at[tower(k)],
+                        out_rows.at[c, t],
+                        oz_s.at[k - 1],
+                        oz_r.at[k - 1],
+                        tp_peer(tower(k)),
+                    )
+                    for k in range(1, count)
+                ]
+
+            @pl.when(inner if r == 0 else jnp.logical_not(inner))
+            def _():
+                for copy in ups:
+                    copy.start()
+
+        sent.extend(ups)
+
+        def turned(vectors, rows):
+            return (
+                vectors * cos_ref[rows] + pltpu.roll(vectors, HD // 2, 1) * sin_ref[rows]
+            ).astype(jnp.bfloat16)
+
+        swaps_kv, queries = [], []
         for r in range(2):
+            for copy in arriving[r]:
+                copy.wait_recv()
             flat = flats[r] + jnp.sum(sq_land[r, :, 0:1, :], axis=0)
             square_sum = jnp.sum(jnp.where(eye, flat, 0.0), axis=1, keepdims=True)
-            scales.append(lax.rsqrt(square_sum / full_width + epsilon))
-        for i in range(3):
-            bands = []
-            for r in range(2):
+            scale = lax.rsqrt(square_sum / full_width + epsilon)
+            total = []
+            for i in range(3):
                 band = own_part[r, i]
                 for k in range(count - 1):
                     band = band + qkv_land[r, k, i].astype(jnp.float32)
-                bands.append(band * scales[r])
-            total.append(jnp.concatenate(bands, axis=0))
-
-        def turned(vectors):
-            return (
-                vectors * cos_ref[...] + pltpu.roll(vectors, HD // 2, 1) * sin_ref[...]
-            ).astype(jnp.bfloat16)
-
-        queries = turned(total[0])
-        kv_own[0] = turned(total[1])
-        kv_own[1] = total[2].astype(jnp.bfloat16)
-        swap = launch(remote(kv_own, kv_other, kv_sems.at[0], kv_sems.at[1], partner))
+                total.append(band * scale)
+            rows = slice(r * half_total, (r + 1) * half_total)
+            kv_own[r, 0] = turned(total[1], rows)
+            kv_own[r, 1] = total[2].astype(jnp.bfloat16)
+            swaps_kv.append(
+                launch(remote(kv_own.at[r], kv_other.at[r], kv_s.at[r], kv_r.at[r], partner))
+            )
+            queries.append(turned(total[0], rows))
+        queries = jnp.concatenate(queries, axis=0)
+
+        def both(ref, i):
+            return jnp.concatenate([ref[0, i], ref[1, i]], axis=0)
         def scored(keys, key_position):
             scores = across_lanes(queries, keys) * (1.0 / math.sqrt(HD))
             return jnp.where(key_position <= position, scores, -1e30)
 
-        scores_a = scored(kv_own[0], key_positions[0])
-        for copy in ups:
+        scores_a = scored(both(kv_own, 0), key_positions[0])
+        for copy in swaps_kv:
             copy.wait_recv()
-        mine_out.wait()
-        halves = launch(
-            remote(out_rows.at[c], out_rows.at[c], oc_sems.at[0], oc_sems.at[1], partner)
-        )
-        swap.wait_recv()
-        scores_b = scored(kv_other[0], key_positions[1])
+        scores_b = scored(both(kv_other, 0), key_positions[1])
         largest = jnp.maximum(
             jnp.max(scores_a, axis=1, keepdims=True), jnp.max(scores_b, axis=1, keepdims=True)
         )
@@ -944,8 +931,8 @@
         weight_sum = jnp.sum(raised_a, axis=1, keepdims=True) + jnp.sum(
             raised_b, axis=1, keepdims=True
         )
-        weighted = product(raised_a.astype(jnp.bfloat16), kv_own[1]) + product(
-            raised_b.astype(jnp.bfloat16), kv_other[1]
+        weighted = product(raised_a.astype(jnp.bfloat16), both(kv_own, 1)) + product(
+            raised_b.astype(jnp.bfloat16), both(kv_other, 1)
         )
         tall[t] = (weighted / weight_sum).astype(jnp.bfloat16).reshape(2, half_total, HD)
         risen = {}
@@ -961,6 +948,12 @@
                         tp_peer(tower(d)),
                     )
                 )
+        for copy in ups:
+            copy.wait_recv()
+        mine_out.wait()
+        halves = launch(
+            remote(out_rows.at[c], out_rows.at[c], oc_sems.at[0], oc_sems.at[1], partner)
+        )
         halves.wait_recv()
         hops, parts_own = [], []
         summed = patch_ref[...].astype(jnp.float32)
@@ -1015,15 +1008,12 @@
 
         for r in range(2):
             for i in range(widths[r]):
-                sent_near(
-                    lambda target, sem: climb(t, r, i, target, sem),
-                    lambda which: climb_over(which, r, i),
-                )
-                for q in range(count):
-
-                    @pl.when(p != q)
-                    def _():
-                        away(q, r, i).wait_send()
+                for k in range(1, count):
+                    away(k, r, i).wait_send()
+
+                @pl.when(p != t)
+                def _():
+                    away(0, r, i).wait_send()
     vmem = pl.BlockSpec(memory_space=pltpu.VMEM)
     hbm = pl.BlockSpec(memory_space=pl.ANY)
     smem = pl.BlockSpec(memory_space=pltpu.SMEM)
@@ -1053,7 +1043,7 @@
             buffer(*cross_kv.shape),
             buffer(slots, width),
             buffer(total_rows, width),
-            buffer(count, 2, part_rows, columns),
+            buffer(2, part_rows, columns),
             buffer(2, count, part_rows, columns),
             buffer(slots, columns),
             buffer(*lat_qkv.shape),
@@ -1064,8 +1054,8 @@
             buffer(2, near, 3, half_total, HD),
             buffer(2, 8, half_total, dtype=jnp.float32),
             buffer(2, near, 8, half_total, dtype=jnp.float32),
-            buffer(2, row_total, HD),
-            buffer(2, row_total, HD),
+            buffer(2, 2, half_total, HD),
+            buffer(2, 2, half_total, HD),
             buffer(count, HD, half),
             buffer(2, count, HD, half),
             buffer(count, 2, half_total, HD),
@@ -1087,8 +1077,6 @@
             dma((2,)),
             dma((2, 5)),
             dma((2, count)),
-            dma((panel_count + 2, 5)),
-            dma((panel_count + 2, count)),
             dma((count, panel_count + 2)),
             dma((count, panel_count + 2)),
             dma((panel_count + 2,)),
@@ -1096,6 +1084,7 @@
             dma((2, near)),
             dma((2, near)),
             dma((2, near)),
+            dma((2,)),
             dma((2,)),
             dma((near,)),
             dma((near,)),

time: 78.7 us -> 69.9 us (0.89)
  Pallas kernels: 77.2 us -> 68.4 us
    pallas_call x1, Pallas kernels: 75.3 us -> 66.5 us  [whole_layer(): pl.pallas_call(kernel, out_shape=[like((byte_rows, width)), like((slots,...]
where the time goes in v4:
time: 69.9 us; the launch traced here: 69.7 us
  Pallas kernels  68.4 us (98%)
  between operations  1.29 us (2%)
    pallas_call x1, Pallas kernels, whole_layer(): pl.pallas_call(kernel, out_shape=[like((byte_rows, width)), like((slots,...  66.5 us
    pallas_call x1, Pallas kernels, settle(): pl.pallas_call(kernel, out_shape=[like(value.shape, value.dtype) for valu...  1.9 us

profile of v4, /device:TPU:0, one launch (start us, length us, event | category | flops | bytes accessed | tf_op | source)
XLA Modules:
  0.0 69.7 jit_solution(15510639990476950322)
XLA Ops:
  1.3 66.5 %shard_map.131 = (bf16[256,1024]{1,0:T(8,128)(2,1)}, bf16[64,1024]{1,0:T(8,128)(2,1)}) custom-call(bf16[256,1024]{1,0:T(8,128)(2,1)} %states_hbm.1, bf16[1024]{0:T(1024)(128)(2,1)} %gain_ref.1, bf16[3,1024,256]{2,1,0:T(8,128)(2,1)} %qkv_hbm.1, bf16[256,1024]{1,0:T(8,128)(2,1)} %proj_hbm.1, s32[1,64]{1,0:T(1,128)} %starts_ref.1, s32[1]{0:T(128)S(6)} %copy.14.counts_ref, ...), custom_call_target="tpu_custom_call" | custom-call | tf_op jit(solution)/shard_map/pallas_call | solution.py:1025
  67.8 1.9 %shard_map.132 = (bf16[256,1024]{1,0:T(8,128)(2,1)}, bf16[64,1024]{1,0:T(8,128)(2,1)}) custom-call(bf16[256,1024]{1,0:T(8,128)(2,1)} %get-tuple-element.4.refs_0_, bf16[64,1024]{1,0:T(8,128)(2,1)} %get-tuple-element.5.refs_1_), custom_call_target="tpu_custom_call" | custom-call | tf_op jit(solution)/shard_map/pallas_call | solution.py:1125

commit v5 on v4

--- a/solution.py
+++ b/solution.py
@@ -321,16 +321,17 @@
     half = lat_qkv.shape[1]
     full_width = columns * count
     rows_half = byte_rows // 2
+    row_spans = ((0, rows_half), (rows_half, rows_half), (byte_rows, EDGE))
     part_rows = slots // 2
     half_total = row_total // 2
     share = enc_cols // 2
     piece = share // count
 
     def kernel(
-        states_hbm, gain_ref, qkv_hbm, proj_hbm, starts_ref, counts_ref, lift_hbm, cross_hbm,
-        lgain_ref, w_own_hbm, o_hbm, table_hbm,
-        enc_hbm, out_ref,
-        states_ref, qkv_ref, query_ref, kv_ref, infos, proj_ref, att_ref, blend_ref, table_ref, cos_ref, sin_ref,
+        states_hbm, gain_hbm, qkv_hbm, proj_hbm, starts_hbm, counts_hbm, lift_hbm, cross_hbm,
+        lgain_hbm, w_own_hbm, o_hbm, table_hbm,
+        enc_hbm, out_hbm,
+        gain_ref, starts_ref, counts_ref, lgain_ref, states_ref, qkv_ref, query_ref, kv_ref, infos, proj_ref, att_ref, near_ref, blend_ref, table_ref, cos_ref, sin_ref,
         lift_ref, cross_ref, pooled_ref, full_ref, panels, rows_ref, patch_ref,
         w_own, w_other, geared, own_part, qkv_send, qkv_land, sq_send, sq_land,
         kv_own, kv_other, out_quarter, out_rows, tall, parts, land,
@@ -409,24 +410,25 @@
             (cross_hbm, cross_ref),
             (w_own_hbm, w_own),
             (o_hbm.at[own_rows], out_quarter.at[p]),
+            (gain_hbm, gain_ref),
+            (starts_hbm, starts_ref),
+            (counts_hbm, counts_ref),
+            (lgain_hbm, lgain_ref),
         )
         loads = [
             pltpu.make_async_copy(source, target, load_sems.at[i])
             for i, (source, target) in enumerate(load_plan)
         ]
-        for load in loads:
-            load.start()
+        for i in (0, 9, 1, 10, 11, 2, 3, 4, 5, 6, 7, 8, 12):
+            loads[i].start()
         sent = []
 
         def launch(copy):
             copy.start()
             sent.append(copy)
             return copy
-        info_lane = iota((8, 128), 1)
-        infos[s] = jnp.where(
-            info_lane == 0, counts_ref[0], jnp.where(info_lane == 1, starts_ref[0:1, 0:1], 0)
-        )
         loads[0].wait()
+        loads[9].wait()
         values = states_ref[0:byte_rows].astype(jnp.float32)
         chip_row = gain_ref[...].astype(jnp.float32).reshape(1, width)
         normed = rms_scale(values, chip_row).astype(jnp.bfloat16)
@@ -439,6 +441,13 @@
         query_ref[0:byte_rows] = (
             product(normed, qkv_ref[0]) * (1.0 / math.sqrt(EH))
         ).astype(jnp.bfloat16)
+        loads[10].wait()
+        loads[11].wait()
+        my_count = counts_ref[...].reshape(1, 1)
+        info_lane = iota((8, 128), 1)
+        infos[s] = jnp.where(
+            info_lane == 0, my_count, jnp.where(info_lane == 1, starts_ref[0:1, 0:1], 0)
+        )
         greetings = size - 1 + count - 1
 
         @pl.when(p == t)
@@ -514,7 +523,6 @@
         offsets = [jnp.zeros((1, 1), jnp.int32)]
         for m in range(size - 1):
             offsets.append(offsets[m] + counted[m])
-        my_count = counts_ref[0]
         next_first = jnp.where(
             s + 1 < size, infos[jnp.minimum(s + 1, size - 1)][0:1, 1:2], size * byte_rows
         )
@@ -535,6 +543,12 @@
         lengths = jnp.maximum(jnp.sum(member, axis=1, keepdims=True), 1.0)
         member = member.astype(jnp.bfloat16)
         bias = jnp.where(allowed, 0.0, -1e30)
+        for begin, rows in row_spans:
+            reach_rows = rows + WIN
+            behind_by = iota((rows, reach_rows), 0) - iota((rows, reach_rows), 1) + WIN
+            known = iota((rows, reach_rows), 1) >= WIN - begin - s * byte_rows
+            near_by = (behind_by >= 0) & (behind_by < WIN) & known
+            near_ref[begin : begin + rows, 0:reach_rows] = jnp.where(near_by, 0.0, -1e30)
         chosen = [
             (
                 jnp.where(c == 0, offsets[2 * i], offsets[2 * i + 1]),
@@ -600,6 +614,17 @@
             )
             for k in far_first
         ]
+        def shared(k):
+            rows = pl.ds(pl.multiple_of(flip(k) * piece, piece), piece)
+            return remote(
+                proj_ref.at[c, pl.ds(1, near), rows],
+                proj_ref.at[c, pl.ds(1, near), rows],
+                pc_s.at[k],
+                pc_r.at[k],
+                partner,
+            )
+
+        launch(shared(0))
         for copy in edges:
             copy.wait_recv()
 
@@ -623,12 +648,7 @@
                 [jnp.where(head_of == h, queries, jnp.zeros_like(queries)) for h in range(share // EH)],
                 axis=0,
             )
-            query_at = iota((rows, reach_rows), 0) + begin
-            key_at = iota((rows, reach_rows), 1) + (begin - WIN)
-            near_by = (
-                (key_at <= query_at) & (key_at > query_at - WIN) & (key_at >= -s * byte_rows)
-            )
-            near_bias = jnp.where(near_by, 0.0, -1e30)
+            near_bias = near_ref[begin : begin + rows, 0:reach_rows]
             scores = across_lanes(stacked, keys)
             raised, sums = [], []
             for h in range(share // EH):
@@ -648,7 +668,7 @@
             if h:
                 halo_arrives(1)
                 beside(1).wait_recv()
-            for begin, rows in ((0, rows_half), (rows_half, rows_half), (byte_rows, EDGE)):
+            for begin, rows in row_spans:
                 attend(h, begin, rows)
             to_near(lambda target, sem: share_heads(t, h, target, sem))
 
@@ -685,17 +705,9 @@
         @pl.when(jnp.logical_not(inner))
         def _():
             gain_heads(2, 0)
-        for copy in spread:
+        for k, copy in zip(far_first[::-1], spread[::-1]):
             copy.wait_recv()
-        shared = launch(
-            remote(
-                proj_ref.at[c, pl.ds(1, near)],
-                proj_ref.at[c, pl.ds(1, near)],
-                pc_s.at[0],
-                pc_r.at[0],
-                partner,
-            )
-        )
+            launch(shared(k))
         quarters = [
             launch(
                 remote(
@@ -715,9 +727,10 @@
         @pl.when(jnp.logical_not(inner))
         def _():
             gain_heads(2, 1)
-        shared.wait_recv()
-        blend_ref[...] = states_ref[...].astype(jnp.float32) + blended(0)
-        full_ref[...] = (blend_ref[...] + blended(1)).astype(jnp.bfloat16)
+        blend_ref[...] = states_ref[...].astype(jnp.float32) + blended(c)
+        for k in range(count):
+            shared(k).wait_recv()
+        full_ref[...] = (blend_ref[...] + blended(1 - c)).astype(jnp.bfloat16)
         enc_out = pltpu.make_async_copy(full_ref.at[pl.ds(0, byte_rows)], enc_hbm, enc_sem.at[0])
         enc_out.start()
 
@@ -796,6 +809,7 @@
 
         arriving, flats = ([], []), []
         eye = iota((half_total, half_total), 0) == iota((half_total, half_total), 1)
+        loads[12].wait()
         chip_gain = lgain_ref[pl.ds(pl.multiple_of(p * columns, columns), columns)]
         chip_gain = chip_gain.astype(jnp.float32).reshape(1, columns)
         for r in range(2):
@@ -995,7 +1009,9 @@
             copy.wait_recv()
         for k in range(count - 1):
             summed = summed + land[k].astype(jnp.float32)
-        out_ref[...] = jnp.where(in_use, summed, 0.0).astype(jnp.bfloat16)
+        patch_ref[...] = jnp.where(in_use, summed, 0.0).astype(jnp.bfloat16)
+        latent_out = pltpu.make_async_copy(patch_ref, out_hbm, enc_sem.at[1])
+        latent_out.start()
         enc_out.wait()
         for copy in sent:
             copy.wait_send()
@@ -1014,9 +1030,9 @@
                 @pl.when(p != t)
                 def _():
                     away(0, r, i).wait_send()
-    vmem = pl.BlockSpec(memory_space=pltpu.VMEM)
+
+        latent_out.wait()
     hbm = pl.BlockSpec(memory_space=pl.ANY)
-    smem = pl.BlockSpec(memory_space=pltpu.SMEM)
     dma = pltpu.SemaphoreType.DMA
 
     def buffer(*shape, dtype=jnp.bfloat16):
@@ -1025,9 +1041,13 @@
     return pl.pallas_call(
         kernel,
         out_shape=[like((byte_rows, width)), like((slots, columns))],
-        in_specs=[hbm, vmem, hbm, hbm, vmem, smem, hbm, hbm, vmem, hbm, hbm, hbm],
-        out_specs=[hbm, vmem],
+        in_specs=[hbm] * 12,
+        out_specs=[hbm, hbm],
         scratch_shapes=[
+            buffer(width),
+            buffer(1, slots, dtype=jnp.int32),
+            buffer(1, dtype=jnp.int32),
+            buffer(full_width),
             buffer(total_rows, width),
             buffer(*enc_qkv.shape),
             buffer(total_rows, enc_cols),
@@ -1035,6 +1055,7 @@
             buffer(size, 8, 128, dtype=jnp.int32),
             buffer(2, count, share, width),
             buffer(count, 2, total_rows, share),
+            buffer(total_rows, rows_half + WIN, dtype=jnp.float32),
             buffer(total_rows, width, dtype=jnp.float32),
             buffer(*table.shape, dtype=jnp.float32),
             buffer(row_total, HD, dtype=jnp.float32),
@@ -1061,7 +1082,7 @@
             buffer(count, 2, half_total, HD),
             buffer(near, slots, columns),
             buffer(near, slots, columns),
-            dma((9,)),
+            dma((13,)),
             dma((size - 1,)),
             dma((size - 1,)),
             dma((2, 2)),
@@ -1072,8 +1093,8 @@
             dma((near,)),
             dma((near,)),
             dma((near,)),
-            dma((1,)),
-            dma((1,)),
+            dma((count,)),
+            dma((count,)),
             dma((2,)),
             dma((2, 5)),
             dma((2, count)),
@@ -1096,7 +1117,7 @@
             dma((count, near)),
             dma((near,)),
             dma((near,)),
-            dma((1,)),
+            dma((2,)),
         ],
         compiler_params=pltpu.CompilerParams(collective_id=call_id, has_side_effects=True),
     )(

time: 69.9 us -> 69.5 us (level)
  no operation moved by 1% of the time
where the time goes in v5:
time: 69.5 us; the launch traced here: 69.3 us
  Pallas kernels  68 us (98%)
  between operations  1.29 us (2%)
    pallas_call x1, Pallas kernels, whole_layer(): pl.pallas_call(kernel, out_shape=[like((byte_rows, width)), like((slots,...  66.1 us
    pallas_call x1, Pallas kernels, settle(): pl.pallas_call(kernel, out_shape=[like(value.shape, value.dtype) for valu...  1.9 us

profile of v5, /device:TPU:0, one launch (start us, length us, event | category | flops | bytes accessed | tf_op | source)
XLA Modules:
  0.0 69.3 jit_solution(18303271567432562103)
XLA Ops:
  1.3 66.1 %shard_map.131 = (bf16[256,1024]{1,0:T(8,128)(2,1)}, bf16[64,1024]{1,0:T(8,128)(2,1)}) custom-call(bf16[256,1024]{1,0:T(8,128)(2,1)} %states_hbm.1, bf16[1024]{0:T(1024)(128)(2,1)} %gain_hbm.1, bf16[3,1024,256]{2,1,0:T(8,128)(2,1)} %qkv_hbm.1, bf16[256,1024]{1,0:T(8,128)(2,1)} %proj_hbm.1, s32[1,64]{1,0:T(1,128)} %starts_hbm.1, s32[1]{0:T(128)S(6)} %copy.14.counts_hbm, ...), custom_call_target="tpu_custom_call" | custom-call | tf_op jit(solution)/shard_map/pallas_call | solution.py:1041
  67.4 1.9 %shard_map.132 = (bf16[256,1024]{1,0:T(8,128)(2,1)}, bf16[64,1024]{1,0:T(8,128)(2,1)}) custom-call(bf16[256,1024]{1,0:T(8,128)(2,1)} %get-tuple-element.4.refs_0_, bf16[64,1024]{1,0:T(8,128)(2,1)} %get-tuple-element.5.refs_1_), custom_call_target="tpu_custom_call" | custom-call | tf_op jit(solution)/shard_map/pallas_call | solution.py:1146

commit v6 on v5

--- a/solution.py
+++ b/solution.py
@@ -330,7 +330,7 @@
     def kernel(
         states_hbm, gain_hbm, qkv_hbm, proj_hbm, starts_hbm, counts_hbm, lift_hbm, cross_hbm,
         lgain_hbm, w_own_hbm, o_hbm, table_hbm,
-        enc_hbm, out_hbm,
+        enc_ref, out_ref,
         gain_ref, starts_ref, counts_ref, lgain_ref, states_ref, qkv_ref, query_ref, kv_ref, infos, proj_ref, att_ref, near_ref, blend_ref, table_ref, cos_ref, sin_ref,
         lift_ref, cross_ref, pooled_ref, full_ref, panels, rows_ref, patch_ref,
         w_own, w_other, geared, own_part, qkv_send, qkv_land, sq_send, sq_land,
@@ -731,7 +731,7 @@
         for k in range(count):
             shared(k).wait_recv()
         full_ref[...] = (blend_ref[...] + blended(1 - c)).astype(jnp.bfloat16)
-        enc_out = pltpu.make_async_copy(full_ref.at[pl.ds(0, byte_rows)], enc_hbm, enc_sem.at[0])
+        enc_out = pltpu.make_async_copy(full_ref.at[pl.ds(0, byte_rows)], enc_ref, enc_sem.at[0])
         enc_out.start()
 
         totals = product(member, full_ref[...])
@@ -1009,9 +1009,7 @@
             copy.wait_recv()
         for k in range(count - 1):
             summed = summed + land[k].astype(jnp.float32)
-        patch_ref[...] = jnp.where(in_use, summed, 0.0).astype(jnp.bfloat16)
-        latent_out = pltpu.make_async_copy(patch_ref, out_hbm, enc_sem.at[1])
-        latent_out.start()
+        out_ref[...] = jnp.where(in_use, summed, 0.0).astype(jnp.bfloat16)
         enc_out.wait()
         for copy in sent:
             copy.wait_send()
@@ -1030,9 +1028,8 @@
                 @pl.when(p != t)
                 def _():
                     away(0, r, i).wait_send()
-
-        latent_out.wait()
     hbm = pl.BlockSpec(memory_space=pl.ANY)
+    vmem = pl.BlockSpec(memory_space=pltpu.VMEM)
     dma = pltpu.SemaphoreType.DMA
 
     def buffer(*shape, dtype=jnp.bfloat16):
@@ -1042,7 +1039,7 @@
         kernel,
         out_shape=[like((byte_rows, width)), like((slots, columns))],
         in_specs=[hbm] * 12,
-        out_specs=[hbm, hbm],
+        out_specs=[vmem, vmem],
         scratch_shapes=[
             buffer(width),
             buffer(1, slots, dtype=jnp.int32),
@@ -1117,9 +1114,11 @@
             dma((count, near)),
             dma((near,)),
             dma((near,)),
-            dma((2,)),
+            dma((1,)),
         ],
-        compiler_params=pltpu.CompilerParams(collective_id=call_id, has_side_effects=True),
+        compiler_params=pltpu.CompilerParams(
+            collective_id=call_id, has_side_effects=True, vmem_limit_bytes=52428800
+        ),
     )(
         states, gain, enc_qkv, proj, starts, counts, lift, cross_kv, latent_gain, lat_qkv, lat_proj,
         table,
@@ -1130,26 +1129,20 @@
     total = len(arrays)
 
     def kernel(*refs):
-        ins, outs, holds = refs[:total], refs[total : 2 * total], refs[2 * total : 3 * total]
-        in_sems, out_sems = refs[3 * total :]
-        takes = [pltpu.make_async_copy(ins[i], holds[i], in_sems.at[i]) for i in range(total)]
-        puts = [pltpu.make_async_copy(holds[i], outs[i], out_sems.at[i]) for i in range(total)]
-        for take in takes:
-            take.start()
-        for take, put in zip(takes, puts):
-            take.wait()
+        ins, outs, sems = refs[:total], refs[total : 2 * total], refs[2 * total]
+        puts = [pltpu.make_async_copy(ins[i], outs[i], sems.at[i]) for i in range(total)]
+        for put in puts:
             put.start()
         for put in puts:
             put.wait()
 
-    hbm = pl.BlockSpec(memory_space=pl.ANY)
     return pl.pallas_call(
         kernel,
         out_shape=[like(value.shape, value.dtype) for value in arrays],
-        in_specs=[hbm] * total,
-        out_specs=[hbm] * total,
-        scratch_shapes=[pltpu.VMEM(value.shape, value.dtype) for value in arrays]
-        + [pltpu.SemaphoreType.DMA((total,))] * 2,
+        in_specs=[pl.BlockSpec(memory_space=pl.ANY)] * total,
+        out_specs=[pl.BlockSpec(memory_space=pltpu.HBM)] * total,
+        scratch_shapes=[pltpu.SemaphoreType.DMA((total,))],
+        compiler_params=pltpu.CompilerParams(vmem_limit_bytes=2**20),
     )(*arrays)
 
 
@@ -1167,21 +1160,24 @@
     lat_proj_out,
 ):
     table = jnp.asarray(turn_table(lax.axis_size("seq") * starts.shape[1]))
-    encoded, latent = whole_layer(
-        byte_states,
-        enc_gain,
-        enc_qkv,
-        enc_proj_out,
-        starts,
-        counts,
-        lift,
-        cross_kv,
-        latent_gain,
-        lat_qkv,
-        lat_proj_out,
-        table,
-        1,
-    )
+    operands = [
+        value if value.size == 1 else pltpu.with_memory_space_constraint(value, pltpu.HBM)
+        for value in (
+            byte_states,
+            enc_gain,
+            enc_qkv,
+            enc_proj_out,
+            starts,
+            counts,
+            lift,
+            cross_kv,
+            latent_gain,
+            lat_qkv,
+            lat_proj_out,
+            table,
+        )
+    ]
+    encoded, latent = whole_layer(*operands, 1)
     return settle(encoded, latent)
 
 

time: 69.5 us -> 67.9 us (0.977)
  Pallas kernels: 68 us -> 66.5 us
    pallas_call x1, Pallas kernels: 1.9 us -> 0.85 us  [settle(): pl.pallas_call(kernel, out_shape=[like(value.shape, value.dtype) for valu...]
where the time goes in v6:
time: 67.9 us; the launch traced here: 67.8 us
  Pallas kernels  66.5 us (98%)
  between operations  1.29 us (2%)
    pallas_call x1, Pallas kernels, whole_layer(): pl.pallas_call(kernel, out_shape=[like((byte_rows, width)), like((slots,...  65.6 us

profile of v6, /device:TPU:0, one launch (start us, length us, event | category | flops | bytes accessed | tf_op | source)
XLA Modules:
  0.0 67.8 jit_solution(1520929657026369848)
XLA Ops:
  1.3 65.6 %shard_map.131 = (bf16[256,1024]{1,0:T(8,128)(2,1)S(1)}, bf16[64,1024]{1,0:T(8,128)(2,1)S(1)}) custom-call(bf16[256,1024]{1,0:T(8,128)(2,1)} %states_hbm.1, bf16[1024]{0:T(1024)(128)(2,1)} %gain_hbm.1, bf16[3,1024,256]{2,1,0:T(8,128)(2,1)} %qkv_hbm.1, bf16[256,1024]{1,0:T(8,128)(2,1)} %proj_hbm.1, s32[1,64]{1,0:T(1,128)} %starts_hbm.1, ...), custom_call_target="tpu_custom_call" | custom-call | tf_op jit(solution)/shard_map/pallas_call | solution.py:1038
  66.9 0.8 %shard_map.132 = (bf16[256,1024]{1,0:T(8,128)(2,1)}, bf16[64,1024]{1,0:T(8,128)(2,1)}) custom-call(bf16[256,1024]{1,0:T(8,128)(2,1)S(1)} %get-tuple-element.4.refs_0_, bf16[64,1024]{1,0:T(8,128)(2,1)S(1)} %get-tuple-element.5.refs_1_), custom_call_target="tpu_custom_call" | custom-call | tf_op jit(solution)/shard_map/pallas_call | solution.py:1139

commit v7 on v6

--- a/solution.py
+++ b/solution.py
@@ -304,8 +304,8 @@
 
 
 def whole_layer(
-    states, gain, enc_qkv, proj, starts, counts, lift, cross_kv, latent_gain, lat_qkv, lat_proj,
-    table, call_id,
+    states, gain, enc_qkv, proj, starts, lift, cross_kv, latent_gain, lat_qkv, lat_proj, table,
+    call_id,
 ):
     count, size = lax.axis_size("tp"), lax.axis_size("seq")
     near = count - 1
@@ -328,10 +328,10 @@
     piece = share // count
 
     def kernel(
-        states_hbm, gain_hbm, qkv_hbm, proj_hbm, starts_hbm, counts_hbm, lift_hbm, cross_hbm,
+        states_hbm, gain_hbm, qkv_hbm, proj_hbm, starts_hbm, lift_hbm, cross_hbm,
         lgain_hbm, w_own_hbm, o_hbm, table_hbm,
         enc_ref, out_ref,
-        gain_ref, starts_ref, counts_ref, lgain_ref, states_ref, qkv_ref, query_ref, kv_ref, infos, proj_ref, att_ref, near_ref, blend_ref, table_ref, cos_ref, sin_ref,
+        gain_ref, starts_ref, lgain_ref, states_ref, qkv_ref, query_ref, kv_ref, infos, proj_ref, att_ref, near_ref, blend_ref, table_ref, cos_ref, sin_ref,
         lift_ref, cross_ref, pooled_ref, full_ref, panels, rows_ref, patch_ref,
         w_own, w_other, geared, own_part, qkv_send, qkv_land, sq_send, sq_land,
         kv_own, kv_other, out_quarter, out_rows, tall, parts, land,
@@ -412,14 +412,13 @@
             (o_hbm.at[own_rows], out_quarter.at[p]),
             (gain_hbm, gain_ref),
             (starts_hbm, starts_ref),
-            (counts_hbm, counts_ref),
             (lgain_hbm, lgain_ref),
         )
         loads = [
             pltpu.make_async_copy(source, target, load_sems.at[i])
             for i, (source, target) in enumerate(load_plan)
         ]
-        for i in (0, 9, 1, 10, 11, 2, 3, 4, 5, 6, 7, 8, 12):
+        for i in (0, 9, 1, 10, 2, 3, 4, 5, 6, 7, 8, 11):
             loads[i].start()
         sent = []
 
@@ -442,8 +441,8 @@
             product(normed, qkv_ref[0]) * (1.0 / math.sqrt(EH))
         ).astype(jnp.bfloat16)
         loads[10].wait()
-        loads[11].wait()
-        my_count = counts_ref[...].reshape(1, 1)
+        listed = jnp.where(starts_ref[...] < size * byte_rows, 1, 0)
+        my_count = jnp.sum(listed, axis=1, keepdims=True)
         info_lane = iota((8, 128), 1)
         infos[s] = jnp.where(
             info_lane == 0, my_count, jnp.where(info_lane == 1, starts_ref[0:1, 0:1], 0)
@@ -806,10 +805,40 @@
         lax.fori_loop(0, panel_count, heads, 0)
         for i in range(widths[1]):
             ship(1, i)
+        for copy in quarters:
+            copy.wait_recv()
+        loads[8].wait()
+        mine_out = pltpu.make_async_copy(
+            out_quarter.at[t], out_rows.at[c, t], own_sems.at[0]
+        )
+        mine_out.start()
+        ups = [
+            remote(
+                out_quarter.at[tower(k)],
+                out_rows.at[c, t],
+                oz_s.at[k - 1],
+                oz_r.at[k - 1],
+                tp_peer(tower(k)),
+            )
+            for k in range(1, count)
+        ]
+
+        @pl.when(inner)
+        def _():
+            for copy in ups:
+                copy.start()
+
+        @pl.when(t == 0)
+        def _():
+            ups[0].start()
+
+        @pl.when(t == count - 1)
+        def _():
+            ups[2].start()
 
         arriving, flats = ([], []), []
         eye = iota((half_total, half_total), 0) == iota((half_total, half_total), 1)
-        loads[12].wait()
+        loads[11].wait()
         chip_gain = lgain_ref[pl.ds(pl.multiple_of(p * columns, columns), columns)]
         chip_gain = chip_gain.astype(jnp.float32).reshape(1, columns)
         for r in range(2):
@@ -830,6 +859,18 @@
             def _():
                 for i in range(widths[r]):
                     stay(r, i).wait()
+
+            if r:
+
+                @pl.when(t == 0)
+                def _():
+                    ups[2].start()
+                    ups[1].start()
+
+                @pl.when(t == count - 1)
+                def _():
+                    ups[0].start()
+                    ups[1].start()
             values = rows_ref[r].reshape(half_total, columns).astype(jnp.float32)
             squares = jnp.sum(values * values, axis=1, keepdims=True)
             flat = jnp.sum(jnp.where(eye, squares, 0.0), axis=0, keepdims=True)
@@ -874,29 +915,6 @@
                             )
                         )
                     )
-            if r == 0:
-                for copy in quarters:
-                    copy.wait_recv()
-                loads[8].wait()
-                mine_out = pltpu.make_async_copy(
-                    out_quarter.at[t], out_rows.at[c, t], own_sems.at[0]
-                )
-                mine_out.start()
-                ups = [
-                    remote(
-                        out_quarter.at[tower(k)],
-                        out_rows.at[c, t],
-                        oz_s.at[k - 1],
-                        oz_r.at[k - 1],
-                        tp_peer(tower(k)),
-                    )
-                    for k in range(1, count)
-                ]
-
-            @pl.when(inner if r == 0 else jnp.logical_not(inner))
-            def _():
-                for copy in ups:
-                    copy.start()
 
         sent.extend(ups)
 
@@ -1038,12 +1056,11 @@
     return pl.pallas_call(
         kernel,
         out_shape=[like((byte_rows, width)), like((slots, columns))],
-        in_specs=[hbm] * 12,
+        in_specs=[hbm] * 11,
         out_specs=[vmem, vmem],
         scratch_shapes=[
             buffer(width),
             buffer(1, slots, dtype=jnp.int32),
-            buffer(1, dtype=jnp.int32),
             buffer(full_width),
             buffer(total_rows, width),
             buffer(*enc_qkv.shape),
@@ -1079,7 +1096,7 @@
             buffer(count, 2, half_total, HD),
             buffer(near, slots, columns),
             buffer(near, slots, columns),
-            dma((13,)),
+            dma((12,)),
             dma((size - 1,)),
             dma((size - 1,)),
             dma((2, 2)),
@@ -1120,8 +1137,7 @@
             collective_id=call_id, has_side_effects=True, vmem_limit_bytes=52428800
         ),
     )(
-        states, gain, enc_qkv, proj, starts, counts, lift, cross_kv, latent_gain, lat_qkv, lat_proj,
-        table,
+        states, gain, enc_qkv, proj, starts, lift, cross_kv, latent_gain, lat_qkv, lat_proj, table,
     )
 
 
@@ -1161,14 +1177,13 @@
 ):
     table = jnp.asarray(turn_table(lax.axis_size("seq") * starts.shape[1]))
     operands = [
-        value if value.size == 1 else pltpu.with_memory_space_constraint(value, pltpu.HBM)
+        pltpu.with_memory_space_constraint(value, pltpu.HBM)
         for value in (
             byte_states,
             enc_gain,
             enc_qkv,
             enc_proj_out,
             starts,
-            counts,
             lift,
             cross_kv,
             latent_gain,

time: 67.9 us -> 67.2 us (0.990)
  no operation moved by 1% of the time
where the time goes in v7:
time: 67.2 us; the launch traced here: 67.1 us
  Pallas kernels  66.5 us (99%)
    pallas_call x1, Pallas kernels, whole_layer(): pl.pallas_call(kernel, out_shape=[like((byte_rows, width)), like((slots,...  65.6 us

profile of v7, /device:TPU:0, one launch (start us, length us, event | category | flops | bytes accessed | tf_op | source)
XLA Modules:
  0.0 67.1 jit_solution(15497016633731830140)
XLA Ops:
  0.6 65.6 %shard_map.122 = (bf16[256,1024]{1,0:T(8,128)(2,1)S(1)}, bf16[64,1024]{1,0:T(8,128)(2,1)S(1)}) custom-call(bf16[256,1024]{1,0:T(8,128)(2,1)} %states_hbm.1, bf16[1024]{0:T(1024)(128)(2,1)} %gain_hbm.1, bf16[3,1024,256]{2,1,0:T(8,128)(2,1)} %qkv_hbm.1, bf16[256,1024]{1,0:T(8,128)(2,1)} %proj_hbm.1, s32[1,64]{1,0:T(1,128)} %starts_hbm.1, ...), custom_call_target="tpu_custom_call" | custom-call | tf_op jit(solution)/shard_map/pallas_call | solution.py:1056
  66.2 0.8 %shard_map.123 = (bf16[256,1024]{1,0:T(8,128)(2,1)}, bf16[64,1024]{1,0:T(8,128)(2,1)}) custom-call(bf16[256,1024]{1,0:T(8,128)(2,1)S(1)} %get-tuple-element.4.refs_0_, bf16[64,1024]{1,0:T(8,128)(2,1)S(1)} %get-tuple-element.5.refs_1_), custom_call_target="tpu_custom_call" | custom-call | tf_op jit(solution)/shard_map/pallas_call | solution.py:1155

commit v8 on v7

--- a/solution.py
+++ b/solution.py
@@ -322,6 +322,7 @@
     full_width = columns * count
     rows_half = byte_rows // 2
     row_spans = ((0, rows_half), (rows_half, rows_half), (byte_rows, EDGE))
+    halves_of = ((0, rows_half), (rows_half, total_rows - rows_half))
     part_rows = slots // 2
     half_total = row_total // 2
     share = enc_cols // 2
@@ -339,7 +340,7 @@
         w_sems, heads_send, heads_recv,
         panel_send, panel_recv, stay_sems,
         qkv_s, qkv_r, sq_s, sq_r, kv_s, kv_r,
-        oq_s, oq_r, oz_s, oz_r, oc_sems, own_sems, tz_s, tz_r, a_s, a_r, enc_sem,
+        oq_s, oq_r, oz_s, oz_r, oc_s, oc_r, own_sems, tz_s, tz_r, a_s, a_r, enc_sem,
     ):
         s, t = lax.axis_index("seq"), lax.axis_index("tp")
         p, c = s // 2, lax.rem(s, 2)
@@ -370,6 +371,7 @@
         second_from = jnp.where(low, t + 2, t - 2)
         third_from = jnp.where(lax.rem(t, 2) == 0, count - 1, 0)
         outer = jnp.where(low, 0, count - 1)
+        outward = (t, third_from, second_from, first_from)
 
         def to_near(copy_to):
             copy_to(first_from, 0).start()
@@ -630,8 +632,8 @@
         beside(0).wait_recv()
         def share_heads(origin, h, target, sem):
             return remote(
-                att_ref.at[origin, h],
-                att_ref.at[origin, h],
+                att_ref.at[origin, h // 2, pl.ds(*halves_of[h % 2])],
+                att_ref.at[origin, h // 2, pl.ds(*halves_of[h % 2])],
                 heads_send.at[h, sem],
                 heads_recv.at[h, origin],
                 tp_peer(target),
@@ -669,7 +671,9 @@
                 beside(1).wait_recv()
             for begin, rows in row_spans:
                 attend(h, begin, rows)
-            to_near(lambda target, sem: share_heads(t, h, target, sem))
+                if begin != rows_half:
+                    piece_id = 2 * h + (begin > 0)
+                    to_near(lambda target, sem: share_heads(t, piece_id, target, sem))
 
         swaps = [launch(remote(w_own_hbm, w_other, w_sems.at[0], w_sems.at[1], partner))]
         sources = (first_from, second_from, third_from)
@@ -688,22 +692,18 @@
         def blended(h):
             attended = jnp.concatenate([att_ref[tower(-k), h] for k in range(count)], axis=1)
             return product(attended, proj_ref[h].reshape(count * share, width))
-        gain_heads(0, 0)
-
+        for h in range(4):
+            gain_heads(0, h)
+
+            @pl.when(inner)
+            def _():
+                gain_heads(2, h)
+                if h > 1:
+                    gain_heads(1, h - 2)
         @pl.when(inner)
         def _():
-            gain_heads(2, 0)
-
-        gain_heads(0, 1)
-
-        @pl.when(inner)
-        def _():
-            gain_heads(2, 1)
-        gain_heads(1, 0)
-
-        @pl.when(jnp.logical_not(inner))
-        def _():
-            gain_heads(2, 0)
+            for h in (2, 3):
+                gain_heads(1, h)
         for k, copy in zip(far_first[::-1], spread[::-1]):
             copy.wait_recv()
             launch(shared(k))
@@ -719,13 +719,19 @@
             )
             for k in far_first
         ]
+        @pl.when(jnp.logical_not(inner))
+        def _():
+            for h in (0, 1):
+                gain_heads(1, h)
+                gain_heads(2, h)
+
         loads[3].wait()
         loads[4].wait()
-        gain_heads(1, 1)
-
         @pl.when(jnp.logical_not(inner))
         def _():
-            gain_heads(2, 1)
+            for h in (2, 3):
+                gain_heads(1, h)
+                gain_heads(2, h)
         blend_ref[...] = states_ref[...].astype(jnp.float32) + blended(c)
         for k in range(count):
             shared(k).wait_recv()
@@ -754,7 +760,7 @@
                 rows_ref.at[r, p, :, window(r, i)],
                 panel_send.at[k, slot_of(r, i)],
                 panel_recv.at[p, slot_of(r, i)],
-                {"seq": 2 * t + c, "tp": tower(k)},
+                {"seq": 2 * t + c, "tp": outward[k]},
             )
 
         def stay(r, i):
@@ -765,7 +771,7 @@
             )
 
         def ship(r, i):
-            for k in (2, 1, 3):
+            for k in range(1, count):
                 away(k, r, i).start()
 
             @pl.when(p != t)
@@ -967,26 +973,34 @@
             raised_b.astype(jnp.bfloat16), both(kv_other, 1)
         )
         tall[t] = (weighted / weight_sum).astype(jnp.bfloat16).reshape(2, half_total, HD)
-        risen = {}
         for k in far_first + (0,):
             take = pl.ds(pl.multiple_of(flip(k) * part_rows, part_rows), part_rows)
-            for d in range(count - 1, 0, -1):
-                risen[k, d] = launch(
+            for d in range(1, count):
+                launch(
                     remote(
                         tall.at[t, :, take],
                         tall.at[t, :, take],
                         tz_s.at[k, d - 1],
-                        tz_r.at[k, d - 1],
-                        tp_peer(tower(d)),
+                        tz_r.at[k, t],
+                        tp_peer(outward[d]),
                     )
                 )
-        for copy in ups:
-            copy.wait_recv()
+        def beside_rows(k):
+            return remote(
+                out_rows.at[c, tower(-k)],
+                out_rows.at[c, tower(-k)],
+                oc_s.at[k],
+                oc_r.at[k],
+                partner,
+            )
+
         mine_out.wait()
-        halves = launch(
-            remote(out_rows.at[c], out_rows.at[c], oc_sems.at[0], oc_sems.at[1], partner)
-        )
-        halves.wait_recv()
+        launch(beside_rows(0))
+        for k in (1, 3, 2):
+            ups[k - 1].wait_recv()
+            launch(beside_rows(k))
+        for k in range(count):
+            beside_rows(k).wait_recv()
         hops, parts_own = [], []
         summed = patch_ref[...].astype(jnp.float32)
         for k in far_first + (0,):
@@ -996,7 +1010,7 @@
                     tall.at[tower(-d), :, take],
                     tall.at[tower(-d), :, take],
                     tz_s.at[k, d - 1],
-                    tz_r.at[k, d - 1],
+                    tz_r.at[k, tower(-d)],
                     tp_peer(tower(-d)),
                 ).wait_recv()
             take = pl.ds(pl.multiple_of(flip(k) * part_rows, part_rows), part_rows)
@@ -1033,7 +1047,7 @@
             copy.wait_send()
         for i in range(2):
             beside(i).wait_send()
-        for h in range(2):
+        for h in range(4):
             sent_near(
                 lambda target, sem: share_heads(t, h, target, sem), lambda which: hand_over(which, h)
             )
@@ -1110,8 +1124,8 @@
             dma((count,)),
             dma((count,)),
             dma((2,)),
-            dma((2, 5)),
-            dma((2, count)),
+            dma((4, 5)),
+            dma((4, count)),
             dma((count, panel_count + 2)),
             dma((count, panel_count + 2)),
             dma((panel_count + 2,)),
@@ -1125,10 +1139,11 @@
             dma((near,)),
             dma((near,)),
             dma((near,)),
-            dma((2,)),
+            dma((count,)),
+            dma((count,)),
             dma((1,)),
             dma((count, near)),
-            dma((count, near)),
+            dma((count, count)),
             dma((near,)),
             dma((near,)),
             dma((1,)),

time: 67.2 us -> 66.2 us (0.985)
  Pallas kernels: 66.5 us -> 65.5 us
    pallas_call x1, Pallas kernels: 65.6 us -> 64.6 us  [whole_layer(): pl.pallas_call(kernel, out_shape=[like((byte_rows, width)), like((slots,...]
where the time goes in v8:
time: 66.2 us; the launch traced here: 66.1 us
  Pallas kernels  65.5 us (99%)
    pallas_call x1, Pallas kernels, whole_layer(): pl.pallas_call(kernel, out_shape=[like((byte_rows, width)), like((slots,...  64.6 us

profile of v8, /device:TPU:0, one launch (start us, length us, event | category | flops | bytes accessed | tf_op | source)
XLA Modules:
  0.0 66.1 jit_solution(9464359049109866443)
XLA Ops:
  0.6 64.6 %shard_map.122 = (bf16[256,1024]{1,0:T(8,128)(2,1)S(1)}, bf16[64,1024]{1,0:T(8,128)(2,1)S(1)}) custom-call(bf16[256,1024]{1,0:T(8,128)(2,1)} %states_hbm.1, bf16[1024]{0:T(1024)(128)(2,1)} %gain_hbm.1, bf16[3,1024,256]{2,1,0:T(8,128)(2,1)} %qkv_hbm.1, bf16[256,1024]{1,0:T(8,128)(2,1)} %proj_hbm.1, s32[1,64]{1,0:T(1,128)} %starts_hbm.1, ...), custom_call_target="tpu_custom_call" | custom-call | tf_op jit(solution)/shard_map/pallas_call | solution.py:1070
  65.2 0.8 %shard_map.123 = (bf16[256,1024]{1,0:T(8,128)(2,1)}, bf16[64,1024]{1,0:T(8,128)(2,1)}) custom-call(bf16[256,1024]{1,0:T(8,128)(2,1)S(1)} %get-tuple-element.4.refs_0_, bf16[64,1024]{1,0:T(8,128)(2,1)S(1)} %get-tuple-element.5.refs_1_), custom_call_target="tpu_custom_call" | custom-call | tf_op jit(solution)/shard_map/pallas_call | solution.py:1170

commit v9 on v8

--- a/solution.py
+++ b/solution.py
@@ -748,7 +748,7 @@
 
         def window(r, i):
             if r == 0:
-                return pl.ds(pl.multiple_of(i * group, group), group)
+                return pl.ds(i * group, group)
             return pl.ds(i * half_lanes, half_lanes)
 
         def slot_of(r, i):
@@ -785,7 +785,7 @@
         widths = (panel_count, 2)
 
         def heads(i, carry):
-            cols = pl.ds(pl.multiple_of(i * group, group), group)
+            cols = pl.ds(i * group, group)
             rows = full_ref[...]
             lifted = product(pooled_ref[...], lift_ref[:, cols])
             keys = product(rows, cross_ref[0, :, cols]).astype(jnp.bfloat16)
@@ -808,7 +808,8 @@
                 panels[r, :, cols] = panel[r * part_rows : (r + 1) * part_rows]
             ship(0, i)
             return carry
-        lax.fori_loop(0, panel_count, heads, 0)
+        for i in range(panel_count):
+            heads(i, 0)
         for i in range(widths[1]):
             ship(1, i)
         for copy in quarters:

time: 66.2 us -> 66.9 us (1.011)
  no operation moved by 1% of the time
where the time goes in v9:
time: 66.9 us; the launch traced here: 66.8 us
  Pallas kernels  66 us (99%)
  between operations  0.8 us (1%)
    pallas_call x1, Pallas kernels, whole_layer(): pl.pallas_call(kernel, out_shape=[like((byte_rows, width)), like((slots,...  65.1 us

profile of v9, /device:TPU:0, one launch (start us, length us, event | category | flops | bytes accessed | tf_op | source)
XLA Modules:
  0.0 66.8 jit_solution(614346210027145387)
XLA Ops:
  0.6 65.1 %shard_map.122 = (bf16[256,1024]{1,0:T(8,128)(2,1)S(1)}, bf16[64,1024]{1,0:T(8,128)(2,1)S(1)}) custom-call(bf16[256,1024]{1,0:T(8,128)(2,1)} %states_hbm.1, bf16[1024]{0:T(1024)(128)(2,1)} %gain_hbm.1, bf16[3,1024,256]{2,1,0:T(8,128)(2,1)} %qkv_hbm.1, bf16[256,1024]{1,0:T(8,128)(2,1)} %proj_hbm.1, s32[1,64]{1,0:T(1,128)} %starts_hbm.1, ...), custom_call_target="tpu_custom_call" | custom-call | tf_op jit(solution)/shard_map/pallas_call | solution.py:1071
  65.8 0.8 %shard_map.123 = (bf16[256,1024]{1,0:T(8,128)(2,1)}, bf16[64,1024]{1,0:T(8,128)(2,1)}) custom-call(bf16[256,1024]{1,0:T(8,128)(2,1)S(1)} %get-tuple-element.4.refs_0_, bf16[64,1024]{1,0:T(8,128)(2,1)S(1)} %get-tuple-element.5.refs_1_), custom_call_target="tpu_custom_call" | custom-call | tf_op jit(solution)/shard_map/pallas_call | solution.py:1171
